TPU v7x, 32 devices: a whole 2x2x4 slice. The times are simulated.
32 devices in a mesh: slides: 2 (over y), seq: 4 (over z), head: 4 (over x, core).
Axes of the slice: x: 2, y: 2, z: 4, core: 2. Of those that a mesh axis runs over, the one named last changes fastest.
Arguments:
- query_rows: bfloat16 [8192, 768], P(('slides', 'seq'), 'head'), parts along dimension 0, may hold values from -64 to 64
- key_rows: bfloat16 [8192, 768], P(('slides', 'seq'), 'head'), parts along dimension 0, may hold values from -4.1 to 4.1
- value_rows: bfloat16 [8192, 768], P(('slides', 'seq'), 'head'), parts along dimension 0, may hold values from -6 to 6
Outputs:
- attended: bfloat16 [8192, 768], P(('slides', 'seq'), 'head'), parts along dimension 0
There are 2 independent parts, one for each index of `slides`. A program takes and returns all parts, laid end to end along the dimension named above; each array names one. Nothing has to cross between parts.
All inputs are finite; a program needn't handle non-finite values.
Results may differ from a plain program's by a relative error of at most 0.0028.
Values may be sent and summed in bfloat16 or wider, within the bound.
No kernel may reach another device: no remote copies, remote signals or barrier semaphores. Data moves between devices by JAX's collectives and lax.ppermute only.
A program may use at most 64 MiB of HBM per device.

v0:
```python
import math

import jax
import jax.numpy as jnp
import numpy as np
from jax import lax
from jax.sharding import PartitionSpec as P

HEAD_DIM = 48
SEG_A = 1024
SEG_B = 4096


def swapped(shard, axis, stride):
    return lax.ppermute(shard, axis, [(i, i ^ 1 << stride) for i in range(lax.axis_size(axis))])


def attend(query_flat, key_flat, value_flat, score_scale):
    local_heads = query_flat.shape[1] // HEAD_DIM
    query_block = query_flat.reshape(query_flat.shape[0], local_heads, HEAD_DIM)
    key_block = key_flat.reshape(key_flat.shape[0], local_heads, HEAD_DIM)
    value_block = value_flat.reshape(value_flat.shape[0], local_heads, HEAD_DIM)
    scores = (
        jnp.einsum("qad,kad->qak", query_block, key_block, preferred_element_type=jnp.float32)
        * score_scale
    )
    row_max = jnp.max(scores, axis=-1)
    exp_scores = jnp.exp(scores - row_max[:, :, None])
    row_total = jnp.sum(exp_scores, axis=-1)
    weighted = jnp.einsum(
        "qak,kad->qad",
        exp_scores.astype(jnp.bfloat16),
        value_block,
        preferred_element_type=jnp.float32,
    )
    level_out = weighted / row_total[:, :, None]
    return (
        level_out.reshape(query_flat.shape[0], local_heads * HEAD_DIM),
        row_max + jnp.log(row_total),
    )


def attend_rows(query_flat, key_flat, value_flat, score_scale):
    count, feature_width = query_flat.shape
    local_heads = feature_width // HEAD_DIM
    keys = key_flat.shape[0]
    rows = math.gcd(count, max(1, 1048576 // (local_heads * keys)))

    def one_piece(query_piece):
        return attend(query_piece, key_flat, value_flat, score_scale)

    outs, lses = lax.map(one_piece, query_flat.reshape(count // rows, rows, feature_width))
    return (outs.reshape(count, feature_width), lses.reshape(count, local_heads))


def local_segments(query_flat, key_flat, value_flat, seg_rows, score_scale):
    count, feature_width = query_flat.shape
    local_heads = feature_width // HEAD_DIM
    shape = (count // seg_rows, seg_rows, feature_width)

    def one_segment(parts):
        return attend_rows(parts[0], parts[1], parts[2], score_scale)

    outs, lses = lax.map(
        one_segment, (query_flat.reshape(shape), key_flat.reshape(shape), value_flat.reshape(shape))
    )
    return (outs.reshape(count, feature_width), lses.reshape(count, local_heads))


def pick_rows(block, stride):
    row_count, feature_width = block.shape
    local_heads = feature_width // HEAD_DIM
    grid = block.reshape(row_count // stride, stride * feature_width)
    columns = []
    for head in range(local_heads):
        begin = head % stride * feature_width + head * HEAD_DIM
        columns.append(grid[:, begin : begin + HEAD_DIM])
    return jnp.concatenate(columns, axis=1)


def spread_rows(level_out, level_lse, stride):
    used_count, feature_width = level_out.shape
    local_heads = feature_width // HEAD_DIM
    head_of_column = np.arange(feature_width) // HEAD_DIM
    out_phases = []
    lse_phases = []
    for phase in range(stride):
        column_mask = jnp.asarray((head_of_column % stride == phase).astype(np.float32))
        head_mask = jnp.asarray(np.arange(local_heads) % stride == phase)
        out_phases.append(level_out * column_mask[None, :])
        lse_phases.append(jnp.where(head_mask[None, :], level_lse, -jnp.inf))
    full_out = jnp.stack(out_phases, axis=1).reshape(used_count * stride, feature_width)
    full_lse = jnp.stack(lse_phases, axis=1).reshape(used_count * stride, local_heads)
    return (full_out, full_lse)


def fold_block(fold_state, queries, keys, values, valid, score_scale):
    running_max, running_total, running_acc = fold_state
    local_heads = queries.shape[1] // HEAD_DIM
    query_block = queries.reshape(queries.shape[0], local_heads, HEAD_DIM)
    key_block = keys.reshape(keys.shape[0], local_heads, HEAD_DIM)
    value_block = values.reshape(values.shape[0], local_heads, HEAD_DIM)
    scores = (
        jnp.einsum("qad,kad->qak", query_block, key_block, preferred_element_type=jnp.float32)
        * score_scale
    )
    scores = jnp.where(valid[None, None, :], scores, -jnp.inf)
    new_max = jnp.maximum(running_max, jnp.max(scores, axis=-1))
    safe_max = jnp.where(new_max == -jnp.inf, 0.0, new_max)
    rescale = jnp.exp(running_max - safe_max)
    exp_scores = jnp.exp(scores - safe_max[:, :, None])
    new_total = running_total * rescale + jnp.sum(exp_scores, axis=-1)
    weighted = jnp.einsum(
        "qak,kad->qad",
        exp_scores.astype(jnp.bfloat16),
        value_block,
        preferred_element_type=jnp.float32,
    )
    new_acc = running_acc * rescale[:, :, None] + weighted
    return (new_max, new_total, new_acc)


def per_device(query_rows, key_rows, value_rows):
    row_count = query_rows.shape[0]
    feature_width = query_rows.shape[1]
    local_heads = feature_width // HEAD_DIM
    shards = lax.axis_size("seq")
    score_scale = HEAD_DIM ** (-0.5)
    first_out, first_lse = local_segments(query_rows, key_rows, value_rows, SEG_A, score_scale)
    used_two = row_count // 2
    seg_two = SEG_B // 2
    query_two = pick_rows(query_rows, 2)
    key_two = pick_rows(key_rows, 2)
    value_two = pick_rows(value_rows, 2)
    stacked = jnp.stack([key_two, value_two])
    for bit_index in range((seg_two // used_two).bit_length() - 1):
        partner = swapped(stacked, "seq", bit_index)
        stacked = jnp.concatenate([stacked, partner], axis=1)
    second_out, second_lse = attend_rows(query_two, stacked[0], stacked[1], score_scale)
    span_tokens = row_count * shards
    group_span = span_tokens // row_count
    used_three = row_count // 4
    wide_queries = pick_rows(query_rows, 4)
    wide_keys = pick_rows(key_rows, 4)
    wide_values = pick_rows(value_rows, 4)
    my_group = lax.axis_index("seq") // group_span
    key_limit = max(1, 1048576 // (local_heads * used_three))
    initial = (
        jnp.full((used_three, local_heads), -jnp.inf, jnp.float32),
        jnp.zeros((used_three, local_heads), jnp.float32),
        jnp.zeros((used_three, local_heads, HEAD_DIM), jnp.float32),
    )
    pieces = (
        lax.all_gather(wide_keys, "seq", axis=0, tiled=True),
        lax.all_gather(wide_values, "seq", axis=0, tiled=True),
    )
    piece_rows = pieces[0].shape[0]
    block = math.gcd(piece_rows, key_limit)
    key_blocks = pieces[0].reshape(piece_rows // block, block, feature_width)
    value_blocks = pieces[1].reshape(piece_rows // block, block, feature_width)
    block_starts = jnp.arange(piece_rows // block, dtype=jnp.int32) * block

    def fold_step(inner_state, items):
        owners = (items[2] + jnp.arange(block, dtype=jnp.int32)) // used_three
        valid = owners // group_span == my_group
        return (fold_block(inner_state, wide_queries, items[0], items[1], valid, score_scale), None)

    final_state, unused = lax.scan(fold_step, initial, (key_blocks, value_blocks, block_starts))
    final_max, final_total, final_acc = final_state
    third_out = (final_acc / final_total[:, :, None]).reshape(used_three, feature_width)
    third_lse = final_max + jnp.log(final_total)
    second_full, second_lse_full = spread_rows(second_out, second_lse, 2)
    third_full, third_lse_full = spread_rows(third_out, third_lse, 4)
    peak = jnp.maximum(jnp.maximum(first_lse, second_lse_full), third_lse_full)
    weight_one = jnp.exp(first_lse - peak)
    weight_two = jnp.exp(second_lse_full - peak)
    weight_three = jnp.exp(third_lse_full - peak)
    denominator = jnp.repeat(weight_one + weight_two + weight_three, HEAD_DIM, axis=1)
    numerator = jnp.repeat(weight_one, HEAD_DIM, axis=1) * first_out
    numerator = numerator + jnp.repeat(weight_two, HEAD_DIM, axis=1) * second_full
    numerator = numerator + jnp.repeat(weight_three, HEAD_DIM, axis=1) * third_full
    return (numerator / denominator).astype(jnp.bfloat16)


def solution(mesh):
    return jax.shard_map(
        per_device,
        mesh=mesh,
        in_specs=(
            P(("slides", "seq"), "head"),
            P(("slides", "seq"), "head"),
            P(("slides", "seq"), "head"),
        ),
        out_specs=P(("slides", "seq"), "head"),
        check_vma=False,
    )
```

profile of v0, /device:TPU:0, one launch (start us, length us, event | category | flops | bytes accessed | tf_op | source)
XLA Modules:
  0.0 164.0 jit_solution(786289299190109567)
XLA Ops:
  0.0 1.2 copy.121
  1.2 1.2 copy.120
  4.0 3.1 %collective-permute-start = (bf16[2,512,192]{2,1,0:T(8,128)(2,1)S(1)}, bf16[2,512,192]{2,1,0:T(8,128)(2,1)S(1)}, u32[]{:S(2)}, u32[]{:S(2)}) collective-permute-start(bf16[2,512,192]{2,1,0:T(8,128)(2,1)S(1)} %pad_maximum_fusion.4), channel_id=1, source_target_pairs={{0,4},{4,0},{8,12},{12,8},{1,5},{5,1},{9,13},{13,9},{2,6},{6,2},{1... | collective-permute-start | bytes 1179656 | tf_op jit(solution)/shard_map/ppermute | solution.py:15
  7.1 1.3 reshape.582
  8.4 1.3 reshape.571
  9.9 1.3 reshape.573
  11.7 1.2 fusion.69
  13.0 19.4 %all_gather.7 = bf16[1024,192]{1,0:T(8,128)(2,1)S(1)} all-gather(bf16[256,192]{1,0:T(8,128)(2,1)S(1)} %pad_maximum_fusion.8), channel_id=1, replica_groups=mesh['slides'=2,'seq'=4,'head'=4] {'seq'}, dimensions={0}, use_global_device_ids=true | all-gather | bytes 491520 | tf_op jit(solution)/shard_map/all_gather | solution.py:155
  32.5 0.9 copy.139
  33.7 14.8 %all_gather.6 = bf16[1024,192]{1,0:T(8,128)(2,1)S(1)} all-gather(bf16[256,192]{1,0:T(8,128)(2,1)S(1)} %pad_maximum_fusion.6), channel_id=1, replica_groups=mesh['slides'=2,'seq'=4,'head'=4] {'seq'}, dimensions={0}, use_global_device_ids=true | all-gather | bytes 491520 | tf_op jit(solution)/shard_map/all_gather | solution.py:154
  48.7 1.2 fusion.67
  50.1 1.4 bitcast_reduce_fusion.2
  51.5 1.9 %copy-done = f32[4,1024,256]{2,1,0:T(8,128)} copy-done((f32[4,1024,256]{2,1,0:T(8,128)}, f32[4,1024,256]{2,1,0:T(8,128)S(1)}, u32[]{:S(2)}) %copy-start) | copy-done | bytes 4194328
  53.5 0.9 fusion.28
  54.4 35.3 %while.23 = (s32[]{:T(128)}, f32[4,256,192]{1,0,2:T(4,128)}, f32[4,256,4]{1,2,0:T(4,128)}, bf16[4,256,192]{1,2,0:T(8,128)(2,1)S(1)}, bf16[1024,192]{0,1:T(8,128)...) while((s32[]{:T(128)}, f32[4,256,192]{1,0,2:T(4,128)}, f32[4,256,4]{1,2,0:T(4,128)}, ...), condition=%wide.region_3.0_spmd, body=%wide.region_0.3_spmd.sunk | while | flops 209763328 | bytes 16253061 | solution.py:52
  55.3 0.9 fusion.95
  56.3 0.9 fusion.96
  57.4 5.3 %dynamic_update_slice.29 = f32[4,256,192]{1,0,2:T(4,128)} dynamic-update-slice(f32[4,256,192]{1,0,2:T(4,128)} %get-tuple-element.357, f32[1,256,192]{1,0,2:T(1,128)S(1)} %copy.156, s32[]{:T(128)S(6)} %copy.173, s32[]{:T(128)} %constant.135.clone.1..sunk, s32[]{:T(128)} %constant.135.clone.1..sunk) | dynamic-update-slice | bytes 393220 | tf_op jit(solution)/shard_map/while/body/eval_jaxpr/while/body/jit(dynamic_update_index_in_dim)/dynamic_update_slice | solution.py:52
  64.1 0.9 fusion.95
  65.1 0.9 fusion.96
  66.2 5.3 %dynamic_update_slice.29 = f32[4,256,192]{1,0,2:T(4,128)} dynamic-update-slice(f32[4,256,192]{1,0,2:T(4,128)} %get-tuple-element.357, f32[1,256,192]{1,0,2:T(1,128)S(1)} %copy.156, s32[]{:T(128)S(6)} %copy.173, s32[]{:T(128)} %constant.135.clone.1..sunk, s32[]{:T(128)} %constant.135.clone.1..sunk) | dynamic-update-slice | bytes 393220 | tf_op jit(solution)/shard_map/while/body/eval_jaxpr/while/body/jit(dynamic_update_index_in_dim)/dynamic_update_slice | solution.py:52
  73.0 0.9 fusion.95
  73.9 0.9 fusion.96
  75.0 5.3 %dynamic_update_slice.29 = f32[4,256,192]{1,0,2:T(4,128)} dynamic-update-slice(f32[4,256,192]{1,0,2:T(4,128)} %get-tuple-element.357, f32[1,256,192]{1,0,2:T(1,128)S(1)} %copy.156, s32[]{:T(128)S(6)} %copy.173, s32[]{:T(128)} %constant.135.clone.1..sunk, s32[]{:T(128)} %constant.135.clone.1..sunk) | dynamic-update-slice | bytes 393220 | tf_op jit(solution)/shard_map/while/body/eval_jaxpr/while/body/jit(dynamic_update_index_in_dim)/dynamic_update_slice | solution.py:52
  81.8 0.9 fusion.95
  82.7 0.9 fusion.96
  83.9 5.3 %dynamic_update_slice.29 = f32[4,256,192]{1,0,2:T(4,128)} dynamic-update-slice(f32[4,256,192]{1,0,2:T(4,128)} %get-tuple-element.357, f32[1,256,192]{1,0,2:T(1,128)S(1)} %copy.156, s32[]{:T(128)S(6)} %copy.173, s32[]{:T(128)} %constant.135.clone.1..sunk, s32[]{:T(128)} %constant.135.clone.1..sunk) | dynamic-update-slice | bytes 393220 | tf_op jit(solution)/shard_map/while/body/eval_jaxpr/while/body/jit(dynamic_update_index_in_dim)/dynamic_update_slice | solution.py:52
  89.8 3.5 %fusion.38 = f32[256,4,48]{0,2,1:T(8,128)S(1)} fusion(bf16[1024,4,48]{0,2,1:T(8,128)(2,1)} %bitcast.201, f32[4,1024,256]{2,1,0:T(8,128)} %copy-done, f32[256,4]{0,1:T(4,128)S(1)} %compare_select_fusion, pred[1024]{0:T(1024)(128)(4,1)S(1)} %fusion.45, f32[256,4]{0,1:T(4,128)S(1)} %get-tuple-element.237, f32[256,4]{0,1:T(4,128)S(1)} %get-tuple-element.236), kind=kOutput, calls=%fused_computation.35 | convolution fusion | flops 104955904 | bytes 4797440 | tf_op jit(solution)/shard_map/while/body/eval_jaxpr/qak,kad->qad/dot_general | solution.py:113
  93.2 0.9 fusion.66
  94.1 0.9 bitcast_multiply_fusion.6
  95.2 1.2 copy.122
  97.2 1.1 pad_maximum_fusion.3
  99.4 1.3 pad_maximum_fusion.5
  101.5 2.2 %copy.152 = f32[24,8,4,256]{3,1,2,0:T(8,128)} copy(f32[24,8,4,256]{3,2,1,0:T(4,128)} %bitcast.199) | data formatting | bytes 1572864
  104.6 23.1 %collective-permute-done.1 = bf16[2,1024,192]{1,2,0:T(8,128)(2,1)} collective-permute-done((bf16[2,1024,192]{1,2,0:T(8,128)(2,1)}, bf16[2,1024,192]{1,2,0:T(8,128)(2,1)}, u32[]{:S(2)}, u32[]{:S(2)}) %collective-permute-start.1) | collective-permute-done | bytes 786464 | tf_op jit(solution)/shard_map/ppermute | solution.py:15
  127.7 1.3 pad_maximum_fusion
  129.1 29.1 %while.24 = (s32[]{:T(128)}, f32[4,128,192]{1,0,2:T(4,128)}, f32[4,128,4]{1,2,0:T(4,128)S(1)}, bf16[4,128,192]{1,2,0:T(8,128)(2,1)}, bf16[1,2048,192]{1,2,0:T(8,...) while((s32[]{:T(128)}, f32[4,128,192]{1,0,2:T(4,128)}, ...), condition=%wide.region_7.8_spmd, body=%wide.region_4.7_spmd.sunk | while | flops 209739264 | bytes 14614633 | solution.py:52
  130.0 0.8 bitcast_reduce_fusion.6
  131.6 0.9 fusion.102
  132.6 3.9 %dynamic_update_slice.31 = f32[4,128,192]{1,0,2:T(4,128)} dynamic-update-slice(f32[4,128,192]{1,0,2:T(4,128)} %get-tuple-element.333, f32[1,128,192]{1,0,2:T(1,128)S(1)} %bitcast.189, s32[]{:T(128)S(6)} %copy.164, s32[]{:T(128)} %constant.135.clone.1..sunk.1, s32[]{:T(128)} %constant.135.clone.1..sunk.1) | dynamic-update-slice | bytes 196612 | tf_op jit(solution)/shard_map/while/body/jit(dynamic_update_index_in_dim)/dynamic_update_slice | solution.py:52
  138.9 0.9 fusion.102
  139.8 3.9 %dynamic_update_slice.31 = f32[4,128,192]{1,0,2:T(4,128)} dynamic-update-slice(f32[4,128,192]{1,0,2:T(4,128)} %get-tuple-element.333, f32[1,128,192]{1,0,2:T(1,128)S(1)} %bitcast.189, s32[]{:T(128)S(6)} %copy.164, s32[]{:T(128)} %constant.135.clone.1..sunk.1, s32[]{:T(128)} %constant.135.clone.1..sunk.1) | dynamic-update-slice | bytes 196612 | tf_op jit(solution)/shard_map/while/body/jit(dynamic_update_index_in_dim)/dynamic_update_slice | solution.py:52
  146.2 0.9 fusion.102
  147.1 3.9 %dynamic_update_slice.31 = f32[4,128,192]{1,0,2:T(4,128)} dynamic-update-slice(f32[4,128,192]{1,0,2:T(4,128)} %get-tuple-element.333, f32[1,128,192]{1,0,2:T(1,128)S(1)} %bitcast.189, s32[]{:T(128)S(6)} %copy.164, s32[]{:T(128)} %constant.135.clone.1..sunk.1, s32[]{:T(128)} %constant.135.clone.1..sunk.1) | dynamic-update-slice | bytes 196612 | tf_op jit(solution)/shard_map/while/body/jit(dynamic_update_index_in_dim)/dynamic_update_slice | solution.py:52
  153.4 0.9 fusion.102
  154.4 3.9 %dynamic_update_slice.31 = f32[4,128,192]{1,0,2:T(4,128)} dynamic-update-slice(f32[4,128,192]{1,0,2:T(4,128)} %get-tuple-element.333, f32[1,128,192]{1,0,2:T(1,128)S(1)} %bitcast.189, s32[]{:T(128)S(6)} %copy.164, s32[]{:T(128)} %constant.135.clone.1..sunk.1, s32[]{:T(128)} %constant.135.clone.1..sunk.1) | dynamic-update-slice | bytes 196612 | tf_op jit(solution)/shard_map/while/body/jit(dynamic_update_index_in_dim)/dynamic_update_slice | solution.py:52
  158.3 1.2 reshape.579
  161.9 2.2 %fusion.41 = bf16[1024,192]{0,1:T(8,128)(2,1)} fusion(f32[1024,192]{0,1:T(8,128)S(1)} %copy.142, f32[1024,192]{0,1:T(8,128)S(1)} %copy.137, f32[1024,192]{0,1:T(8,128)} %bitcast.193, f32[1024,4]{0,1:T(4,128)S(1)} %get-tuple-element.189, f32[1024,4]{0,1:T(4,128)S(1)} %get-tuple-element.192, f32[1024,4]{0,1:T(4,128)S(1)} %get-tuple-element.190, ...), kind=kLoop, calls=%fused_computation.40 | loop fusion | flops 1376256 | bytes 2818048 | tf_op jit(solution)/shard_map/convert_element_type | solution.py:182
  (121 shorter events, 25.1 us)
Async XLA Ops:
  2.4 7.2 %copy-start.2 = (bf16[1024,192]{0,1:T(8,128)(2,1)S(1)}, bf16[1024,192]{0,1:T(8,128)(2,1)}, u32[]{:S(2)}) copy-start(bf16[1024,192]{0,1:T(8,128)(2,1)} %param.19) | copy-start | bytes 1179652
  4.0 91.0 %collective-permute-start = (bf16[2,512,192]{2,1,0:T(8,128)(2,1)S(1)}, bf16[2,512,192]{2,1,0:T(8,128)(2,1)S(1)}, u32[]{:S(2)}, u32[]{:S(2)}) collective-permute-start(bf16[2,512,192]{2,1,0:T(8,128)(2,1)S(1)} %pad_maximum_fusion.4), channel_id=1, source_target_pairs={{0,4},{4,0},{8,12},{12,8},{1,5},{5,1},{9,13},{13,9},{2,6},{6,2},{1... | collective-permute-start | bytes 1179656 | tf_op jit(solution)/shard_map/ppermute | solution.py:15
  9.9 23.6 %copy-start.4 = (bf16[256,768]{1,0:T(8,128)(2,1)S(1)}, bf16[256,768]{1,0:T(8,128)(2,1)}, u32[]{:S(2)}) copy-start(bf16[256,768]{1,0:T(8,128)(2,1)} %reshape.571) | copy-start | bytes 1179652
  50.1 4.3 %copy-start.3 = (bf16[1024,192]{0,1:T(8,128)(2,1)S(1)}, bf16[1024,192]{0,1:T(8,128)(2,1)}, u32[]{:S(2)}) copy-start(bf16[1024,192]{0,1:T(8,128)(2,1)} %param.19) | copy-start | bytes 1179652
  50.1 4.3 %copy-start.1 = (bf16[1024,192]{0,1:T(8,128)(2,1)S(1)}, bf16[1024,192]{0,1:T(8,128)(2,1)}, u32[]{:S(2)}) copy-start(bf16[1024,192]{0,1:T(8,128)(2,1)} %param.20) | copy-start | bytes 1179652
  51.5 1.9 %copy-start = (f32[4,1024,256]{2,1,0:T(8,128)}, f32[4,1024,256]{2,1,0:T(8,128)S(1)}, u32[]{:S(2)}) copy-start(f32[4,1024,256]{2,1,0:T(8,128)S(1)} %get-tuple-element.239) | copy-start | bytes 12582916
  54.5 1.8 %copy-start.5 = (bf16[1024,192]{0,1:T(8,128)(2,1)S(1)}, bf16[1024,192]{0,1:T(8,128)(2,1)}, u32[]{:S(2)}) copy-start(bf16[1024,192]{0,1:T(8,128)(2,1)} %get-tuple-element.369) | copy-start | bytes 1179652 | tf_op jit(solution)/shard_map/while/body/eval_jaxpr/while
  63.3 1.8 %copy-start.5 = (bf16[1024,192]{0,1:T(8,128)(2,1)S(1)}, bf16[1024,192]{0,1:T(8,128)(2,1)}, u32[]{:S(2)}) copy-start(bf16[1024,192]{0,1:T(8,128)(2,1)} %get-tuple-element.369) | copy-start | bytes 1179652 | tf_op jit(solution)/shard_map/while/body/eval_jaxpr/while
  72.1 1.8 %copy-start.5 = (bf16[1024,192]{0,1:T(8,128)(2,1)S(1)}, bf16[1024,192]{0,1:T(8,128)(2,1)}, u32[]{:S(2)}) copy-start(bf16[1024,192]{0,1:T(8,128)(2,1)} %get-tuple-element.369) | copy-start | bytes 1179652 | tf_op jit(solution)/shard_map/while/body/eval_jaxpr/while
  80.9 1.8 %copy-start.5 = (bf16[1024,192]{0,1:T(8,128)(2,1)S(1)}, bf16[1024,192]{0,1:T(8,128)(2,1)}, u32[]{:S(2)}) copy-start(bf16[1024,192]{0,1:T(8,128)(2,1)} %get-tuple-element.369) | copy-start | bytes 1179652 | tf_op jit(solution)/shard_map/while/body/eval_jaxpr/while
  89.7 4.4 %copy-start.9 = (f32[192]{0:T(256)S(1)}, f32[192]{0:T(256)}, u32[]{:S(2)}) copy-start(f32[192]{0:T(256)} %constant.151.clone) | copy-start | bytes 2308
  89.7 4.4 %copy-start.10 = (f32[192]{0:T(256)S(1)}, f32[192]{0:T(256)}, u32[]{:S(2)}) copy-start(f32[192]{0:T(256)} %constant.153.clone) | copy-start | bytes 2308
  89.8 4.4 %copy-start.11 = (f32[192]{0:T(256)S(1)}, f32[192]{0:T(256)}, u32[]{:S(2)}) copy-start(f32[192]{0:T(256)} %constant.155.clone) | copy-start | bytes 2308
  89.8 4.4 %copy-start.12 = (f32[192]{0:T(256)S(1)}, f32[192]{0:T(256)}, u32[]{:S(2)}) copy-start(f32[192]{0:T(256)} %constant.157.clone) | copy-start | bytes 2308
  96.5 31.2 %collective-permute-start.1 = (bf16[2,1024,192]{1,2,0:T(8,128)(2,1)}, bf16[2,1024,192]{1,2,0:T(8,128)(2,1)}, u32[]{:S(2)}, u32[]{:S(2)}) collective-permute-start(bf16[2,1024,192]{1,2,0:T(8,128)(2,1)} %copy.122), channel_id=1, source_target_pairs={{0,8},{4,12},{8,0},{12,4},{1,9},{5,13},{9,1},{13,5},{2,10},{6,14},... | collective-permute-start | bytes 2359304 | tf_op jit(solution)/shard_map/ppermute | solution.py:15
  98.3 5.4 %copy-start.18 = (pred[4]{0:T(512)(128)(4,1)S(1)}, pred[4]{0:T(512)(128)(4,1)}, u32[]{:S(2)}) copy-start(pred[4]{0:T(512)(128)(4,1)} %constant.152.clone) | copy-start | bytes 16
  98.3 5.5 %copy-start.15 = (pred[4]{0:T(512)(128)(4,1)S(1)}, pred[4]{0:T(512)(128)(4,1)}, u32[]{:S(2)}) copy-start(pred[4]{0:T(512)(128)(4,1)} %constant.154.clone) | copy-start | bytes 16
  98.3 5.5 %copy-start.16 = (pred[4]{0:T(512)(128)(4,1)S(1)}, pred[4]{0:T(512)(128)(4,1)}, u32[]{:S(2)}) copy-start(pred[4]{0:T(512)(128)(4,1)} %constant.156.clone) | copy-start | bytes 16
  98.3 5.5 %copy-start.17 = (pred[4]{0:T(512)(128)(4,1)S(1)}, pred[4]{0:T(512)(128)(4,1)}, u32[]{:S(2)}) copy-start(pred[4]{0:T(512)(128)(4,1)} %constant.158.clone) | copy-start | bytes 16
  129.1 30.3 %copy-start.7 = (f32[192]{0:T(256)S(1)}, f32[192]{0:T(256)}, u32[]{:S(2)}) copy-start(f32[192]{0:T(256)} %constant.147.clone) | copy-start | bytes 2308
  129.1 30.3 %copy-start.8 = (f32[192]{0:T(256)S(1)}, f32[192]{0:T(256)}, u32[]{:S(2)}) copy-start(f32[192]{0:T(256)} %constant.149.clone) | copy-start | bytes 2308
  159.4 1.8 %copy-start.13 = (pred[4]{0:T(512)(128)(4,1)S(1)}, pred[4]{0:T(512)(128)(4,1)}, u32[]{:S(2)}) copy-start(pred[4]{0:T(512)(128)(4,1)} %constant.148.clone) | copy-start | bytes 16
  159.4 1.8 %copy-start.14 = (pred[4]{0:T(512)(128)(4,1)S(1)}, pred[4]{0:T(512)(128)(4,1)}, u32[]{:S(2)}) copy-start(pred[4]{0:T(512)(128)(4,1)} %constant.150.clone) | copy-start | bytes 16
  159.6 2.3 %copy-start.6 = (f32[4,256,4]{1,2,0:T(4,128)S(1)}, f32[4,256,4]{1,2,0:T(4,128)}, u32[]{:S(2)}) copy-start(f32[4,256,4]{1,2,0:T(4,128)} %get-tuple-element.113) | copy-start | bytes 49156
where the time goes:
time: 165 us; the launch traced here: 164 us
  local copies, waits for them, and re-layouts  64.5 us (39%)
  blocking collectives  34.2 us (21%)
  waiting for transfers between devices  23.1 us (14%)
  matrix products  18.9 us (11%)
  other arithmetic  18.8 us (11%)
  starting transfers between devices  3.83 us (2%)
    dynamic_update_slice x12, local copies, waits for them, and re-layouts, attend_rows(): lax.map(one_piece, query_flat.reshape(count // rows, rows, feature_width))  37.4 us
    ppermute x2, waiting for transfers between devices, swapped(): lax.ppermute(shard, axis, [(i, i ^ 1 << stride) for i in range(lax.axis_s...  23.1 us
    all_gather x1, blocking collectives, per_device(): lax.all_gather(wide_values, 'seq', axis=0, tiled=True)  19.4 us
    all_gather x1, blocking collectives, per_device(): lax.all_gather(wide_keys, 'seq', axis=0, tiled=True)  14.8 us
    dot_general x8, matrix products, attend(): jnp.einsum('qak,kad->qad', exp_scores.astype(jnp.bfloat16), value_block,...  7.47 us
    reduce_sum x8, other arithmetic, attend(): row_total = jnp.sum(exp_scores, axis=-1)  7.01 us
    unnamed x40, local copies, waits for them, and re-layouts  6.78 us
    dot_general x8, matrix products, attend(): jnp.einsum('qad,kad->qak', query_block, key_block, preferred_element_type...  6.63 us
  transfers between devices with their start and end apart: 2, of which 1 were waited for; matrix products, arithmetic and copies ran while one was open for 36% of the time, Pallas kernels for 0%

commit v1 on v0

--- a/solution.py
+++ b/solution.py
@@ -4,6 +4,8 @@
 import jax.numpy as jnp
 import numpy as np
 from jax import lax
+from jax.experimental import pallas as pl
+from jax.experimental.pallas import tpu as pltpu
 from jax.sharding import PartitionSpec as P
 
 HEAD_DIM = 48
@@ -120,7 +122,7 @@
     return (new_max, new_total, new_acc)
 
 
-def per_device(query_rows, key_rows, value_rows):
+def any_length(query_rows, key_rows, value_rows):
     row_count = query_rows.shape[0]
     feature_width = query_rows.shape[1]
     local_heads = feature_width // HEAD_DIM
@@ -182,6 +184,211 @@
     return (numerator / denominator).astype(jnp.bfloat16)
 
 
+STRIDES = 4
+LANES = 128
+LOG2E = 1.4426950408889634
+VMEM_BYTES = 60 * 1024 * 1024
+
+
+def dot_nn(left, right):
+    return lax.dot_general(left, right, (((1,), (0,)), ((), ())), preferred_element_type=jnp.float32)
+
+
+def dot_nt(left, right):
+    return lax.dot_general(left, right, (((1,), (1,)), ((), ())), preferred_element_type=jnp.float32)
+
+
+def identity(size):
+    rows = lax.broadcasted_iota(jnp.int32, (size, size), 0)
+    columns = lax.broadcasted_iota(jnp.int32, (size, size), 1)
+    return jnp.where(rows == columns, 1.0, 0.0).astype(jnp.bfloat16)
+
+
+def call(kernel, outs, args, scratch, flops):
+    return pl.pallas_call(
+        kernel,
+        out_shape=outs,
+        in_specs=[pl.BlockSpec(memory_space=pltpu.VMEM)] * len(args),
+        out_specs=jax.tree.map(lambda out: pl.BlockSpec(memory_space=pltpu.VMEM), outs),
+        scratch_shapes=scratch,
+        compiler_params=pltpu.CompilerParams(vmem_limit_bytes=VMEM_BYTES),
+        cost_estimate=pl.CostEstimate(flops=flops, bytes_accessed=4 << 20, transcendentals=0),
+    )(*args)
+
+
+def pack_kernel(q_ref, k_ref, v_ref, m0, m1, m2, m3, qt_ref, kc_ref, vt_ref, wide, by_head):
+    rows, width = q_ref.shape
+    heads = width // HEAD_DIM
+    part = rows // STRIDES
+    eye = identity(width)
+    for which, (ref, turned) in enumerate(((q_ref, qt_ref), (k_ref, None), (v_ref, vt_ref))):
+        full = ref[...].astype(jnp.float32)
+        wide[0] = full[:, :LANES]
+        wide[1, :, pl.ds(0, width - LANES)] = full[:, LANES:]
+        for phase in range(STRIDES):
+            spread = pl.ds(phase, part, stride=STRIDES)
+            chunk = jnp.concatenate([wide[0, spread, :], wide[1, spread, :][:, : width - LANES]], axis=1).astype(jnp.bfloat16)
+            if which == 1:
+                kc_ref[pl.ds(phase * part, part), :] = chunk
+            flat = dot_nt(eye, chunk).astype(jnp.bfloat16)
+            if turned is not None:
+                turned[:, pl.ds(phase * part, part)] = flat
+            for head in range(heads):
+                offset = (phase - head) % STRIDES
+                if offset % 2 == 0:
+                    by_head[head, pl.ds(which * HEAD_DIM, HEAD_DIM), pl.ds(offset // 2 * part, part)] = flat[
+                        head * HEAD_DIM : (head + 1) * HEAD_DIM
+                    ]
+    me = lax.axis_index("seq")
+    for shift, message in enumerate((m0, m1, m2, m3)):
+        message[...] = by_head[lax.rem(me + shift, heads)]
+
+
+def with_ones(block):
+    count = block.shape[1]
+    extra = jnp.where(lax.broadcasted_iota(jnp.int32, (16, count), 0) == 0, 1.0, 0.0).astype(jnp.bfloat16)
+    return jnp.concatenate([block, extra], axis=0)
+
+
+def near_kernel(qt_ref, kc_ref, vt_ref, out_ref):
+    width, rows = qt_ref.shape
+    heads = width // HEAD_DIM
+    part = rows // STRIDES
+    factor = HEAD_DIM ** (-0.5) * LOG2E
+    for head in range(heads):
+        features = pl.ds(head * HEAD_DIM, HEAD_DIM)
+        keys = kc_ref[...][:, head * HEAD_DIM : (head + 1) * HEAD_DIM]
+        values = with_ones(vt_ref[features, :])
+        for piece in range(STRIDES):
+            lanes = pl.ds(piece * part, part)
+            scores = dot_nn(keys, qt_ref[features, lanes])
+            top = jnp.max(scores, axis=0, keepdims=True) * factor
+            probs = jnp.exp2(scores * factor - top).astype(jnp.bfloat16)
+            out_ref[head, :, lanes] = dot_nn(values, probs)
+            out_ref[head, pl.ds(HEAD_DIM + 1, 1), lanes] = top
+
+
+def far_kernel(m0, m1, m2, m3, o0, o1, o2, o3, keys_ref):
+    count = m0.shape[1]
+    half = count // 2
+    factor = HEAD_DIM ** (-0.5) * LOG2E
+    sources = (m0, m1, m2, m3)
+    eye = identity(count)
+    for at, source in enumerate(sources):
+        keys_ref[pl.ds(at * count, count), :] = dot_nt(eye, source[pl.ds(HEAD_DIM, HEAD_DIM), :]).astype(jnp.bfloat16)
+    values = [with_ones(source[pl.ds(2 * HEAD_DIM, HEAD_DIM), :]) for source in sources]
+    for source, out in zip(sources, (o0, o1, o2, o3)):
+        for klass in range(2):
+            lanes = pl.ds(klass * half, half)
+            scores = dot_nn(keys_ref[...], source[pl.ds(0, HEAD_DIM), lanes])
+            top = jnp.max(scores, axis=0, keepdims=True) * factor
+            twice = top - 1.0 if klass == 0 else top
+            acc = jnp.zeros((HEAD_DIM + 16, half), jnp.float32)
+            for at in range(len(sources)):
+                first = jnp.exp2(scores[at * count : at * count + half] * factor - twice).astype(jnp.bfloat16)
+                second = jnp.exp2(scores[at * count + half : (at + 1) * count] * factor - top).astype(jnp.bfloat16)
+                acc = acc + dot_nn(values[at], jnp.concatenate([first, second], axis=0))
+            total = acc[HEAD_DIM : HEAD_DIM + 1]
+            lse = top + jnp.log2(total)
+            high = lse.astype(jnp.bfloat16)
+            rest = lse - high.astype(jnp.float32)
+            middle = rest.astype(jnp.bfloat16)
+            low = (rest - middle.astype(jnp.float32)).astype(jnp.bfloat16)
+            row = lax.broadcasted_iota(jnp.int32, (16, half), 0)
+            parts = jnp.where(row == 0, high.astype(jnp.float32), 0.0)
+            parts = jnp.where(row == 1, middle.astype(jnp.float32), parts)
+            parts = jnp.where(row == 2, low.astype(jnp.float32), parts)
+            out[pl.ds(0, HEAD_DIM), lanes] = (acc[:HEAD_DIM] / total).astype(jnp.bfloat16)
+            out[pl.ds(HEAD_DIM, 16), lanes] = parts.astype(jnp.bfloat16)
+
+
+def merge_kernel(near_ref, g0, g1, g2, g3, out_ref, by_head, wide):
+    heads = near_ref.shape[0]
+    rows = near_ref.shape[2]
+    part = rows // STRIDES
+    me = lax.axis_index("seq")
+    for shift, result in enumerate((g0, g1, g2, g3)):
+        by_head[lax.rem(me + shift, heads)] = result[...]
+    eye = identity(part)
+    for phase in range(STRIDES):
+        lanes = pl.ds(phase * part, part)
+        columns = []
+        for head in range(heads):
+            near = near_ref[head, pl.ds(0, HEAD_DIM), lanes]
+            total = near_ref[head, pl.ds(HEAD_DIM, 1), lanes]
+            offset = (phase - head) % STRIDES
+            if offset % 2 == 0:
+                top = near_ref[head, pl.ds(HEAD_DIM + 1, 1), lanes]
+                there = by_head[head, :, pl.ds(offset // 2 * part, part)].astype(jnp.float32)
+                lse = there[HEAD_DIM : HEAD_DIM + 1] + there[HEAD_DIM + 1 : HEAD_DIM + 2] + there[HEAD_DIM + 2 : HEAD_DIM + 3]
+                peak = jnp.maximum(top, lse)
+                weight = jnp.exp2(top - peak)
+                far = jnp.exp2(lse - peak)
+                near = near * weight + there[:HEAD_DIM] * far
+                total = total * weight + far
+            columns.append((near / total).astype(jnp.bfloat16))
+        padding = [jnp.zeros((2 * LANES - heads * HEAD_DIM, part), jnp.bfloat16)]
+        upright = dot_nt(eye, jnp.concatenate(columns + padding, axis=0))
+        wide[0, pl.ds(phase, part, stride=STRIDES), :] = upright[:, :LANES]
+        wide[1, pl.ds(phase, part, stride=STRIDES), :] = upright[:, LANES:]
+    out_ref[:, pl.ds(0, LANES)] = wide[0].astype(jnp.bfloat16)
+    out_ref[:, pl.ds(LANES, heads * HEAD_DIM - LANES)] = wide[1][:, : heads * HEAD_DIM - LANES].astype(jnp.bfloat16)
+
+
+def by_rotation(blocks, sign):
+    shards = lax.axis_size("seq")
+    moved = [blocks[0]]
+    for shift in range(1, shards):
+        moved.append(lax.ppermute(blocks[shift], "seq", [(i, (i + sign * shift) % shards) for i in range(shards)]))
+    return moved
+
+
+def whole_slide(query_rows, key_rows, value_rows):
+    rows, width = query_rows.shape
+    heads = width // HEAD_DIM
+    half = rows // 2
+    bf16, f32 = jnp.bfloat16, jnp.float32
+    message = jax.ShapeDtypeStruct((3 * HEAD_DIM, half), bf16)
+    packed = call(
+        pack_kernel,
+        [message] * heads + [jax.ShapeDtypeStruct(s, bf16) for s in ((width, rows), (rows, width), (width, rows))],
+        (query_rows, key_rows, value_rows),
+        [pltpu.VMEM((2, rows, LANES), f32), pltpu.VMEM((heads, 3 * HEAD_DIM, half), bf16)],
+        1 << 28,
+    )
+    arrived = by_rotation(packed[:heads], 1)
+    near = call(
+        near_kernel,
+        jax.ShapeDtypeStruct((heads, HEAD_DIM + 16, rows), f32),
+        packed[heads:],
+        [],
+        4 * heads * rows * rows * 256,
+    )
+    far = call(
+        far_kernel,
+        [jax.ShapeDtypeStruct((HEAD_DIM + 16, half), bf16)] * heads,
+        arrived,
+        [pltpu.VMEM((heads * half, HEAD_DIM), bf16)],
+        4 * heads * rows * rows * 256,
+    )
+    back = by_rotation(far, -1)
+    return call(
+        merge_kernel,
+        jax.ShapeDtypeStruct((rows, width), bf16),
+        [near, *back],
+        [pltpu.VMEM((heads, HEAD_DIM + 16, half), bf16), pltpu.VMEM((2, rows, LANES), f32)],
+        1 << 28,
+    )
+
+
+def per_device(query_rows, key_rows, value_rows):
+    rows, width = query_rows.shape
+    shards = lax.axis_size("seq")
+    if rows == SEG_A and rows * shards == SEG_B and width == shards * HEAD_DIM and shards == STRIDES and LANES < width <= 2 * LANES:
+        return whole_slide(query_rows, key_rows, value_rows)
+    return any_length(query_rows, key_rows, value_rows)
+
+
 def solution(mesh):
     return jax.shard_map(
         per_device,

time: 165 us -> 60.1 us (0.36)
  local copies, waits for them, and re-layouts: 64.5 us -> 7.4 us
  blocking collectives: 34.2 us -> 0 us
  Pallas kernels: 0 us -> 31.5 us
  matrix products: 18.9 us -> 0 us
  other arithmetic: 18.8 us -> 0 us
  waiting for transfers between devices: 23.1 us -> 8.57 us
  starting transfers between devices: 3.83 us -> 12.2 us
    dynamic_update_slice x12 -> x0, local copies, waits for them, and re-layouts: 37.4 us -> none  [attend_rows(): lax.map(one_piece, query_flat.reshape(count // rows, rows, feature_width))]
    all_gather x2 -> x0, blocking collectives: 34.2 us -> none  [the longest x1 19.4 us: per_device(): lax.all_gather(wide_values, 'seq', axis=0, tiled=True)]
    pallas_call x0 -> x4, Pallas kernels: none -> 31.5 us  [call(): pl.pallas_call(kernel, out_shape=outs, in_specs=[pl.BlockSpec(memory_spac...]
    dot_general x18 -> x0, matrix products: 18.9 us -> none  [the longest x8 7.47 us: attend(): jnp.einsum('qak,kad->qad', exp_scores.astype(jnp.bfloat16), value_block,...]
    ppermute x2 -> x6, waiting for transfers between devices: 23.1 us -> 8.57 us  [by_rotation(): lax.ppermute(blocks[shift], 'seq', [(i, (i + sign * shift) % shards) for...]
    ppermute x2 -> x6, starting transfers between devices: 3.83 us -> 12.2 us  [by_rotation(): lax.ppermute(blocks[shift], 'seq', [(i, (i + sign * shift) % shards) for...]
    reshape x14 -> x0, local copies, waits for them, and re-layouts: 8.13 us -> none  [the longest x6 4.75 us: pick_rows(): grid = block.reshape(row_count // stride, stride * feature_width)]
    reduce_sum x9 -> x0, other arithmetic: 7.93 us -> none  [the longest x8 7.01 us: attend(): row_total = jnp.sum(exp_scores, axis=-1)]
  transfers between devices with their start and end apart: 2 -> 6, of which waited for: 1 -> 2; matrix products, arithmetic and copies ran while one was open for 36% -> 0% of each run, Pallas kernels for 0% -> 23%
where the time goes in v1:
time: 60.1 us; the launch traced here: 59.8 us
  Pallas kernels  31.5 us (52%)
  starting transfers between devices  12.2 us (20%)
  waiting for transfers between devices  8.57 us (14%)
  local copies, waits for them, and re-layouts  7.4 us (12%)
    pallas_call x4, Pallas kernels, call(): pl.pallas_call(kernel, out_shape=outs, in_specs=[pl.BlockSpec(memory_spac...  31.5 us
    ppermute x6, starting transfers between devices, by_rotation(): lax.ppermute(blocks[shift], 'seq', [(i, (i + sign * shift) % shards) for...  12.2 us
    ppermute x6, waiting for transfers between devices, by_rotation(): lax.ppermute(blocks[shift], 'seq', [(i, (i + sign * shift) % shards) for...  8.57 us
    unnamed x19, local copies, waits for them, and re-layouts  5.42 us
    pallas_call x1, local copies, waits for them, and re-layouts, call(): pl.pallas_call(kernel, out_shape=outs, in_specs=[pl.BlockSpec(memory_spac...  1.98 us
  transfers between devices with their start and end apart: 6, of which 2 were waited for; matrix products, arithmetic and copies ran while one was open for 0% of the time, Pallas kernels for 23%

profile of v1, /device:TPU:0, one launch (start us, length us, event | category | flops | bytes accessed | tf_op | source)
XLA Modules:
  0.0 59.8 jit_solution(10839744163893335665)
XLA Ops:
  0.0 0.0 copy-start
  0.0 2.0 %copy.4.q_ref = bf16[1024,192]{1,0:T(8,128)(2,1)} copy(bf16[1024,192]{0,1:T(8,128)(2,1)} %param.3) | data formatting | bytes 786432 | tf_op args[0]
  2.0 0.0 copy-done
  2.0 0.0 copy-start.1
  2.0 1.0 %copy.5.k_ref = bf16[1024,192]{1,0:T(8,128)(2,1)} copy(bf16[1024,192]{0,1:T(8,128)(2,1)S(1)} %copy-done) | data formatting | bytes 786432 | tf_op args[1]
  3.1 0.0 copy-done.1
  3.1 1.0 %copy.6.v_ref = bf16[1024,192]{1,0:T(8,128)(2,1)} copy(bf16[1024,192]{0,1:T(8,128)(2,1)S(1)} %copy-done.1) | data formatting | bytes 786432 | tf_op args[2]
  4.1 3.2 %shard_map.37 = (bf16[144,512]{1,0:T(8,128)(2,1)}, bf16[144,512]{1,0:T(8,128)(2,1)}, bf16[144,512]{1,0:T(8,128)(2,1)}, bf16[144,512]{1,0:T(8,128)(2,1)}, bf16[19...) custom-call(bf16[1024,192]{1,0:T(8,128)(2,1)} %copy.4.q_ref, ...), custom_call_target="tpu_custom_call" | custom-call | flops 268435456 | bytes 4194304 | tf_op jit(solution)/shard_map/pallas_call | solution.py:208
  7.3 3.0 %collective-permute-start = (bf16[144,512]{1,0:T(8,128)(2,1)}, bf16[144,512]{1,0:T(8,128)(2,1)S(1)}, u32[]{:S(2)}, u32[]{:S(2)}) collective-permute-start(bf16[144,512]{1,0:T(8,128)(2,1)} %get-tuple-element.20), channel_id=1, source_target_pairs={{0,4},{4,8},{8,12},{12,0},{1,5},{5,9},{9,13},{13,1},{2,6},{6,10},{... | collective-permute-start | bytes 442376 | tf_op jit(solution)/shard_map/ppermute | solution.py:342
  10.3 2.6 %collective-permute-start.1 = (bf16[144,512]{1,0:T(8,128)(2,1)}, bf16[144,512]{1,0:T(8,128)(2,1)S(1)}, u32[]{:S(2)}, u32[]{:S(2)}) collective-permute-start(bf16[144,512]{1,0:T(8,128)(2,1)} %get-tuple-element.21), channel_id=1, source_target_pairs={{0,8},{4,12},{8,0},{12,4},{1,9},{5,13},{9,1},{13,5},{2,10},{6,14},... | collective-permute-start | bytes 442376 | tf_op jit(solution)/shard_map/ppermute | solution.py:342
  12.9 1.3 %collective-permute-start.2 = (bf16[144,512]{1,0:T(8,128)(2,1)}, bf16[144,512]{1,0:T(8,128)(2,1)S(1)}, u32[]{:S(2)}, u32[]{:S(2)}) collective-permute-start(bf16[144,512]{1,0:T(8,128)(2,1)} %get-tuple-element.22), channel_id=1, source_target_pairs={{0,12},{4,0},{8,4},{12,8},{1,13},{5,1},{9,5},{13,9},{2,14},{6,2},{... | collective-permute-start | bytes 442376 | tf_op jit(solution)/shard_map/ppermute | solution.py:342
  14.3 3.1 %collective-permute-done.m1 = bf16[144,512]{1,0:T(8,128)(2,1)S(1)} collective-permute-done((bf16[144,512]{1,0:T(8,128)(2,1)}, bf16[144,512]{1,0:T(8,128)(2,1)S(1)}, u32[]{:S(2)}, u32[]{:S(2)}) %collective-permute-start) | collective-permute-done | bytes 147488 | tf_op jit(solution)/shard_map/ppermute | solution.py:342
  17.3 0.0 copy-start.5
  17.3 5.5 %collective-permute-done.1.m2 = bf16[144,512]{1,0:T(8,128)(2,1)S(1)} collective-permute-done((bf16[144,512]{1,0:T(8,128)(2,1)}, bf16[144,512]{1,0:T(8,128)(2,1)S(1)}, u32[]{:S(2)}, u32[]{:S(2)}) %collective-permute-start.1) | collective-permute-done | bytes 147488 | tf_op jit(solution)/shard_map/ppermute | solution.py:342
  22.8 0.0 copy-start.6
  22.8 0.0 collective-permute-done.2.m3
  22.8 0.0 copy-start.7
  22.8 0.0 copy-done.5
  22.8 0.6 %copy-done.6 = bf16[144,512]{1,0:T(8,128)(2,1)} copy-done((bf16[144,512]{1,0:T(8,128)(2,1)}, bf16[144,512]{1,0:T(8,128)(2,1)S(1)}, u32[]{:S(2)}) %copy-start.6) | copy-done | bytes 147480
  23.5 0.1 copy-done.7
  23.6 12.1 %shard_map.39 = (bf16[64,512]{1,0:T(8,128)(2,1)}, bf16[64,512]{1,0:T(8,128)(2,1)}, bf16[64,512]{1,0:T(8,128)(2,1)}, bf16[64,512]{1,0:T(8,128)(2,1)}) custom-call(bf16[144,512]{1,0:T(8,128)(2,1)} %get-tuple-element.19.m0, bf16[144,512]{1,0:T(8,128)(2,1)} %copy-done.5, bf16[144,512]{1,0:T(8,128)(2,1)} %copy-done.6, bf16[144,512]{1,0:T(8,128)(2,1)} %copy-done.7), custom_call_target="tpu_custom_call" | custom-call | flops 4294967296 | bytes 4194304 | tf_op jit(solution)/shard_map/pallas_call | solution.py:208
  35.7 4.7 %collective-permute-start.3 = (bf16[64,512]{1,0:T(8,128)(2,1)}, bf16[64,512]{1,0:T(8,128)(2,1)S(1)}, u32[]{:S(2)}, u32[]{:S(2)}) collective-permute-start(bf16[64,512]{1,0:T(8,128)(2,1)} %get-tuple-element.24), channel_id=1, source_target_pairs={{0,12},{4,0},{8,4},{12,8},{1,13},{5,1},{9,5},{13,9},{2,14},{6,2},{... | collective-permute-start | bytes 196616 | tf_op jit(solution)/shard_map/ppermute | solution.py:342
  40.4 0.3 collective-permute-start.4
  40.7 0.2 collective-permute-start.5
  40.9 13.6 %shard_map.38.near_ref = f32[4,64,1024]{2,1,0:T(8,128)} custom-call(bf16[192,1024]{1,0:T(8,128)(2,1)} %get-tuple-element.16.qt_ref, bf16[1024,192]{1,0:T(8,128)(2,1)} %get-tuple-element.17.kc_ref, bf16[192,1024]{1,0:T(8,128)(2,1)} %get-tuple-element.18.vt_ref), custom_call_target="tpu_custom_call" | custom-call | flops 4294967296 | bytes 4194304 | tf_op jit(solution)/shard_map/pallas_call | solution.py:208
  54.5 0.0 collective-permute-done.3.g1
  54.5 0.0 copy-start.2
  54.5 0.0 collective-permute-done.4.g2
  54.5 0.0 copy-start.3
  54.5 0.0 collective-permute-done.5.g3
  54.6 0.0 copy-start.4
  54.6 0.6 copy-done.2
  55.2 0.0 copy-done.3
  55.2 0.0 copy-done.4
  55.2 2.6 %shard_map.40 = bf16[1024,192]{1,0:T(8,128)(2,1)} custom-call(f32[4,64,1024]{2,1,0:T(8,128)} %shard_map.38.near_ref, bf16[64,512]{1,0:T(8,128)(2,1)} %get-tuple-element.23.g0, bf16[64,512]{1,0:T(8,128)(2,1)} %copy-done.2, bf16[64,512]{1,0:T(8,128)(2,1)} %copy-done.3, bf16[64,512]{1,0:T(8,128)(2,1)} %copy-done.4), custom_call_target="tpu_custom_call" | custom-call | flops 268435456 | bytes 4194304 | tf_op jit(solution)/shard_map/pallas_call | solution.py:208
  57.8 2.0 %copy.7 = bf16[1024,192]{0,1:T(8,128)(2,1)} copy(bf16[1024,192]{1,0:T(8,128)(2,1)} %shard_map.40) | data formatting | bytes 786432 | tf_op jit(solution)/shard_map/pallas_call | solution.py:208
Async XLA Ops:
  0.0 2.0 %copy-start = (bf16[1024,192]{0,1:T(8,128)(2,1)S(1)}, bf16[1024,192]{0,1:T(8,128)(2,1)}, u32[]{:S(2)}) copy-start(bf16[1024,192]{0,1:T(8,128)(2,1)} %param.4) | copy-start | bytes 1179652
  2.0 1.0 %copy-start.1 = (bf16[1024,192]{0,1:T(8,128)(2,1)S(1)}, bf16[1024,192]{0,1:T(8,128)(2,1)}, u32[]{:S(2)}) copy-start(bf16[1024,192]{0,1:T(8,128)(2,1)} %param.5) | copy-start | bytes 1179652
  7.3 10.0 %collective-permute-start = (bf16[144,512]{1,0:T(8,128)(2,1)}, bf16[144,512]{1,0:T(8,128)(2,1)S(1)}, u32[]{:S(2)}, u32[]{:S(2)}) collective-permute-start(bf16[144,512]{1,0:T(8,128)(2,1)} %get-tuple-element.20), channel_id=1, source_target_pairs={{0,4},{4,8},{8,12},{12,0},{1,5},{5,9},{9,13},{13,1},{2,6},{6,10},{... | collective-permute-start | bytes 442376 | tf_op jit(solution)/shard_map/ppermute | solution.py:342
  10.3 12.5 %collective-permute-start.1 = (bf16[144,512]{1,0:T(8,128)(2,1)}, bf16[144,512]{1,0:T(8,128)(2,1)S(1)}, u32[]{:S(2)}, u32[]{:S(2)}) collective-permute-start(bf16[144,512]{1,0:T(8,128)(2,1)} %get-tuple-element.21), channel_id=1, source_target_pairs={{0,8},{4,12},{8,0},{12,4},{1,9},{5,13},{9,1},{13,5},{2,10},{6,14},... | collective-permute-start | bytes 442376 | tf_op jit(solution)/shard_map/ppermute | solution.py:342
  12.9 9.9 %collective-permute-start.2 = (bf16[144,512]{1,0:T(8,128)(2,1)}, bf16[144,512]{1,0:T(8,128)(2,1)S(1)}, u32[]{:S(2)}, u32[]{:S(2)}) collective-permute-start(bf16[144,512]{1,0:T(8,128)(2,1)} %get-tuple-element.22), channel_id=1, source_target_pairs={{0,12},{4,0},{8,4},{12,8},{1,13},{5,1},{9,5},{13,9},{2,14},{6,2},{... | collective-permute-start | bytes 442376 | tf_op jit(solution)/shard_map/ppermute | solution.py:342
  17.3 5.5 %copy-start.5 = (bf16[144,512]{1,0:T(8,128)(2,1)}, bf16[144,512]{1,0:T(8,128)(2,1)S(1)}, u32[]{:S(2)}) copy-start(bf16[144,512]{1,0:T(8,128)(2,1)S(1)} %collective-permute-done.m1) | copy-start | bytes 442372
  22.8 0.7 %copy-start.6 = (bf16[144,512]{1,0:T(8,128)(2,1)}, bf16[144,512]{1,0:T(8,128)(2,1)S(1)}, u32[]{:S(2)}) copy-start(bf16[144,512]{1,0:T(8,128)(2,1)S(1)} %collective-permute-done.1.m2) | copy-start | bytes 442372
  22.8 0.7 %copy-start.7 = (bf16[144,512]{1,0:T(8,128)(2,1)}, bf16[144,512]{1,0:T(8,128)(2,1)S(1)}, u32[]{:S(2)}) copy-start(bf16[144,512]{1,0:T(8,128)(2,1)S(1)} %collective-permute-done.2.m3) | copy-start | bytes 442372
  35.7 18.8 %collective-permute-start.3 = (bf16[64,512]{1,0:T(8,128)(2,1)}, bf16[64,512]{1,0:T(8,128)(2,1)S(1)}, u32[]{:S(2)}, u32[]{:S(2)}) collective-permute-start(bf16[64,512]{1,0:T(8,128)(2,1)} %get-tuple-element.24), channel_id=1, source_target_pairs={{0,12},{4,0},{8,4},{12,8},{1,13},{5,1},{9,5},{13,9},{2,14},{6,2},{... | collective-permute-start | bytes 196616 | tf_op jit(solution)/shard_map/ppermute | solution.py:342
  40.4 14.2 %collective-permute-start.4 = (bf16[64,512]{1,0:T(8,128)(2,1)}, bf16[64,512]{1,0:T(8,128)(2,1)S(1)}, u32[]{:S(2)}, u32[]{:S(2)}) collective-permute-start(bf16[64,512]{1,0:T(8,128)(2,1)} %get-tuple-element.25), channel_id=1, source_target_pairs={{0,8},{4,12},{8,0},{12,4},{1,9},{5,13},{9,1},{13,5},{2,10},{6,14},... | collective-permute-start | bytes 196616 | tf_op jit(solution)/shard_map/ppermute | solution.py:342
  40.7 13.8 %collective-permute-start.5 = (bf16[64,512]{1,0:T(8,128)(2,1)}, bf16[64,512]{1,0:T(8,128)(2,1)S(1)}, u32[]{:S(2)}, u32[]{:S(2)}) collective-permute-start(bf16[64,512]{1,0:T(8,128)(2,1)} %get-tuple-element.26), channel_id=1, source_target_pairs={{0,4},{4,8},{8,12},{12,0},{1,5},{5,9},{9,13},{13,1},{2,6},{6,10},{... | collective-permute-start | bytes 196616 | tf_op jit(solution)/shard_map/ppermute | solution.py:342
  54.5 0.6 %copy-start.2 = (bf16[64,512]{1,0:T(8,128)(2,1)}, bf16[64,512]{1,0:T(8,128)(2,1)S(1)}, u32[]{:S(2)}) copy-start(bf16[64,512]{1,0:T(8,128)(2,1)S(1)} %collective-permute-done.3.g1) | copy-start | bytes 196612
  54.5 0.6 %copy-start.3 = (bf16[64,512]{1,0:T(8,128)(2,1)}, bf16[64,512]{1,0:T(8,128)(2,1)S(1)}, u32[]{:S(2)}) copy-start(bf16[64,512]{1,0:T(8,128)(2,1)S(1)} %collective-permute-done.4.g2) | copy-start | bytes 196612
  54.6 0.6 %copy-start.4 = (bf16[64,512]{1,0:T(8,128)(2,1)}, bf16[64,512]{1,0:T(8,128)(2,1)S(1)}, u32[]{:S(2)}) copy-start(bf16[64,512]{1,0:T(8,128)(2,1)S(1)} %collective-permute-done.5.g3) | copy-start | bytes 196612

commit v2 on v0

--- a/solution.py
+++ b/solution.py
@@ -1,9 +1,12 @@
+import functools
 import math
 
 import jax
 import jax.numpy as jnp
 import numpy as np
 from jax import lax
+from jax.experimental import pallas as pl
+from jax.experimental.pallas import tpu as pltpu
 from jax.sharding import PartitionSpec as P
 
 HEAD_DIM = 48
@@ -120,7 +123,7 @@
     return (new_max, new_total, new_acc)
 
 
-def per_device(query_rows, key_rows, value_rows):
+def any_length(query_rows, key_rows, value_rows):
     row_count = query_rows.shape[0]
     feature_width = query_rows.shape[1]
     local_heads = feature_width // HEAD_DIM
@@ -182,6 +185,267 @@
     return (numerator / denominator).astype(jnp.bfloat16)
 
 
+STRIDES = 4
+LANES = 128
+SPAN = STRIDES * LANES
+TAIL = 8
+LOG2E = 1.4426950408889634
+FACTOR = HEAD_DIM ** (-0.5) * LOG2E
+LEAST_TOTAL = 2.0 ** -60
+MOST_TOTAL = 2.0 ** 100
+VMEM_BYTES = 60 * 1024 * 1024
+
+
+def dot_nn(left, right):
+    return lax.dot_general(left, right, (((1,), (0,)), ((), ())), preferred_element_type=jnp.float32)
+
+
+def dot_nt(left, right):
+    return lax.dot_general(left, right, (((1,), (1,)), ((), ())), preferred_element_type=jnp.float32)
+
+
+def one_hot(shape, which):
+    rows = lax.broadcasted_iota(jnp.int32, shape, 0)
+    columns = lax.broadcasted_iota(jnp.int32, shape, 1)
+    return jnp.where(which(rows, columns), 1.0, 0.0).astype(jnp.bfloat16)
+
+
+def call(kernel, outs, args, scratch, flops):
+    return pl.pallas_call(
+        kernel,
+        out_shape=outs,
+        in_specs=[pl.BlockSpec(memory_space=pltpu.VMEM)] * len(args),
+        out_specs=jax.tree.map(lambda out: pl.BlockSpec(memory_space=pltpu.VMEM), outs),
+        scratch_shapes=scratch,
+        compiler_params=pltpu.CompilerParams(vmem_limit_bytes=VMEM_BYTES),
+        cost_estimate=pl.CostEstimate(flops=flops, bytes_accessed=2 << 20, transcendentals=0),
+    )(*args)
+
+
+def pack_kernel(q_ref, k_ref, v_ref, m0, m1, m2, m3, by_head):
+    width, rows = q_ref.shape
+    heads = width // HEAD_DIM
+    for parity in range(2):
+        pick = one_hot(
+            (SPAN, 2 * LANES), lambda row, column: row == column % LANES * STRIDES + column // LANES * 2 + parity
+        )
+        mine = range(parity, heads, 2)
+        for block in range(rows // SPAN):
+            pieces = [
+                ref[pl.ds(head * HEAD_DIM, HEAD_DIM), pl.ds(block * SPAN, SPAN)]
+                for head in mine
+                for ref in (q_ref, k_ref, v_ref)
+            ]
+            picked = dot_nn(jnp.concatenate(pieces, axis=0), pick).astype(jnp.bfloat16)
+            for at, head in enumerate(mine):
+                features = picked[at * 3 * HEAD_DIM : (at + 1) * 3 * HEAD_DIM]
+                for klass in range(2):
+                    phase = (head + 2 * klass) % STRIDES // 2
+                    by_head[head, :, pl.ds(klass * rows // STRIDES + block * LANES, LANES)] = features[
+                        :, phase * LANES : (phase + 1) * LANES
+                    ]
+    me = lax.axis_index("seq")
+    for shift, message in enumerate((m0, m1, m2, m3)):
+        message[...] = by_head[lax.rem(me + shift, heads)]
+
+
+def with_ones(block):
+    count = block.shape[1]
+    extra = one_hot((2 * TAIL, count), lambda row, column: row == 0)
+    return jnp.concatenate([block, extra], axis=0)
+
+
+def upright(block):
+    count = block.shape[1]
+    size = min(count, 2 * LANES)
+    eye = one_hot((size, size), lambda row, column: row == column)
+    pieces = [dot_nt(eye, block[:, at : at + size]) for at in range(0, count, size)]
+    return jnp.concatenate(pieces, axis=0).astype(jnp.bfloat16)
+
+
+def plain(keys, queries, values):
+    return dot_nn(values, jnp.exp2(dot_nn(keys, queries) * FACTOR).astype(jnp.bfloat16))
+
+
+def shifted(keys, queries, values):
+    scores = dot_nn(keys, queries)
+    top = jnp.max(scores, axis=0, keepdims=True) * FACTOR
+    return dot_nn(values, jnp.exp2(scores * FACTOR - top).astype(jnp.bfloat16)), top
+
+
+def in_range(totals):
+    low = functools.reduce(jnp.minimum, totals)
+    high = functools.reduce(jnp.maximum, totals)
+    return jnp.logical_and(jnp.min(low) >= LEAST_TOTAL, jnp.max(high) <= MOST_TOTAL)
+
+
+def near_kernel(qt_ref, kt_ref, vt_ref, out_ref, keys_ref):
+    width, rows = qt_ref.shape
+    heads = width // HEAD_DIM
+    keys = upright(kt_ref[...])
+    for head in range(heads):
+        keys_ref[head] = keys[:, head * HEAD_DIM : (head + 1) * HEAD_DIM]
+    totals = []
+    for head in range(heads):
+        features = pl.ds(head * HEAD_DIM, HEAD_DIM)
+        values = with_ones(vt_ref[features, :])
+        for start in range(0, rows, SPAN):
+            lanes = pl.ds(start, SPAN)
+            result = plain(keys_ref[head], qt_ref[features, lanes], values)
+            out_ref[head, :, lanes] = result[: HEAD_DIM + TAIL]
+            totals.append(result[HEAD_DIM : HEAD_DIM + 1])
+
+    @pl.when(jnp.logical_not(in_range(totals)))
+    def again():
+        @pl.loop(0, heads)
+        def one_head(head):
+            features = pl.ds(pl.multiple_of(head * HEAD_DIM, 16), HEAD_DIM)
+            values = with_ones(vt_ref[features, :])
+            for start in range(0, rows, 2 * LANES):
+                lanes = pl.ds(start, 2 * LANES)
+                result, top = shifted(keys_ref[head], qt_ref[features, lanes], values)
+                out_ref[head, :, lanes] = result[: HEAD_DIM + TAIL]
+                out_ref[head, pl.ds(HEAD_DIM + 1, 1), lanes] = top
+
+
+def finished(result, top):
+    total = result[HEAD_DIM : HEAD_DIM + 1]
+    lse = jnp.log2(total) if top is None else top + jnp.log2(total)
+    high = lse.astype(jnp.bfloat16).astype(jnp.float32)
+    middle = (lse - high).astype(jnp.bfloat16).astype(jnp.float32)
+    low = lse - high - middle
+    row = lax.broadcasted_iota(jnp.int32, (TAIL, total.shape[1]), 0)
+    parts = jnp.where(row == 0, high, jnp.where(row == 1, middle, jnp.where(row == 2, low, 0.0)))
+    return jnp.concatenate([result[:HEAD_DIM] / total, parts], axis=0).astype(jnp.bfloat16)
+
+
+def far_kernel(m0, m1, m2, m3, o0, o1, o2, o3, keys_ref, queries_ref, values_ref):
+    count = m0.shape[1]
+    half = count // 2
+    sources, outs = (m0, m1, m2, m3), (o0, o1, o2, o3)
+    twice = jnp.where(lax.broadcasted_iota(jnp.int32, (1, count), 1) < half, 2.0, 1.0).astype(jnp.bfloat16)
+    for at, source in enumerate(sources):
+        keys_ref[pl.ds(at * count, count), :] = upright(source[pl.ds(HEAD_DIM, HEAD_DIM), :])
+        values = with_ones(source[pl.ds(2 * HEAD_DIM, HEAD_DIM), :])
+        values_ref[0, :, pl.ds(at * count, count)] = values * twice
+        values_ref[1, :, pl.ds(at * count, count)] = values
+        for klass in range(2):
+            queries_ref[klass, :, pl.ds(at * half, half)] = source[pl.ds(0, HEAD_DIM), pl.ds(klass * half, half)]
+    totals = []
+    for klass in range(2):
+        for pair in range(0, len(sources), 2):
+            queries = queries_ref[klass, :, pl.ds(pair * half, count)]
+            result = plain(keys_ref[...], queries, values_ref[klass])
+            done = finished(result, None)
+            totals.append(result[HEAD_DIM : HEAD_DIM + 1])
+            for at in range(2):
+                outs[pair + at][:, pl.ds(klass * half, half)] = done[:, at * half : (at + 1) * half]
+
+    @pl.when(jnp.logical_not(in_range(totals)))
+    def again():
+        @pl.loop(0, 2)
+        def one_class(klass):
+            for at, out in enumerate(outs):
+                result, top = shifted(keys_ref[...], queries_ref[klass, :, pl.ds(at * half, half)], values_ref[klass])
+                out[:, pl.ds(pl.multiple_of(klass * half, LANES), half)] = finished(result, top)
+
+
+def merge_kernel(near_ref, g0, g1, g2, g3, out_ref, by_head):
+    heads, _, rows = near_ref.shape
+    half = rows // STRIDES
+    me = lax.axis_index("seq")
+    for shift, result in enumerate((g0, g1, g2, g3)):
+        by_head[lax.rem(me + shift, heads)] = result[...]
+    position = lax.broadcasted_iota(jnp.int32, (1, SPAN), 1)
+    for parity in range(2):
+        place = one_hot(
+            (2 * LANES, SPAN), lambda row, column: column == row % LANES * STRIDES + row // LANES * 2 + parity
+        )
+        used = position % 2 == parity
+        for block in range(rows // SPAN):
+            lanes = pl.ds(block * SPAN, SPAN)
+            mine = range(parity, heads, 2)
+            pieces = []
+            for head in mine:
+                order = [(phase * 2 + parity - head) % STRIDES // 2 for phase in range(2)]
+                pieces.append(
+                    jnp.concatenate(
+                        [by_head[head, :, pl.ds(klass * half + block * LANES, LANES)] for klass in order], axis=1
+                    )
+                )
+            for head, piece in zip(mine, pieces):
+                there = dot_nn(piece, place)
+                near = near_ref[head, pl.ds(0, HEAD_DIM), lanes]
+                total = near_ref[head, pl.ds(HEAD_DIM, 1), lanes]
+                top = near_ref[head, pl.ds(HEAD_DIM + 1, 1), lanes]
+                lse = there[HEAD_DIM : HEAD_DIM + 1] + there[HEAD_DIM + 1 : HEAD_DIM + 2] + there[HEAD_DIM + 2 : HEAD_DIM + 3]
+                near_lse = top + jnp.log2(total)
+                peak = jnp.where(used, jnp.maximum(near_lse, lse), near_lse)
+                weight = jnp.exp2(top - peak)
+                far = jnp.where(used, jnp.exp2(lse - peak), 0.0)
+                share = 1.0 / (total * weight + far)
+                merged = near * (weight * share) + there[:HEAD_DIM] * (far * share)
+                out_ref[pl.ds(head * HEAD_DIM, HEAD_DIM), lanes] = merged.astype(jnp.bfloat16)
+
+
+def by_rotation(blocks, sign):
+    shards = lax.axis_size("seq")
+    moved = [blocks[0]]
+    for shift in range(1, shards):
+        moved.append(lax.ppermute(blocks[shift], "seq", [(i, (i + sign * shift) % shards) for i in range(shards)]))
+    return moved
+
+
+def whole_slide(query_rows, key_rows, value_rows):
+    rows, width = query_rows.shape
+    heads = width // HEAD_DIM
+    count = rows // 2
+    bf16, f32 = jnp.bfloat16, jnp.float32
+    turned = [block.T for block in (query_rows, key_rows, value_rows)]
+    messages = call(
+        pack_kernel,
+        [jax.ShapeDtypeStruct((3 * HEAD_DIM, count), bf16)] * heads,
+        turned,
+        [pltpu.VMEM((heads, 3 * HEAD_DIM, count), bf16)],
+        1 << 28,
+    )
+    arrived = by_rotation(messages, 1)
+    near = call(
+        near_kernel,
+        jax.ShapeDtypeStruct((heads, HEAD_DIM + TAIL, rows), f32),
+        turned,
+        [pltpu.VMEM((heads, rows, HEAD_DIM), bf16)],
+        4 * heads * rows * rows * 256,
+    )
+    far = call(
+        far_kernel,
+        [jax.ShapeDtypeStruct((HEAD_DIM + TAIL, count), bf16)] * heads,
+        arrived,
+        [
+            pltpu.VMEM((heads * count, HEAD_DIM), bf16),
+            pltpu.VMEM((2, HEAD_DIM, heads * count // 2), bf16),
+            pltpu.VMEM((2, HEAD_DIM + 2 * TAIL, heads * count), bf16),
+        ],
+        4 * heads * rows * rows * 256,
+    )
+    back = by_rotation(far, -1)
+    return call(
+        merge_kernel,
+        jax.ShapeDtypeStruct((width, rows), bf16),
+        [near, *back],
+        [pltpu.VMEM((heads, HEAD_DIM + TAIL, count), bf16)],
+        1 << 28,
+    ).T
+
+
+def per_device(query_rows, key_rows, value_rows):
+    rows, width = query_rows.shape
+    shards = lax.axis_size("seq")
+    if rows == SEG_A and rows * shards == SEG_B and width == shards * HEAD_DIM and shards == STRIDES:
+        return whole_slide(query_rows, key_rows, value_rows)
+    return any_length(query_rows, key_rows, value_rows)
+
+
 def solution(mesh):
     return jax.shard_map(
         per_device,

time: 165 us -> 61.6 us (0.37)
  local copies, waits for them, and re-layouts: 64.5 us -> 1.36 us
  Pallas kernels: 0 us -> 39.2 us
  blocking collectives: 34.2 us -> 0 us
  matrix products: 18.9 us -> 0 us
  other arithmetic: 18.8 us -> 0 us
  waiting for transfers between devices: 23.1 us -> 8.56 us
  starting transfers between devices: 3.83 us -> 12.2 us
    pallas_call x0 -> x4, Pallas kernels: none -> 39.2 us  [call(): pl.pallas_call(kernel, out_shape=outs, in_specs=[pl.BlockSpec(memory_spac...]
    dynamic_update_slice x12 -> x0, local copies, waits for them, and re-layouts: 37.4 us -> none  [attend_rows(): lax.map(one_piece, query_flat.reshape(count // rows, rows, feature_width))]
    all_gather x2 -> x0, blocking collectives: 34.2 us -> none  [the longest x1 19.4 us: per_device(): lax.all_gather(wide_values, 'seq', axis=0, tiled=True)]
    dot_general x18 -> x0, matrix products: 18.9 us -> none  [the longest x8 7.47 us: attend(): jnp.einsum('qak,kad->qad', exp_scores.astype(jnp.bfloat16), value_block,...]
    ppermute x2 -> x6, waiting for transfers between devices: 23.1 us -> 8.56 us  [by_rotation(): lax.ppermute(blocks[shift], 'seq', [(i, (i + sign * shift) % shards) for...]
    ppermute x2 -> x6, starting transfers between devices: 3.83 us -> 12.2 us  [by_rotation(): lax.ppermute(blocks[shift], 'seq', [(i, (i + sign * shift) % shards) for...]
    reshape x14 -> x0, local copies, waits for them, and re-layouts: 8.13 us -> none  [the longest x6 4.75 us: pick_rows(): grid = block.reshape(row_count // stride, stride * feature_width)]
    reduce_sum x9 -> x0, other arithmetic: 7.93 us -> none  [the longest x8 7.01 us: attend(): row_total = jnp.sum(exp_scores, axis=-1)]
  transfers between devices with their start and end apart: 2 -> 6, of which waited for: 1 -> 2; matrix products, arithmetic and copies ran while one was open for 36% -> 0% of each run, Pallas kernels for 0% -> 29%
where the time goes in v2:
time: 61.6 us; the launch traced here: 61.4 us
  Pallas kernels  39.2 us (64%)
  starting transfers between devices  12.2 us (20%)
  waiting for transfers between devices  8.56 us (14%)
  local copies, waits for them, and re-layouts  1.36 us (2%)
    pallas_call x4, Pallas kernels, call(): pl.pallas_call(kernel, out_shape=outs, in_specs=[pl.BlockSpec(memory_spac...  39.2 us
    ppermute x6, starting transfers between devices, by_rotation(): lax.ppermute(blocks[shift], 'seq', [(i, (i + sign * shift) % shards) for...  12.2 us
    ppermute x6, waiting for transfers between devices, by_rotation(): lax.ppermute(blocks[shift], 'seq', [(i, (i + sign * shift) % shards) for...  8.56 us
    unnamed x12, local copies, waits for them, and re-layouts  1.36 us
  transfers between devices with their start and end apart: 6, of which 2 were waited for; matrix products, arithmetic and copies ran while one was open for 0% of the time, Pallas kernels for 29%

profile of v2, /device:TPU:0, one launch (start us, length us, event | category | flops | bytes accessed | tf_op | source)
XLA Modules:
  0.0 61.4 jit_solution(5338370148906649822)
XLA Ops:
  0.0 2.6 %shard_map.38 = (bf16[144,512]{1,0:T(8,128)(2,1)}, bf16[144,512]{1,0:T(8,128)(2,1)}, bf16[144,512]{1,0:T(8,128)(2,1)}, bf16[144,512]{1,0:T(8,128)(2,1)}) custom-call(bf16[192,1024]{1,0:T(8,128)(2,1)} %bitcast.4, bf16[192,1024]{1,0:T(8,128)(2,1)} %bitcast.6, bf16[192,1024]{1,0:T(8,128)(2,1)} %bitcast.8), custom_call_target="tpu_custom_call" | custom-call | flops 268435456 | bytes 2097152 | tf_op jit(solution)/shard_map/pallas_call | solution.py:214
  2.6 3.0 %collective-permute-start = (bf16[144,512]{1,0:T(8,128)(2,1)}, bf16[144,512]{1,0:T(8,128)(2,1)S(1)}, u32[]{:S(2)}, u32[]{:S(2)}) collective-permute-start(bf16[144,512]{1,0:T(8,128)(2,1)} %get-tuple-element.14), channel_id=1, source_target_pairs={{0,4},{4,8},{8,12},{12,0},{1,5},{5,9},{9,13},{13,1},{2,6},{6,10},{... | collective-permute-start | bytes 442376 | tf_op jit(solution)/shard_map/ppermute | solution.py:395
  5.6 2.6 %collective-permute-start.1 = (bf16[144,512]{1,0:T(8,128)(2,1)}, bf16[144,512]{1,0:T(8,128)(2,1)S(1)}, u32[]{:S(2)}, u32[]{:S(2)}) collective-permute-start(bf16[144,512]{1,0:T(8,128)(2,1)} %get-tuple-element.15), channel_id=1, source_target_pairs={{0,8},{4,12},{8,0},{12,4},{1,9},{5,13},{9,1},{13,5},{2,10},{6,14},... | collective-permute-start | bytes 442376 | tf_op jit(solution)/shard_map/ppermute | solution.py:395
  8.2 1.3 %collective-permute-start.2 = (bf16[144,512]{1,0:T(8,128)(2,1)}, bf16[144,512]{1,0:T(8,128)(2,1)S(1)}, u32[]{:S(2)}, u32[]{:S(2)}) collective-permute-start(bf16[144,512]{1,0:T(8,128)(2,1)} %get-tuple-element.16), channel_id=1, source_target_pairs={{0,12},{4,0},{8,4},{12,8},{1,13},{5,1},{9,5},{13,9},{2,14},{6,2},{... | collective-permute-start | bytes 442376 | tf_op jit(solution)/shard_map/ppermute | solution.py:395
  9.6 3.1 %collective-permute-done.m1 = bf16[144,512]{1,0:T(8,128)(2,1)S(1)} collective-permute-done((bf16[144,512]{1,0:T(8,128)(2,1)}, bf16[144,512]{1,0:T(8,128)(2,1)S(1)}, u32[]{:S(2)}, u32[]{:S(2)}) %collective-permute-start) | collective-permute-done | bytes 147488 | tf_op jit(solution)/shard_map/ppermute | solution.py:395
  12.6 0.0 copy-start.3
  12.6 5.5 %collective-permute-done.1.m2 = bf16[144,512]{1,0:T(8,128)(2,1)S(1)} collective-permute-done((bf16[144,512]{1,0:T(8,128)(2,1)}, bf16[144,512]{1,0:T(8,128)(2,1)S(1)}, u32[]{:S(2)}, u32[]{:S(2)}) %collective-permute-start.1) | collective-permute-done | bytes 147488 | tf_op jit(solution)/shard_map/ppermute | solution.py:395
  18.1 0.0 copy-start.4
  18.1 0.0 collective-permute-done.2.m3
  18.1 0.0 copy-start.5
  18.1 0.0 copy-done.3
  18.1 0.6 %copy-done.4 = bf16[144,512]{1,0:T(8,128)(2,1)} copy-done((bf16[144,512]{1,0:T(8,128)(2,1)}, bf16[144,512]{1,0:T(8,128)(2,1)S(1)}, u32[]{:S(2)}) %copy-start.4) | copy-done | bytes 147480
  18.8 0.1 copy-done.5
  18.8 16.2 %shard_map.39 = (bf16[56,512]{1,0:T(8,128)(2,1)}, bf16[56,512]{1,0:T(8,128)(2,1)}, bf16[56,512]{1,0:T(8,128)(2,1)}, bf16[56,512]{1,0:T(8,128)(2,1)}) custom-call(bf16[144,512]{1,0:T(8,128)(2,1)} %get-tuple-element.13.m0, bf16[144,512]{1,0:T(8,128)(2,1)} %copy-done.3, bf16[144,512]{1,0:T(8,128)(2,1)} %copy-done.4, bf16[144,512]{1,0:T(8,128)(2,1)} %copy-done.5), custom_call_target="tpu_custom_call" | custom-call | flops 4294967296 | bytes 2097152 | tf_op jit(solution)/shard_map/pallas_call | solution.py:214
  35.0 4.7 %collective-permute-start.3 = (bf16[56,512]{1,0:T(8,128)(2,1)}, bf16[56,512]{1,0:T(8,128)(2,1)S(1)}, u32[]{:S(2)}, u32[]{:S(2)}) collective-permute-start(bf16[56,512]{1,0:T(8,128)(2,1)} %get-tuple-element.18), channel_id=1, source_target_pairs={{0,12},{4,0},{8,4},{12,8},{1,13},{5,1},{9,5},{13,9},{2,14},{6,2},{... | collective-permute-start | bytes 172040 | tf_op jit(solution)/shard_map/ppermute | solution.py:395
  39.7 0.3 collective-permute-start.4
  40.0 0.2 collective-permute-start.5
  40.3 17.8 %shard_map.37.near_ref = f32[4,56,1024]{2,1,0:T(8,128)} custom-call(bf16[192,1024]{1,0:T(8,128)(2,1)} %bitcast.5, bf16[192,1024]{1,0:T(8,128)(2,1)} %bitcast.7, bf16[192,1024]{1,0:T(8,128)(2,1)} %bitcast.9), custom_call_target="tpu_custom_call" | custom-call | flops 4294967296 | bytes 2097152 | tf_op jit(solution)/shard_map/pallas_call | solution.py:214
  58.1 0.0 collective-permute-done.3.g1
  58.1 0.0 copy-start
  58.1 0.0 collective-permute-done.4.g2
  58.1 0.0 copy-start.1
  58.1 0.0 collective-permute-done.5.g3
  58.1 0.0 copy-start.2
  58.1 0.6 copy-done
  58.7 0.0 copy-done.1
  58.7 0.0 copy-done.2
  58.8 2.6 %shard_map.40 = bf16[192,1024]{1,0:T(8,128)(2,1)} custom-call(f32[4,56,1024]{2,1,0:T(8,128)} %shard_map.37.near_ref, bf16[56,512]{1,0:T(8,128)(2,1)} %get-tuple-element.17.g0, bf16[56,512]{1,0:T(8,128)(2,1)} %copy-done, bf16[56,512]{1,0:T(8,128)(2,1)} %copy-done.1, bf16[56,512]{1,0:T(8,128)(2,1)} %copy-done.2), custom_call_target="tpu_custom_call" | custom-call | flops 268435456 | bytes 2097152 | tf_op jit(solution)/shard_map/pallas_call | solution.py:214
Async XLA Ops:
  2.6 10.0 %collective-permute-start = (bf16[144,512]{1,0:T(8,128)(2,1)}, bf16[144,512]{1,0:T(8,128)(2,1)S(1)}, u32[]{:S(2)}, u32[]{:S(2)}) collective-permute-start(bf16[144,512]{1,0:T(8,128)(2,1)} %get-tuple-element.14), channel_id=1, source_target_pairs={{0,4},{4,8},{8,12},{12,0},{1,5},{5,9},{9,13},{13,1},{2,6},{6,10},{... | collective-permute-start | bytes 442376 | tf_op jit(solution)/shard_map/ppermute | solution.py:395
  5.6 12.5 %collective-permute-start.1 = (bf16[144,512]{1,0:T(8,128)(2,1)}, bf16[144,512]{1,0:T(8,128)(2,1)S(1)}, u32[]{:S(2)}, u32[]{:S(2)}) collective-permute-start(bf16[144,512]{1,0:T(8,128)(2,1)} %get-tuple-element.15), channel_id=1, source_target_pairs={{0,8},{4,12},{8,0},{12,4},{1,9},{5,13},{9,1},{13,5},{2,10},{6,14},... | collective-permute-start | bytes 442376 | tf_op jit(solution)/shard_map/ppermute | solution.py:395
  8.2 9.9 %collective-permute-start.2 = (bf16[144,512]{1,0:T(8,128)(2,1)}, bf16[144,512]{1,0:T(8,128)(2,1)S(1)}, u32[]{:S(2)}, u32[]{:S(2)}) collective-permute-start(bf16[144,512]{1,0:T(8,128)(2,1)} %get-tuple-element.16), channel_id=1, source_target_pairs={{0,12},{4,0},{8,4},{12,8},{1,13},{5,1},{9,5},{13,9},{2,14},{6,2},{... | collective-permute-start | bytes 442376 | tf_op jit(solution)/shard_map/ppermute | solution.py:395
  12.6 5.5 %copy-start.3 = (bf16[144,512]{1,0:T(8,128)(2,1)}, bf16[144,512]{1,0:T(8,128)(2,1)S(1)}, u32[]{:S(2)}) copy-start(bf16[144,512]{1,0:T(8,128)(2,1)S(1)} %collective-permute-done.m1) | copy-start | bytes 442372
  18.1 0.7 %copy-start.4 = (bf16[144,512]{1,0:T(8,128)(2,1)}, bf16[144,512]{1,0:T(8,128)(2,1)S(1)}, u32[]{:S(2)}) copy-start(bf16[144,512]{1,0:T(8,128)(2,1)S(1)} %collective-permute-done.1.m2) | copy-start | bytes 442372
  18.1 0.7 %copy-start.5 = (bf16[144,512]{1,0:T(8,128)(2,1)}, bf16[144,512]{1,0:T(8,128)(2,1)S(1)}, u32[]{:S(2)}) copy-start(bf16[144,512]{1,0:T(8,128)(2,1)S(1)} %collective-permute-done.2.m3) | copy-start | bytes 442372
  35.0 23.1 %collective-permute-start.3 = (bf16[56,512]{1,0:T(8,128)(2,1)}, bf16[56,512]{1,0:T(8,128)(2,1)S(1)}, u32[]{:S(2)}, u32[]{:S(2)}) collective-permute-start(bf16[56,512]{1,0:T(8,128)(2,1)} %get-tuple-element.18), channel_id=1, source_target_pairs={{0,12},{4,0},{8,4},{12,8},{1,13},{5,1},{9,5},{13,9},{2,14},{6,2},{... | collective-permute-start | bytes 172040 | tf_op jit(solution)/shard_map/ppermute | solution.py:395
  39.7 18.4 %collective-permute-start.4 = (bf16[56,512]{1,0:T(8,128)(2,1)}, bf16[56,512]{1,0:T(8,128)(2,1)S(1)}, u32[]{:S(2)}, u32[]{:S(2)}) collective-permute-start(bf16[56,512]{1,0:T(8,128)(2,1)} %get-tuple-element.19), channel_id=1, source_target_pairs={{0,8},{4,12},{8,0},{12,4},{1,9},{5,13},{9,1},{13,5},{2,10},{6,14},... | collective-permute-start | bytes 172040 | tf_op jit(solution)/shard_map/ppermute | solution.py:395
  40.0 18.1 %collective-permute-start.5 = (bf16[56,512]{1,0:T(8,128)(2,1)}, bf16[56,512]{1,0:T(8,128)(2,1)S(1)}, u32[]{:S(2)}, u32[]{:S(2)}) collective-permute-start(bf16[56,512]{1,0:T(8,128)(2,1)} %get-tuple-element.20), channel_id=1, source_target_pairs={{0,4},{4,8},{8,12},{12,0},{1,5},{5,9},{9,13},{13,1},{2,6},{6,10},{... | collective-permute-start | bytes 172040 | tf_op jit(solution)/shard_map/ppermute | solution.py:395
  58.1 0.6 %copy-start = (bf16[56,512]{1,0:T(8,128)(2,1)}, bf16[56,512]{1,0:T(8,128)(2,1)S(1)}, u32[]{:S(2)}) copy-start(bf16[56,512]{1,0:T(8,128)(2,1)S(1)} %collective-permute-done.3.g1) | copy-start | bytes 172036
  58.1 0.6 %copy-start.1 = (bf16[56,512]{1,0:T(8,128)(2,1)}, bf16[56,512]{1,0:T(8,128)(2,1)S(1)}, u32[]{:S(2)}) copy-start(bf16[56,512]{1,0:T(8,128)(2,1)S(1)} %collective-permute-done.4.g2) | copy-start | bytes 172036
  58.1 0.7 %copy-start.2 = (bf16[56,512]{1,0:T(8,128)(2,1)}, bf16[56,512]{1,0:T(8,128)(2,1)S(1)}, u32[]{:S(2)}) copy-start(bf16[56,512]{1,0:T(8,128)(2,1)S(1)} %collective-permute-done.5.g3) | copy-start | bytes 172036

commit v3 on v2

--- a/solution.py
+++ b/solution.py
@@ -188,12 +188,13 @@
 STRIDES = 4
 LANES = 128
 SPAN = STRIDES * LANES
+NEAR_KEYS = 256
 TAIL = 8
 LOG2E = 1.4426950408889634
 FACTOR = HEAD_DIM ** (-0.5) * LOG2E
 LEAST_TOTAL = 2.0 ** -60
 MOST_TOTAL = 2.0 ** 100
-VMEM_BYTES = 60 * 1024 * 1024
+VMEM_BYTES = 16 * 1024 * 1024
 
 
 def dot_nn(left, right):
@@ -285,27 +286,39 @@
     keys = upright(kt_ref[...])
     for head in range(heads):
         keys_ref[head] = keys[:, head * HEAD_DIM : (head + 1) * HEAD_DIM]
-    totals = []
-    for head in range(heads):
-        features = pl.ds(head * HEAD_DIM, HEAD_DIM)
-        values = with_ones(vt_ref[features, :])
-        for start in range(0, rows, SPAN):
-            lanes = pl.ds(start, SPAN)
-            result = plain(keys_ref[head], qt_ref[features, lanes], values)
-            out_ref[head, :, lanes] = result[: HEAD_DIM + TAIL]
-            totals.append(result[HEAD_DIM : HEAD_DIM + 1])
-
-    @pl.when(jnp.logical_not(in_range(totals)))
-    def again():
-        @pl.loop(0, heads)
-        def one_head(head):
-            features = pl.ds(pl.multiple_of(head * HEAD_DIM, 16), HEAD_DIM)
-            values = with_ones(vt_ref[features, :])
-            for start in range(0, rows, 2 * LANES):
-                lanes = pl.ds(start, 2 * LANES)
-                result, top = shifted(keys_ref[head], qt_ref[features, lanes], values)
-                out_ref[head, :, lanes] = result[: HEAD_DIM + TAIL]
-                out_ref[head, pl.ds(HEAD_DIM + 1, 1), lanes] = top
+    blocks = [(head, start) for head in range(heads) for start in range(0, rows, SPAN)]
+    pieces = range(0, rows, NEAR_KEYS)
+
+    def scores_of(block, piece):
+        head, start = block
+        queries = qt_ref[pl.ds(head * HEAD_DIM, HEAD_DIM), pl.ds(start, SPAN)]
+        return dot_nn(keys_ref[head, pl.ds(piece, NEAR_KEYS), :], queries)
+
+    def folded(values, join, held):
+        parts = [values[at : at + 8] for at in range(0, NEAR_KEYS, 8)]
+        return functools.reduce(join, parts if held is None else [held, *parts])
+
+    now, peaks = [], None
+    for piece in pieces:
+        now.append(scores_of(blocks[0], piece))
+        peaks = folded(now[-1], jnp.maximum, peaks)
+    for at, (head, start) in enumerate(blocks):
+        top = jnp.max(peaks, axis=0, keepdims=True) * FACTOR
+        later, peaks, result, totals = [], None, None, None
+        for piece, scores in zip(pieces, now):
+            if at + 1 < len(blocks):
+                later.append(scores_of(blocks[at + 1], piece))
+                peaks = folded(later[-1], jnp.maximum, peaks)
+            probs = jnp.exp2(scores * FACTOR - top)
+            totals = folded(probs, jnp.add, totals)
+            values = vt_ref[pl.ds(head * HEAD_DIM, HEAD_DIM), pl.ds(piece, NEAR_KEYS)]
+            term = dot_nn(values, probs.astype(jnp.bfloat16))
+            result = term if result is None else result + term
+        lanes = pl.ds(start, SPAN)
+        out_ref[head, pl.ds(0, HEAD_DIM), lanes] = result
+        out_ref[head, pl.ds(HEAD_DIM, 1), lanes] = jnp.sum(totals, axis=0, keepdims=True)
+        out_ref[head, pl.ds(HEAD_DIM + 1, 1), lanes] = top
+        now = later
 
 
 def finished(result, top):
@@ -417,6 +430,7 @@
         [pltpu.VMEM((heads, rows, HEAD_DIM), bf16)],
         4 * heads * rows * rows * 256,
     )
+    near, *arrived = lax.optimization_barrier((near, *arrived))
     far = call(
         far_kernel,
         [jax.ShapeDtypeStruct((HEAD_DIM + TAIL, count), bf16)] * heads,

time: 61.6 us -> 46.1 us (0.75)
  Pallas kernels: 39.2 us -> 22.7 us
  local copies, waits for them, and re-layouts: 1.36 us -> 2.99 us
  waiting for transfers between devices: 8.56 us -> 7.79 us
    pallas_call x4, Pallas kernels: 39.2 us -> 22.7 us  [call(): pl.pallas_call(kernel, out_shape=outs, in_specs=[pl.BlockSpec(memory_spac...]
    unnamed x12 -> x6, local copies, waits for them, and re-layouts: 1.36 us -> 2.99 us
    ppermute x6, waiting for transfers between devices: 8.56 us -> 7.79 us  [by_rotation(): lax.ppermute(blocks[shift], 'seq', [(i, (i + sign * shift) % shards) for...]
  transfers between devices with their start and end apart: 6 -> 6, of which waited for: 2 -> 4; matrix products, arithmetic and copies ran while one was open for 0% -> 0% of each run, Pallas kernels for 29% -> 14%
where the time goes in v3:
time: 46.1 us; the launch traced here: 45.9 us
  Pallas kernels  22.7 us (49%)
  starting transfers between devices  12.4 us (27%)
  waiting for transfers between devices  7.79 us (17%)
  local copies, waits for them, and re-layouts  2.99 us (6%)
    pallas_call x4, Pallas kernels, call(): pl.pallas_call(kernel, out_shape=outs, in_specs=[pl.BlockSpec(memory_spac...  22.7 us
    ppermute x6, starting transfers between devices, by_rotation(): lax.ppermute(blocks[shift], 'seq', [(i, (i + sign * shift) % shards) for...  12.4 us
    ppermute x6, waiting for transfers between devices, by_rotation(): lax.ppermute(blocks[shift], 'seq', [(i, (i + sign * shift) % shards) for...  7.79 us
    unnamed x6, local copies, waits for them, and re-layouts  2.99 us
  transfers between devices with their start and end apart: 6, of which 4 were waited for; matrix products, arithmetic and copies ran while one was open for 0% of the time, Pallas kernels for 14%

profile of v3, /device:TPU:0, one launch (start us, length us, event | category | flops | bytes accessed | tf_op | source)
XLA Modules:
  0.0 45.9 jit_solution(14898145464883363749)
XLA Ops:
  0.0 0.0 copy-start
  0.0 1.0 %copy-done = bf16[1024,192]{0,1:T(8,128)(2,1)S(1)} copy-done((bf16[1024,192]{0,1:T(8,128)(2,1)S(1)}, bf16[1024,192]{0,1:T(8,128)(2,1)}, u32[]{:S(2)}) %copy-start) | copy-done | bytes 393240
  1.0 0.0 copy-start.1
  1.0 1.0 %copy-done.1 = bf16[1024,192]{0,1:T(8,128)(2,1)S(1)} copy-done((bf16[1024,192]{0,1:T(8,128)(2,1)S(1)}, bf16[1024,192]{0,1:T(8,128)(2,1)}, u32[]{:S(2)}) %copy-start.1) | copy-done | bytes 393240
  2.0 0.0 copy-start.2
  2.0 1.0 %copy-done.2 = bf16[1024,192]{0,1:T(8,128)(2,1)S(1)} copy-done((bf16[1024,192]{0,1:T(8,128)(2,1)S(1)}, bf16[1024,192]{0,1:T(8,128)(2,1)}, u32[]{:S(2)}) %copy-start.2) | copy-done | bytes 393240
  3.0 0.5 %shard_map.38 = (bf16[144,512]{1,0:T(8,128)(2,1)S(1)}, bf16[144,512]{1,0:T(8,128)(2,1)S(1)}, bf16[144,512]{1,0:T(8,128)(2,1)S(1)}, bf16[144,512]{1,0:T(8,128)(2,1)S(1)}) custom-call(bf16[192,1024]{1,0:T(8,128)(2,1)S(1)} %bitcast.4, bf16[192,1024]{1,0:T(8,128)(2,1)S(1)} %bitcast.6, bf16[192,1024]{1,0:T(8,128)(2,1)S(1)} %bitcast.8), custom_call_target="tpu_custom_call" | custom-call | flops 268435456 | bytes 2097152 | tf_op jit(solution)/shard_map/pallas_call | solution.py:215
  3.5 3.1 %collective-permute-start = (bf16[144,512]{1,0:T(8,128)(2,1)S(1)}, bf16[144,512]{1,0:T(8,128)(2,1)S(1)}, u32[]{:S(2)}, u32[]{:S(2)}) collective-permute-start(bf16[144,512]{1,0:T(8,128)(2,1)S(1)} %get-tuple-element.19), channel_id=1, source_target_pairs={{0,4},{4,8},{8,12},{12,0},{1,5},{5,9},{9,13},{13,1},{2,6},{6,10},{... | collective-permute-start | bytes 442376 | tf_op jit(solution)/shard_map/ppermute | solution.py:408
  6.6 2.6 %collective-permute-start.1 = (bf16[144,512]{1,0:T(8,128)(2,1)S(1)}, bf16[144,512]{1,0:T(8,128)(2,1)S(1)}, u32[]{:S(2)}, u32[]{:S(2)}) collective-permute-start(bf16[144,512]{1,0:T(8,128)(2,1)S(1)} %get-tuple-element.20), channel_id=1, source_target_pairs={{0,8},{4,12},{8,0},{12,4},{1,9},{5,13},{9,1},{13,5},{2,10},{6,14},... | collective-permute-start | bytes 442376 | tf_op jit(solution)/shard_map/ppermute | solution.py:408
  9.2 1.3 %collective-permute-start.2 = (bf16[144,512]{1,0:T(8,128)(2,1)S(1)}, bf16[144,512]{1,0:T(8,128)(2,1)S(1)}, u32[]{:S(2)}, u32[]{:S(2)}) collective-permute-start(bf16[144,512]{1,0:T(8,128)(2,1)S(1)} %get-tuple-element.21), channel_id=1, source_target_pairs={{0,12},{4,0},{8,4},{12,8},{1,13},{5,1},{9,5},{13,9},{2,14},{6,2},{... | collective-permute-start | bytes 442376 | tf_op jit(solution)/shard_map/ppermute | solution.py:408
  10.6 6.3 %shard_map.37.near_ref = f32[4,56,1024]{2,1,0:T(8,128)S(1)} custom-call(bf16[192,1024]{1,0:T(8,128)(2,1)S(1)} %bitcast.5, bf16[192,1024]{1,0:T(8,128)(2,1)S(1)} %bitcast.7, bf16[192,1024]{1,0:T(8,128)(2,1)S(1)} %bitcast.9), custom_call_target="tpu_custom_call" | custom-call | flops 4294967296 | bytes 2097152 | tf_op jit(solution)/shard_map/pallas_call | solution.py:215
  16.8 0.0 collective-permute-done.m1
  16.8 2.1 %collective-permute-done.1.m2 = bf16[144,512]{1,0:T(8,128)(2,1)S(1)} collective-permute-done((bf16[144,512]{1,0:T(8,128)(2,1)S(1)}, bf16[144,512]{1,0:T(8,128)(2,1)S(1)}, u32[]{:S(2)}, u32[]{:S(2)}) %collective-permute-start.1) | collective-permute-done | bytes 147488 | tf_op jit(solution)/shard_map/ppermute | solution.py:408
  18.9 0.0 collective-permute-done.2.m3
  18.9 14.5 %shard_map.39 = (bf16[56,512]{1,0:T(8,128)(2,1)S(1)}, bf16[56,512]{1,0:T(8,128)(2,1)S(1)}, bf16[56,512]{1,0:T(8,128)(2,1)S(1)}, bf16[56,512]{1,0:T(8,128)(2,1)S(1)}) custom-call(bf16[144,512]{1,0:T(8,128)(2,1)S(1)} %get-tuple-element.23.m0, bf16[144,512]{1,0:T(8,128)(2,1)S(1)} %collective-permute-done.m1, bf16[144,512]{1,0:T(8,128)(2,1)S(1)} %collective-permute-done.1.m2, ...), custom_call_target="tpu_custom_call" | custom-call | flops 4294967296 | bytes 2097152 | tf_op jit(solution)/shard_map/pallas_call | solution.py:215
  33.4 4.7 %collective-permute-start.3 = (bf16[56,512]{1,0:T(8,128)(2,1)S(1)}, bf16[56,512]{1,0:T(8,128)(2,1)S(1)}, u32[]{:S(2)}, u32[]{:S(2)}) collective-permute-start(bf16[56,512]{1,0:T(8,128)(2,1)S(1)} %get-tuple-element.28), channel_id=1, source_target_pairs={{0,12},{4,0},{8,4},{12,8},{1,13},{5,1},{9,5},{13,9},{2,14},{6,2},{... | collective-permute-start | bytes 172040 | tf_op jit(solution)/shard_map/ppermute | solution.py:408
  38.2 0.4 collective-permute-start.4
  38.6 0.2 collective-permute-start.5
  38.8 1.4 %collective-permute-done.3.g1 = bf16[56,512]{1,0:T(8,128)(2,1)S(1)} collective-permute-done((bf16[56,512]{1,0:T(8,128)(2,1)S(1)}, bf16[56,512]{1,0:T(8,128)(2,1)S(1)}, u32[]{:S(2)}, u32[]{:S(2)}) %collective-permute-start.3) | collective-permute-done | bytes 57376 | tf_op jit(solution)/shard_map/ppermute | solution.py:408
  40.3 3.5 %collective-permute-done.4.g2 = bf16[56,512]{1,0:T(8,128)(2,1)S(1)} collective-permute-done((bf16[56,512]{1,0:T(8,128)(2,1)S(1)}, bf16[56,512]{1,0:T(8,128)(2,1)S(1)}, u32[]{:S(2)}, u32[]{:S(2)}) %collective-permute-start.4) | collective-permute-done | bytes 57376 | tf_op jit(solution)/shard_map/ppermute | solution.py:408
  43.8 0.8 %collective-permute-done.5.g3 = bf16[56,512]{1,0:T(8,128)(2,1)S(1)} collective-permute-done((bf16[56,512]{1,0:T(8,128)(2,1)S(1)}, bf16[56,512]{1,0:T(8,128)(2,1)S(1)}, u32[]{:S(2)}, u32[]{:S(2)}) %collective-permute-start.5) | collective-permute-done | bytes 57376 | tf_op jit(solution)/shard_map/ppermute | solution.py:408
  44.5 1.4 %shard_map.40 = bf16[192,1024]{1,0:T(8,128)(2,1)} custom-call(f32[4,56,1024]{2,1,0:T(8,128)S(1)} %shard_map.37.near_ref, bf16[56,512]{1,0:T(8,128)(2,1)S(1)} %get-tuple-element.27.g0, bf16[56,512]{1,0:T(8,128)(2,1)S(1)} %collective-permute-done.3.g1, bf16[56,512]{1,0:T(8,128)(2,1)S(1)} %collective-permute-done.4.g2, ...), custom_call_target="tpu_custom_call" | custom-call | flops 268435456 | bytes 2097152 | tf_op jit(solution)/shard_map/pallas_call | solution.py:215
Async XLA Ops:
  0.0 1.0 %copy-start = (bf16[1024,192]{0,1:T(8,128)(2,1)S(1)}, bf16[1024,192]{0,1:T(8,128)(2,1)}, u32[]{:S(2)}) copy-start(bf16[1024,192]{0,1:T(8,128)(2,1)} %param.3) | copy-start | bytes 1179652
  1.0 1.0 %copy-start.1 = (bf16[1024,192]{0,1:T(8,128)(2,1)S(1)}, bf16[1024,192]{0,1:T(8,128)(2,1)}, u32[]{:S(2)}) copy-start(bf16[1024,192]{0,1:T(8,128)(2,1)} %param.4) | copy-start | bytes 1179652
  2.0 1.0 %copy-start.2 = (bf16[1024,192]{0,1:T(8,128)(2,1)S(1)}, bf16[1024,192]{0,1:T(8,128)(2,1)}, u32[]{:S(2)}) copy-start(bf16[1024,192]{0,1:T(8,128)(2,1)} %param.5) | copy-start | bytes 1179652
  3.5 13.3 %collective-permute-start = (bf16[144,512]{1,0:T(8,128)(2,1)S(1)}, bf16[144,512]{1,0:T(8,128)(2,1)S(1)}, u32[]{:S(2)}, u32[]{:S(2)}) collective-permute-start(bf16[144,512]{1,0:T(8,128)(2,1)S(1)} %get-tuple-element.19), channel_id=1, source_target_pairs={{0,4},{4,8},{8,12},{12,0},{1,5},{5,9},{9,13},{13,1},{2,6},{6,10},{... | collective-permute-start | bytes 442376 | tf_op jit(solution)/shard_map/ppermute | solution.py:408
  6.6 12.3 %collective-permute-start.1 = (bf16[144,512]{1,0:T(8,128)(2,1)S(1)}, bf16[144,512]{1,0:T(8,128)(2,1)S(1)}, u32[]{:S(2)}, u32[]{:S(2)}) collective-permute-start(bf16[144,512]{1,0:T(8,128)(2,1)S(1)} %get-tuple-element.20), channel_id=1, source_target_pairs={{0,8},{4,12},{8,0},{12,4},{1,9},{5,13},{9,1},{13,5},{2,10},{6,14},... | collective-permute-start | bytes 442376 | tf_op jit(solution)/shard_map/ppermute | solution.py:408
  9.2 9.7 %collective-permute-start.2 = (bf16[144,512]{1,0:T(8,128)(2,1)S(1)}, bf16[144,512]{1,0:T(8,128)(2,1)S(1)}, u32[]{:S(2)}, u32[]{:S(2)}) collective-permute-start(bf16[144,512]{1,0:T(8,128)(2,1)S(1)} %get-tuple-element.21), channel_id=1, source_target_pairs={{0,12},{4,0},{8,4},{12,8},{1,13},{5,1},{9,5},{13,9},{2,14},{6,2},{... | collective-permute-start | bytes 442376 | tf_op jit(solution)/shard_map/ppermute | solution.py:408
  33.4 6.8 %collective-permute-start.3 = (bf16[56,512]{1,0:T(8,128)(2,1)S(1)}, bf16[56,512]{1,0:T(8,128)(2,1)S(1)}, u32[]{:S(2)}, u32[]{:S(2)}) collective-permute-start(bf16[56,512]{1,0:T(8,128)(2,1)S(1)} %get-tuple-element.28), channel_id=1, source_target_pairs={{0,12},{4,0},{8,4},{12,8},{1,13},{5,1},{9,5},{13,9},{2,14},{6,2},{... | collective-permute-start | bytes 172040 | tf_op jit(solution)/shard_map/ppermute | solution.py:408
  38.2 5.6 %collective-permute-start.4 = (bf16[56,512]{1,0:T(8,128)(2,1)S(1)}, bf16[56,512]{1,0:T(8,128)(2,1)S(1)}, u32[]{:S(2)}, u32[]{:S(2)}) collective-permute-start(bf16[56,512]{1,0:T(8,128)(2,1)S(1)} %get-tuple-element.29), channel_id=1, source_target_pairs={{0,8},{4,12},{8,0},{12,4},{1,9},{5,13},{9,1},{13,5},{2,10},{6,14},... | collective-permute-start | bytes 172040 | tf_op jit(solution)/shard_map/ppermute | solution.py:408
  38.6 6.0 %collective-permute-start.5 = (bf16[56,512]{1,0:T(8,128)(2,1)S(1)}, bf16[56,512]{1,0:T(8,128)(2,1)S(1)}, u32[]{:S(2)}, u32[]{:S(2)}) collective-permute-start(bf16[56,512]{1,0:T(8,128)(2,1)S(1)} %get-tuple-element.30), channel_id=1, source_target_pairs={{0,4},{4,8},{8,12},{12,0},{1,5},{5,9},{9,13},{13,1},{2,6},{6,10},{... | collective-permute-start | bytes 172040 | tf_op jit(solution)/shard_map/ppermute | solution.py:408

commit v4 on v3

--- a/solution.py
+++ b/solution.py
@@ -211,11 +211,11 @@
     return jnp.where(which(rows, columns), 1.0, 0.0).astype(jnp.bfloat16)
 
 
-def call(kernel, outs, args, scratch, flops):
+def call(kernel, outs, args, scratch, flops, space=pltpu.VMEM):
     return pl.pallas_call(
         kernel,
         out_shape=outs,
-        in_specs=[pl.BlockSpec(memory_space=pltpu.VMEM)] * len(args),
+        in_specs=[pl.BlockSpec(memory_space=space)] * len(args),
         out_specs=jax.tree.map(lambda out: pl.BlockSpec(memory_space=pltpu.VMEM), outs),
         scratch_shapes=scratch,
         compiler_params=pltpu.CompilerParams(vmem_limit_bytes=VMEM_BYTES),
@@ -223,8 +223,16 @@
     )(*args)
 
 
-def pack_kernel(q_ref, k_ref, v_ref, m0, m1, m2, m3, by_head):
+def pack_kernel(q_hbm, k_hbm, v_hbm, q_ref, k_ref, v_ref, m0, m1, m2, m3, by_head, arrivals):
     width, rows = q_ref.shape
+    copies = [
+        pltpu.make_async_copy(source, target, arrivals.at[at])
+        for at, (source, target) in enumerate(((q_hbm, q_ref), (k_hbm, k_ref), (v_hbm, v_ref)))
+    ]
+    for copy in copies:
+        copy.start()
+    for copy in copies:
+        copy.wait()
     heads = width // HEAD_DIM
     for parity in range(2):
         pick = one_hot(
@@ -414,19 +422,20 @@
     heads = width // HEAD_DIM
     count = rows // 2
     bf16, f32 = jnp.bfloat16, jnp.float32
-    turned = [block.T for block in (query_rows, key_rows, value_rows)]
-    messages = call(
+    turned = [pltpu.with_memory_space_constraint(block.T, pltpu.HBM) for block in (query_rows, key_rows, value_rows)]
+    *here, m0, m1, m2, m3 = call(
         pack_kernel,
-        [jax.ShapeDtypeStruct((3 * HEAD_DIM, count), bf16)] * heads,
+        [jax.ShapeDtypeStruct((width, rows), bf16)] * 3 + [jax.ShapeDtypeStruct((3 * HEAD_DIM, count), bf16)] * heads,
         turned,
-        [pltpu.VMEM((heads, 3 * HEAD_DIM, count), bf16)],
+        [pltpu.VMEM((heads, 3 * HEAD_DIM, count), bf16), pltpu.SemaphoreType.DMA((3,))],
         1 << 28,
-    )
-    arrived = by_rotation(messages, 1)
+        pltpu.HBM,
+    )
+    arrived = by_rotation((m0, m1, m2, m3), 1)
     near = call(
         near_kernel,
         jax.ShapeDtypeStruct((heads, HEAD_DIM + TAIL, rows), f32),
-        turned,
+        here,
         [pltpu.VMEM((heads, rows, HEAD_DIM), bf16)],
         4 * heads * rows * rows * 256,
     )

time: 46.1 us -> 44.3 us (0.961)
  local copies, waits for them, and re-layouts: 2.99 us -> 0 us
  Pallas kernels: 22.7 us -> 24 us
    unnamed x6 -> x0, local copies, waits for them, and re-layouts: 2.99 us -> none
    pallas_call x4, Pallas kernels: 22.7 us -> 24 us  [call(): pl.pallas_call(kernel, out_shape=outs, in_specs=[pl.BlockSpec(memory_spac...]
where the time goes in v4:
time: 44.3 us; the launch traced here: 44.2 us
  Pallas kernels  24 us (54%)
  starting transfers between devices  12.4 us (28%)
  waiting for transfers between devices  7.79 us (18%)
    pallas_call x4, Pallas kernels, call(): pl.pallas_call(kernel, out_shape=outs, in_specs=[pl.BlockSpec(memory_spac...  24 us
    ppermute x6, starting transfers between devices, by_rotation(): lax.ppermute(blocks[shift], 'seq', [(i, (i + sign * shift) % shards) for...  12.4 us
    ppermute x6, waiting for transfers between devices, by_rotation(): lax.ppermute(blocks[shift], 'seq', [(i, (i + sign * shift) % shards) for...  7.79 us
  transfers between devices with their start and end apart: 6, of which 4 were waited for; matrix products, arithmetic and copies ran while one was open for 0% of the time, Pallas kernels for 14%

profile of v4, /device:TPU:0, one launch (start us, length us, event | category | flops | bytes accessed | tf_op | source)
XLA Modules:
  0.0 44.2 jit_solution(2508774744416288316)
XLA Ops:
  0.0 1.8 %shard_map.37 = (bf16[192,1024]{1,0:T(8,128)(2,1)S(1)}, bf16[192,1024]{1,0:T(8,128)(2,1)S(1)}, bf16[192,1024]{1,0:T(8,128)(2,1)S(1)}, bf16[144,512]{1,0:T(8,128)...) custom-call(bf16[192,1024]{1,0:T(8,128)(2,1)} %bitcast.4, ...), custom_call_target="tpu_custom_call" | custom-call | flops 268435456 | bytes 2097152 | tf_op jit(solution)/shard_map/pallas_call | solution.py:215
  1.8 3.1 %collective-permute-start = (bf16[144,512]{1,0:T(8,128)(2,1)S(1)}, bf16[144,512]{1,0:T(8,128)(2,1)S(1)}, u32[]{:S(2)}, u32[]{:S(2)}) collective-permute-start(bf16[144,512]{1,0:T(8,128)(2,1)S(1)} %get-tuple-element.25), channel_id=1, source_target_pairs={{0,4},{4,8},{8,12},{12,0},{1,5},{5,9},{9,13},{13,1},{2,6},{6,10},{... | collective-permute-start | bytes 442376 | tf_op jit(solution)/shard_map/ppermute | solution.py:416
  4.9 2.6 %collective-permute-start.1 = (bf16[144,512]{1,0:T(8,128)(2,1)S(1)}, bf16[144,512]{1,0:T(8,128)(2,1)S(1)}, u32[]{:S(2)}, u32[]{:S(2)}) collective-permute-start(bf16[144,512]{1,0:T(8,128)(2,1)S(1)} %get-tuple-element.26), channel_id=1, source_target_pairs={{0,8},{4,12},{8,0},{12,4},{1,9},{5,13},{9,1},{13,5},{2,10},{6,14},... | collective-permute-start | bytes 442376 | tf_op jit(solution)/shard_map/ppermute | solution.py:416
  7.5 1.3 %collective-permute-start.2 = (bf16[144,512]{1,0:T(8,128)(2,1)S(1)}, bf16[144,512]{1,0:T(8,128)(2,1)S(1)}, u32[]{:S(2)}, u32[]{:S(2)}) collective-permute-start(bf16[144,512]{1,0:T(8,128)(2,1)S(1)} %get-tuple-element.27), channel_id=1, source_target_pairs={{0,12},{4,0},{8,4},{12,8},{1,13},{5,1},{9,5},{13,9},{2,14},{6,2},{... | collective-permute-start | bytes 442376 | tf_op jit(solution)/shard_map/ppermute | solution.py:416
  8.8 6.3 %shard_map.38.near_ref = f32[4,56,1024]{2,1,0:T(8,128)S(1)} custom-call(bf16[192,1024]{1,0:T(8,128)(2,1)S(1)} %get-tuple-element.21.qt_ref, bf16[192,1024]{1,0:T(8,128)(2,1)S(1)} %get-tuple-element.22.kt_ref, bf16[192,1024]{1,0:T(8,128)(2,1)S(1)} %get-tuple-element.23.vt_ref), custom_call_target="tpu_custom_call" | custom-call | flops 4294967296 | bytes 2097152 | tf_op jit(solution)/shard_map/pallas_call | solution.py:215
  15.1 0.0 collective-permute-done.m1
  15.1 2.1 %collective-permute-done.1.m2 = bf16[144,512]{1,0:T(8,128)(2,1)S(1)} collective-permute-done((bf16[144,512]{1,0:T(8,128)(2,1)S(1)}, bf16[144,512]{1,0:T(8,128)(2,1)S(1)}, u32[]{:S(2)}, u32[]{:S(2)}) %collective-permute-start.1) | collective-permute-done | bytes 147488 | tf_op jit(solution)/shard_map/ppermute | solution.py:416
  17.2 0.0 collective-permute-done.2.m3
  17.2 14.5 %shard_map.39 = (bf16[56,512]{1,0:T(8,128)(2,1)S(1)}, bf16[56,512]{1,0:T(8,128)(2,1)S(1)}, bf16[56,512]{1,0:T(8,128)(2,1)S(1)}, bf16[56,512]{1,0:T(8,128)(2,1)S(1)}) custom-call(bf16[144,512]{1,0:T(8,128)(2,1)S(1)} %get-tuple-element.29.m0, bf16[144,512]{1,0:T(8,128)(2,1)S(1)} %collective-permute-done.m1, bf16[144,512]{1,0:T(8,128)(2,1)S(1)} %collective-permute-done.1.m2, ...), custom_call_target="tpu_custom_call" | custom-call | flops 4294967296 | bytes 2097152 | tf_op jit(solution)/shard_map/pallas_call | solution.py:215
  31.7 4.8 %collective-permute-start.3 = (bf16[56,512]{1,0:T(8,128)(2,1)S(1)}, bf16[56,512]{1,0:T(8,128)(2,1)S(1)}, u32[]{:S(2)}, u32[]{:S(2)}) collective-permute-start(bf16[56,512]{1,0:T(8,128)(2,1)S(1)} %get-tuple-element.34), channel_id=1, source_target_pairs={{0,12},{4,0},{8,4},{12,8},{1,13},{5,1},{9,5},{13,9},{2,14},{6,2},{... | collective-permute-start | bytes 172040 | tf_op jit(solution)/shard_map/ppermute | solution.py:416
  36.5 0.4 collective-permute-start.4
  36.8 0.2 collective-permute-start.5
  37.1 1.4 %collective-permute-done.3.g1 = bf16[56,512]{1,0:T(8,128)(2,1)S(1)} collective-permute-done((bf16[56,512]{1,0:T(8,128)(2,1)S(1)}, bf16[56,512]{1,0:T(8,128)(2,1)S(1)}, u32[]{:S(2)}, u32[]{:S(2)}) %collective-permute-start.3) | collective-permute-done | bytes 57376 | tf_op jit(solution)/shard_map/ppermute | solution.py:416
  38.5 3.5 %collective-permute-done.4.g2 = bf16[56,512]{1,0:T(8,128)(2,1)S(1)} collective-permute-done((bf16[56,512]{1,0:T(8,128)(2,1)S(1)}, bf16[56,512]{1,0:T(8,128)(2,1)S(1)}, u32[]{:S(2)}, u32[]{:S(2)}) %collective-permute-start.4) | collective-permute-done | bytes 57376 | tf_op jit(solution)/shard_map/ppermute | solution.py:416
  42.1 0.8 %collective-permute-done.5.g3 = bf16[56,512]{1,0:T(8,128)(2,1)S(1)} collective-permute-done((bf16[56,512]{1,0:T(8,128)(2,1)S(1)}, bf16[56,512]{1,0:T(8,128)(2,1)S(1)}, u32[]{:S(2)}, u32[]{:S(2)}) %collective-permute-start.5) | collective-permute-done | bytes 57376 | tf_op jit(solution)/shard_map/ppermute | solution.py:416
  42.8 1.4 %shard_map.40 = bf16[192,1024]{1,0:T(8,128)(2,1)} custom-call(f32[4,56,1024]{2,1,0:T(8,128)S(1)} %shard_map.38.near_ref, bf16[56,512]{1,0:T(8,128)(2,1)S(1)} %get-tuple-element.33.g0, bf16[56,512]{1,0:T(8,128)(2,1)S(1)} %collective-permute-done.3.g1, bf16[56,512]{1,0:T(8,128)(2,1)S(1)} %collective-permute-done.4.g2, ...), custom_call_target="tpu_custom_call" | custom-call | flops 268435456 | bytes 2097152 | tf_op jit(solution)/shard_map/pallas_call | solution.py:215
Async XLA Ops:
  1.8 13.3 %collective-permute-start = (bf16[144,512]{1,0:T(8,128)(2,1)S(1)}, bf16[144,512]{1,0:T(8,128)(2,1)S(1)}, u32[]{:S(2)}, u32[]{:S(2)}) collective-permute-start(bf16[144,512]{1,0:T(8,128)(2,1)S(1)} %get-tuple-element.25), channel_id=1, source_target_pairs={{0,4},{4,8},{8,12},{12,0},{1,5},{5,9},{9,13},{13,1},{2,6},{6,10},{... | collective-permute-start | bytes 442376 | tf_op jit(solution)/shard_map/ppermute | solution.py:416
  4.9 12.3 %collective-permute-start.1 = (bf16[144,512]{1,0:T(8,128)(2,1)S(1)}, bf16[144,512]{1,0:T(8,128)(2,1)S(1)}, u32[]{:S(2)}, u32[]{:S(2)}) collective-permute-start(bf16[144,512]{1,0:T(8,128)(2,1)S(1)} %get-tuple-element.26), channel_id=1, source_target_pairs={{0,8},{4,12},{8,0},{12,4},{1,9},{5,13},{9,1},{13,5},{2,10},{6,14},... | collective-permute-start | bytes 442376 | tf_op jit(solution)/shard_map/ppermute | solution.py:416
  7.5 9.7 %collective-permute-start.2 = (bf16[144,512]{1,0:T(8,128)(2,1)S(1)}, bf16[144,512]{1,0:T(8,128)(2,1)S(1)}, u32[]{:S(2)}, u32[]{:S(2)}) collective-permute-start(bf16[144,512]{1,0:T(8,128)(2,1)S(1)} %get-tuple-element.27), channel_id=1, source_target_pairs={{0,12},{4,0},{8,4},{12,8},{1,13},{5,1},{9,5},{13,9},{2,14},{6,2},{... | collective-permute-start | bytes 442376 | tf_op jit(solution)/shard_map/ppermute | solution.py:416
  31.7 6.8 %collective-permute-start.3 = (bf16[56,512]{1,0:T(8,128)(2,1)S(1)}, bf16[56,512]{1,0:T(8,128)(2,1)S(1)}, u32[]{:S(2)}, u32[]{:S(2)}) collective-permute-start(bf16[56,512]{1,0:T(8,128)(2,1)S(1)} %get-tuple-element.34), channel_id=1, source_target_pairs={{0,12},{4,0},{8,4},{12,8},{1,13},{5,1},{9,5},{13,9},{2,14},{6,2},{... | collective-permute-start | bytes 172040 | tf_op jit(solution)/shard_map/ppermute | solution.py:416
  36.5 5.6 %collective-permute-start.4 = (bf16[56,512]{1,0:T(8,128)(2,1)S(1)}, bf16[56,512]{1,0:T(8,128)(2,1)S(1)}, u32[]{:S(2)}, u32[]{:S(2)}) collective-permute-start(bf16[56,512]{1,0:T(8,128)(2,1)S(1)} %get-tuple-element.35), channel_id=1, source_target_pairs={{0,8},{4,12},{8,0},{12,4},{1,9},{5,13},{9,1},{13,5},{2,10},{6,14},... | collective-permute-start | bytes 172040 | tf_op jit(solution)/shard_map/ppermute | solution.py:416
  36.8 6.0 %collective-permute-start.5 = (bf16[56,512]{1,0:T(8,128)(2,1)S(1)}, bf16[56,512]{1,0:T(8,128)(2,1)S(1)}, u32[]{:S(2)}, u32[]{:S(2)}) collective-permute-start(bf16[56,512]{1,0:T(8,128)(2,1)S(1)} %get-tuple-element.36), channel_id=1, source_target_pairs={{0,4},{4,8},{8,12},{12,0},{1,5},{5,9},{9,13},{13,1},{2,6},{6,10},{... | collective-permute-start | bytes 172040 | tf_op jit(solution)/shard_map/ppermute | solution.py:416

commit v5 on v4

--- a/solution.py
+++ b/solution.py
@@ -255,7 +255,7 @@
                     ]
     me = lax.axis_index("seq")
     for shift, message in enumerate((m0, m1, m2, m3)):
-        message[...] = by_head[lax.rem(me + shift, heads)]
+        message[...] = by_head[jnp.bitwise_xor(me, shift)]
 
 
 def with_ones(block):
@@ -340,27 +340,25 @@
     return jnp.concatenate([result[:HEAD_DIM] / total, parts], axis=0).astype(jnp.bfloat16)
 
 
-def far_kernel(m0, m1, m2, m3, o0, o1, o2, o3, keys_ref, queries_ref, values_ref):
+def far_kernel(m0, m1, m2, m3, o0, o1, keys_ref, queries_ref, values_ref):
     count = m0.shape[1]
     half = count // 2
-    sources, outs = (m0, m1, m2, m3), (o0, o1, o2, o3)
+    sources, outs = (m0, m1, m2, m3), (o0, o1)
     twice = jnp.where(lax.broadcasted_iota(jnp.int32, (1, count), 1) < half, 2.0, 1.0).astype(jnp.bfloat16)
     for at, source in enumerate(sources):
         keys_ref[pl.ds(at * count, count), :] = upright(source[pl.ds(HEAD_DIM, HEAD_DIM), :])
         values = with_ones(source[pl.ds(2 * HEAD_DIM, HEAD_DIM), :])
         values_ref[0, :, pl.ds(at * count, count)] = values * twice
         values_ref[1, :, pl.ds(at * count, count)] = values
-        for klass in range(2):
-            queries_ref[klass, :, pl.ds(at * half, half)] = source[pl.ds(0, HEAD_DIM), pl.ds(klass * half, half)]
     totals = []
     for klass in range(2):
-        for pair in range(0, len(sources), 2):
-            queries = queries_ref[klass, :, pl.ds(pair * half, count)]
-            result = plain(keys_ref[...], queries, values_ref[klass])
-            done = finished(result, None)
-            totals.append(result[HEAD_DIM : HEAD_DIM + 1])
-            for at in range(2):
-                outs[pair + at][:, pl.ds(klass * half, half)] = done[:, at * half : (at + 1) * half]
+        for at in range(2):
+            queries_ref[klass, :, pl.ds(at * half, half)] = sources[at][pl.ds(0, HEAD_DIM), pl.ds(klass * half, half)]
+        result = plain(keys_ref[...], queries_ref[klass], values_ref[klass])
+        done = finished(result, None)
+        totals.append(result[HEAD_DIM : HEAD_DIM + 1])
+        for at, out in enumerate(outs):
+            out[:, pl.ds(klass * half, half)] = done[:, at * half : (at + 1) * half]
 
     @pl.when(jnp.logical_not(in_range(totals)))
     def again():
@@ -371,50 +369,45 @@
                 out[:, pl.ds(pl.multiple_of(klass * half, LANES), half)] = finished(result, top)
 
 
-def merge_kernel(near_ref, g0, g1, g2, g3, out_ref, by_head):
-    heads, _, rows = near_ref.shape
+def merge_kernel(steps, near_ref, *refs):
+    results = refs[: len(steps)]
+    out_hbm, rows_ref, sent = refs[-3:]
+    rows = near_ref.shape[2]
     half = rows // STRIDES
     me = lax.axis_index("seq")
-    for shift, result in enumerate((g0, g1, g2, g3)):
-        by_head[lax.rem(me + shift, heads)] = result[...]
     position = lax.broadcasted_iota(jnp.int32, (1, SPAN), 1)
-    for parity in range(2):
+    copies = []
+    for at, (step, result) in enumerate(zip(steps, results)):
+        head = jnp.bitwise_xor(me, step)
         place = one_hot(
-            (2 * LANES, SPAN), lambda row, column: column == row % LANES * STRIDES + row // LANES * 2 + parity
+            (2 * LANES, SPAN),
+            lambda row, column: column == row % LANES * STRIDES + (head + row // LANES * 2) % STRIDES,
         )
-        used = position % 2 == parity
+        used = position % 2 == head % 2
         for block in range(rows // SPAN):
             lanes = pl.ds(block * SPAN, SPAN)
-            mine = range(parity, heads, 2)
-            pieces = []
-            for head in mine:
-                order = [(phase * 2 + parity - head) % STRIDES // 2 for phase in range(2)]
-                pieces.append(
-                    jnp.concatenate(
-                        [by_head[head, :, pl.ds(klass * half + block * LANES, LANES)] for klass in order], axis=1
-                    )
-                )
-            for head, piece in zip(mine, pieces):
-                there = dot_nn(piece, place)
-                near = near_ref[head, pl.ds(0, HEAD_DIM), lanes]
-                total = near_ref[head, pl.ds(HEAD_DIM, 1), lanes]
-                top = near_ref[head, pl.ds(HEAD_DIM + 1, 1), lanes]
-                lse = there[HEAD_DIM : HEAD_DIM + 1] + there[HEAD_DIM + 1 : HEAD_DIM + 2] + there[HEAD_DIM + 2 : HEAD_DIM + 3]
-                near_lse = top + jnp.log2(total)
-                peak = jnp.where(used, jnp.maximum(near_lse, lse), near_lse)
-                weight = jnp.exp2(top - peak)
-                far = jnp.where(used, jnp.exp2(lse - peak), 0.0)
-                share = 1.0 / (total * weight + far)
-                merged = near * (weight * share) + there[:HEAD_DIM] * (far * share)
-                out_ref[pl.ds(head * HEAD_DIM, HEAD_DIM), lanes] = merged.astype(jnp.bfloat16)
-
-
-def by_rotation(blocks, sign):
-    shards = lax.axis_size("seq")
-    moved = [blocks[0]]
-    for shift in range(1, shards):
-        moved.append(lax.ppermute(blocks[shift], "seq", [(i, (i + sign * shift) % shards) for i in range(shards)]))
-    return moved
+            piece = [result[:, pl.ds(klass * half + block * LANES, LANES)] for klass in range(2)]
+            there = dot_nn(jnp.concatenate(piece, axis=1), place)
+            near = near_ref[head, pl.ds(0, HEAD_DIM), lanes]
+            total = near_ref[head, pl.ds(HEAD_DIM, 1), lanes]
+            top = near_ref[head, pl.ds(HEAD_DIM + 1, 1), lanes]
+            lse = there[HEAD_DIM : HEAD_DIM + 1] + there[HEAD_DIM + 1 : HEAD_DIM + 2] + there[HEAD_DIM + 2 : HEAD_DIM + 3]
+            near_lse = top + jnp.log2(total)
+            peak = jnp.where(used, jnp.maximum(near_lse, lse), near_lse)
+            weight = jnp.exp2(top - peak)
+            far = jnp.where(used, jnp.exp2(lse - peak), 0.0)
+            share = 1.0 / (total * weight + far)
+            merged = near * (weight * share) + there[:HEAD_DIM] * (far * share)
+            rows_ref[at, :, lanes] = merged.astype(jnp.bfloat16)
+        features = pl.ds(pl.multiple_of(head * HEAD_DIM, HEAD_DIM), HEAD_DIM)
+        copies.append(pltpu.make_async_copy(rows_ref.at[at], out_hbm.at[features], sent.at[at]))
+        copies[-1].start()
+    for copy in copies:
+        copy.wait()
+
+
+def exchanged(block, step):
+    return lax.ppermute(block, "seq", [(i, i ^ step) for i in range(lax.axis_size("seq"))])
 
 
 def whole_slide(query_rows, key_rows, value_rows):
@@ -431,7 +424,7 @@
         1 << 28,
         pltpu.HBM,
     )
-    arrived = by_rotation((m0, m1, m2, m3), 1)
+    arrived = [m0, *(exchanged(message, step) for step, message in ((1, m1), (2, m2), (3, m3)))]
     near = call(
         near_kernel,
         jax.ShapeDtypeStruct((heads, HEAD_DIM + TAIL, rows), f32),
@@ -439,26 +432,42 @@
         [pltpu.VMEM((heads, rows, HEAD_DIM), bf16)],
         4 * heads * rows * rows * 256,
     )
-    near, *arrived = lax.optimization_barrier((near, *arrived))
-    far = call(
-        far_kernel,
-        [jax.ShapeDtypeStruct((HEAD_DIM + TAIL, count), bf16)] * heads,
-        arrived,
-        [
-            pltpu.VMEM((heads * count, HEAD_DIM), bf16),
-            pltpu.VMEM((2, HEAD_DIM, heads * count // 2), bf16),
-            pltpu.VMEM((2, HEAD_DIM + 2 * TAIL, heads * count), bf16),
-        ],
-        4 * heads * rows * rows * 256,
-    )
-    back = by_rotation(far, -1)
-    return call(
-        merge_kernel,
-        jax.ShapeDtypeStruct((width, rows), bf16),
-        [near, *back],
-        [pltpu.VMEM((heads, HEAD_DIM + TAIL, count), bf16)],
-        1 << 28,
-    ).T
+    def far(messages):
+        return call(
+            far_kernel,
+            [jax.ShapeDtypeStruct((HEAD_DIM + TAIL, count), bf16)] * 2,
+            messages,
+            [
+                pltpu.VMEM((heads * count, HEAD_DIM), bf16),
+                pltpu.VMEM((2, HEAD_DIM, count), bf16),
+                pltpu.VMEM((2, HEAD_DIM + 2 * TAIL, heads * count), bf16),
+            ],
+            2 * heads * rows * rows * 256,
+        )
+
+    def merged(steps, results, begun):
+        vmem, hbm = pl.BlockSpec(memory_space=pltpu.VMEM), pl.BlockSpec(memory_space=pl.ANY)
+        args = (near, *results, *begun)
+        return pl.pallas_call(
+            functools.partial(merge_kernel, steps),
+            out_shape=jax.ShapeDtypeStruct((width, rows), bf16),
+            in_specs=[vmem] * (1 + len(results)) + [hbm] * len(begun),
+            out_specs=hbm,
+            scratch_shapes=[pltpu.VMEM((len(steps), HEAD_DIM, rows), bf16), pltpu.SemaphoreType.DMA((len(steps),))],
+            input_output_aliases={len(args) - 1: 0} if begun else {},
+            compiler_params=pltpu.CompilerParams(vmem_limit_bytes=VMEM_BYTES),
+            cost_estimate=pl.CostEstimate(flops=len(steps) << 29, bytes_accessed=len(steps) << 20, transcendentals=0),
+        )(*args)
+
+    near, m0, m1, m2, m3 = lax.optimization_barrier((near, *arrived))
+    f2, f3 = far((m2, m3, m0, m1))
+    f2, f3, m0, m1, m2, m3 = lax.optimization_barrier((f2, f3, m0, m1, m2, m3))
+    g2, g3 = exchanged(f2, 2), exchanged(f3, 3)
+    g0, f1 = far((m0, m1, m2, m3))
+    g1 = exchanged(f1, 1)
+    own = merged((0,), (g0,), ())
+    most = merged((2, 3), (g2, g3), (own,))
+    return merged((1,), (g1,), (most,)).T
 
 
 def per_device(query_rows, key_rows, value_rows):

time: 44.3 us -> 44.4 us (level)
  Pallas kernels: 24 us -> 26.6 us
  starting transfers between devices: 12.4 us -> 10.5 us
  waiting for transfers between devices: 7.79 us -> 7 us
    pallas_call x0 -> x3, Pallas kernels: none -> 3.24 us  [merged(): pl.pallas_call(functools.partial(merge_kernel, steps), out_shape=jax.Shap...]
    ppermute x6, starting transfers between devices: 12.4 us -> 10.5 us  [exchanged(): lax.ppermute(block, 'seq', [(i, i ^ step) for i in range(lax.axis_size('s...]
    ppermute x6, waiting for transfers between devices: 7.79 us -> 7 us  [exchanged(): lax.ppermute(block, 'seq', [(i, i ^ step) for i in range(lax.axis_size('s...]
    pallas_call x4, Pallas kernels: 24 us -> 23.3 us  [call(): pl.pallas_call(kernel, out_shape=outs, in_specs=[pl.BlockSpec(memory_spac...]
  transfers between devices with their start and end apart: 6 -> 6, of which waited for: 4 -> 2; matrix products, arithmetic and copies ran while one was open for 0% -> 0% of each run, Pallas kernels for 14% -> 36%
where the time goes in v5:
time: 44.4 us; the launch traced here: 44.3 us
  Pallas kernels  26.6 us (60%)
  starting transfers between devices  10.5 us (24%)
  waiting for transfers between devices  7 us (16%)
    pallas_call x4, Pallas kernels, call(): pl.pallas_call(kernel, out_shape=outs, in_specs=[pl.BlockSpec(memory_spac...  23.3 us
    ppermute x6, starting transfers between devices, exchanged(): lax.ppermute(block, 'seq', [(i, i ^ step) for i in range(lax.axis_size('s...  10.5 us
    ppermute x6, waiting for transfers between devices, exchanged(): lax.ppermute(block, 'seq', [(i, i ^ step) for i in range(lax.axis_size('s...  7 us
    pallas_call x3, Pallas kernels, merged(): pl.pallas_call(functools.partial(merge_kernel, steps), out_shape=jax.Shap...  3.24 us
  transfers between devices with their start and end apart: 6, of which 2 were waited for; matrix products, arithmetic and copies ran while one was open for 0% of the time, Pallas kernels for 36%

profile of v5, /device:TPU:0, one launch (start us, length us, event | category | flops | bytes accessed | tf_op | source)
XLA Modules:
  0.0 44.3 jit_solution(13364346991517954667)
XLA Ops:
  0.0 1.8 %shard_map.37 = (bf16[192,1024]{1,0:T(8,128)(2,1)S(1)}, bf16[192,1024]{1,0:T(8,128)(2,1)S(1)}, bf16[192,1024]{1,0:T(8,128)(2,1)S(1)}, bf16[144,512]{1,0:T(8,128)...) custom-call(bf16[192,1024]{1,0:T(8,128)(2,1)} %bitcast.4, ...), custom_call_target="tpu_custom_call" | custom-call | flops 268435456 | bytes 2097152 | tf_op jit(solution)/shard_map/pallas_call | solution.py:215
  1.8 3.1 %collective-permute-start = (bf16[144,512]{1,0:T(8,128)(2,1)S(1)}, bf16[144,512]{1,0:T(8,128)(2,1)S(1)}, u32[]{:S(2)}, u32[]{:S(2)}) collective-permute-start(bf16[144,512]{1,0:T(8,128)(2,1)S(1)} %get-tuple-element.31), channel_id=1, source_target_pairs={{0,4},{4,0},{8,12},{12,8},{1,5},{5,1},{9,13},{13,9},{2,6},{6,2},{1... | collective-permute-start | bytes 442376 | tf_op jit(solution)/shard_map/ppermute | solution.py:410
  4.9 2.6 %collective-permute-start.1 = (bf16[144,512]{1,0:T(8,128)(2,1)S(1)}, bf16[144,512]{1,0:T(8,128)(2,1)S(1)}, u32[]{:S(2)}, u32[]{:S(2)}) collective-permute-start(bf16[144,512]{1,0:T(8,128)(2,1)S(1)} %get-tuple-element.32), channel_id=1, source_target_pairs={{0,8},{4,12},{8,0},{12,4},{1,9},{5,13},{9,1},{13,5},{2,10},{6,14},... | collective-permute-start | bytes 442376 | tf_op jit(solution)/shard_map/ppermute | solution.py:410
  7.5 0.0 collective-permute-start.2
  7.5 6.3 %shard_map.38.near_ref = f32[4,56,1024]{2,1,0:T(8,128)S(1)} custom-call(bf16[192,1024]{1,0:T(8,128)(2,1)S(1)} %get-tuple-element.27.qt_ref, bf16[192,1024]{1,0:T(8,128)(2,1)S(1)} %get-tuple-element.28.kt_ref, bf16[192,1024]{1,0:T(8,128)(2,1)S(1)} %get-tuple-element.29.vt_ref), custom_call_target="tpu_custom_call" | custom-call | flops 4294967296 | bytes 2097152 | tf_op jit(solution)/shard_map/pallas_call | solution.py:215
  13.8 0.0 collective-permute-done.m3.m1
  13.8 5.1 %collective-permute-done.1.m0.m2 = bf16[144,512]{1,0:T(8,128)(2,1)S(1)} collective-permute-done((bf16[144,512]{1,0:T(8,128)(2,1)S(1)}, bf16[144,512]{1,0:T(8,128)(2,1)S(1)}, u32[]{:S(2)}, u32[]{:S(2)}) %collective-permute-start.1) | collective-permute-done | bytes 147488 | tf_op jit(solution)/shard_map/ppermute | solution.py:410
  18.9 0.0 collective-permute-done.2.m1.m3
  18.9 7.7 %shard_map.39 = (bf16[56,512]{1,0:T(8,128)(2,1)S(1)}, bf16[56,512]{1,0:T(8,128)(2,1)S(1)}) custom-call(bf16[144,512]{1,0:T(8,128)(2,1)S(1)} %collective-permute-done.1.m0.m2, bf16[144,512]{1,0:T(8,128)(2,1)S(1)} %collective-permute-done.2.m1.m3, bf16[144,512]{1,0:T(8,128)(2,1)S(1)} %get-tuple-element.41.m2.m0, bf16[144,512]{1,0:T(8,128)(2,1)S(1)} %collective-permute-done.m3.m1), custom_call_target="tpu_custom_call" | custom-call | flops 2147483648 | bytes 2097152 | tf_op jit(solution)/shard_map/pallas_call | solution.py:215
  26.6 3.4 %collective-permute-start.4 = (bf16[56,512]{1,0:T(8,128)(2,1)S(1)}, bf16[56,512]{1,0:T(8,128)(2,1)S(1)}, u32[]{:S(2)}, u32[]{:S(2)}) collective-permute-start(bf16[56,512]{1,0:T(8,128)(2,1)S(1)} %get-tuple-element.46), channel_id=1, source_target_pairs={{0,8},{4,12},{8,0},{12,4},{1,9},{5,13},{9,1},{13,5},{2,10},{6,14},... | collective-permute-start | bytes 172040 | tf_op jit(solution)/shard_map/ppermute | solution.py:410
  30.0 1.4 %collective-permute-start.5 = (bf16[56,512]{1,0:T(8,128)(2,1)S(1)}, bf16[56,512]{1,0:T(8,128)(2,1)S(1)}, u32[]{:S(2)}, u32[]{:S(2)}) collective-permute-start(bf16[56,512]{1,0:T(8,128)(2,1)S(1)} %get-tuple-element.47), channel_id=1, source_target_pairs={{0,12},{4,8},{8,4},{12,0},{1,13},{5,9},{9,5},{13,1},{2,14},{6,10},... | collective-permute-start | bytes 172040 | tf_op jit(solution)/shard_map/ppermute | solution.py:410
  31.4 7.5 %shard_map.40 = (bf16[56,512]{1,0:T(8,128)(2,1)S(1)}, bf16[56,512]{1,0:T(8,128)(2,1)S(1)}) custom-call(bf16[144,512]{1,0:T(8,128)(2,1)S(1)} %get-tuple-element.41.m2.m0, bf16[144,512]{1,0:T(8,128)(2,1)S(1)} %collective-permute-done.m3.m1, bf16[144,512]{1,0:T(8,128)(2,1)S(1)} %collective-permute-done.1.m0.m2, bf16[144,512]{1,0:T(8,128)(2,1)S(1)} %collective-permute-done.2.m1.m3), custom_call_target="tpu_custom_call" | custom-call | flops 2147483648 | bytes 2097152 | tf_op jit(solution)/shard_map/pallas_call | solution.py:215
  38.9 0.1 collective-permute-start.3
  39.0 1.0 %shard_map.41.refs_2_ = bf16[192,1024]{1,0:T(8,128)(2,1)} custom-call(f32[4,56,1024]{2,1,0:T(8,128)S(1)} %shard_map.38.near_ref, bf16[56,512]{1,0:T(8,128)(2,1)S(1)} %get-tuple-element.48.refs_0_), custom_call_target="tpu_custom_call" | custom-call | flops 536870912 | bytes 1048576 | tf_op jit(solution)/shard_map/pallas_call | solution.py:451
  40.0 0.0 collective-permute-done.4.refs_0_
  40.0 0.0 collective-permute-done.5.refs_1_
  40.0 1.2 %shard_map.42.refs_1_ = bf16[192,1024]{1,0:T(8,128)(2,1)} custom-call(f32[4,56,1024]{2,1,0:T(8,128)S(1)} %shard_map.38.near_ref, bf16[56,512]{1,0:T(8,128)(2,1)S(1)} %collective-permute-done.4.refs_0_, bf16[56,512]{1,0:T(8,128)(2,1)S(1)} %collective-permute-done.5.refs_1_, bf16[192,1024]{1,0:T(8,128)(2,1)} %shard_map.41.refs_2_), custom_call_target="tpu_custom_call", output_to_operand_aliasing={{}: (3, {})} | custom-call | flops 1073741824 | bytes 2097152 | tf_op jit(solution)/shard_map/pallas_call | solution.py:451
  41.2 1.9 %collective-permute-done.3.refs_0_ = bf16[56,512]{1,0:T(8,128)(2,1)S(1)} collective-permute-done((bf16[56,512]{1,0:T(8,128)(2,1)S(1)}, bf16[56,512]{1,0:T(8,128)(2,1)S(1)}, u32[]{:S(2)}, u32[]{:S(2)}) %collective-permute-start.3) | collective-permute-done | bytes 57376 | tf_op jit(solution)/shard_map/ppermute | solution.py:410
  43.1 1.0 %shard_map.43 = bf16[192,1024]{1,0:T(8,128)(2,1)} custom-call(f32[4,56,1024]{2,1,0:T(8,128)S(1)} %shard_map.38.near_ref, bf16[56,512]{1,0:T(8,128)(2,1)S(1)} %collective-permute-done.3.refs_0_, bf16[192,1024]{1,0:T(8,128)(2,1)} %shard_map.42.refs_1_), custom_call_target="tpu_custom_call", output_to_operand_aliasing={{}: (2, {})} | custom-call | flops 536870912 | bytes 1048576 | tf_op jit(solution)/shard_map/pallas_call | solution.py:451
Async XLA Ops:
  1.8 12.0 %collective-permute-start = (bf16[144,512]{1,0:T(8,128)(2,1)S(1)}, bf16[144,512]{1,0:T(8,128)(2,1)S(1)}, u32[]{:S(2)}, u32[]{:S(2)}) collective-permute-start(bf16[144,512]{1,0:T(8,128)(2,1)S(1)} %get-tuple-element.31), channel_id=1, source_target_pairs={{0,4},{4,0},{8,12},{12,8},{1,5},{5,1},{9,13},{13,9},{2,6},{6,2},{1... | collective-permute-start | bytes 442376 | tf_op jit(solution)/shard_map/ppermute | solution.py:410
  4.9 14.0 %collective-permute-start.1 = (bf16[144,512]{1,0:T(8,128)(2,1)S(1)}, bf16[144,512]{1,0:T(8,128)(2,1)S(1)}, u32[]{:S(2)}, u32[]{:S(2)}) collective-permute-start(bf16[144,512]{1,0:T(8,128)(2,1)S(1)} %get-tuple-element.32), channel_id=1, source_target_pairs={{0,8},{4,12},{8,0},{12,4},{1,9},{5,13},{9,1},{13,5},{2,10},{6,14},... | collective-permute-start | bytes 442376 | tf_op jit(solution)/shard_map/ppermute | solution.py:410
  7.5 11.4 %collective-permute-start.2 = (bf16[144,512]{1,0:T(8,128)(2,1)S(1)}, bf16[144,512]{1,0:T(8,128)(2,1)S(1)}, u32[]{:S(2)}, u32[]{:S(2)}) collective-permute-start(bf16[144,512]{1,0:T(8,128)(2,1)S(1)} %get-tuple-element.33), channel_id=1, source_target_pairs={{0,12},{4,8},{8,4},{12,0},{1,13},{5,9},{9,5},{13,1},{2,14},{6,10},... | collective-permute-start | bytes 442376 | tf_op jit(solution)/shard_map/ppermute | solution.py:410
  26.6 13.4 %collective-permute-start.4 = (bf16[56,512]{1,0:T(8,128)(2,1)S(1)}, bf16[56,512]{1,0:T(8,128)(2,1)S(1)}, u32[]{:S(2)}, u32[]{:S(2)}) collective-permute-start(bf16[56,512]{1,0:T(8,128)(2,1)S(1)} %get-tuple-element.46), channel_id=1, source_target_pairs={{0,8},{4,12},{8,0},{12,4},{1,9},{5,13},{9,1},{13,5},{2,10},{6,14},... | collective-permute-start | bytes 172040 | tf_op jit(solution)/shard_map/ppermute | solution.py:410
  30.0 10.0 %collective-permute-start.5 = (bf16[56,512]{1,0:T(8,128)(2,1)S(1)}, bf16[56,512]{1,0:T(8,128)(2,1)S(1)}, u32[]{:S(2)}, u32[]{:S(2)}) collective-permute-start(bf16[56,512]{1,0:T(8,128)(2,1)S(1)} %get-tuple-element.47), channel_id=1, source_target_pairs={{0,12},{4,8},{8,4},{12,0},{1,13},{5,9},{9,5},{13,1},{2,14},{6,10},... | collective-permute-start | bytes 172040 | tf_op jit(solution)/shard_map/ppermute | solution.py:410
  38.9 4.2 %collective-permute-start.3 = (bf16[56,512]{1,0:T(8,128)(2,1)S(1)}, bf16[56,512]{1,0:T(8,128)(2,1)S(1)}, u32[]{:S(2)}, u32[]{:S(2)}) collective-permute-start(bf16[56,512]{1,0:T(8,128)(2,1)S(1)} %get-tuple-element.45), channel_id=1, source_target_pairs={{0,4},{4,0},{8,12},{12,8},{1,5},{5,1},{9,13},{13,9},{2,6},{6,2},{1... | collective-permute-start | bytes 172040 | tf_op jit(solution)/shard_map/ppermute | solution.py:410

commit v6 on v5

--- a/solution.py
+++ b/solution.py
@@ -223,7 +223,7 @@
     )(*args)
 
 
-def pack_kernel(q_hbm, k_hbm, v_hbm, q_ref, k_ref, v_ref, m0, m1, m2, m3, by_head, arrivals):
+def pack_kernel(q_hbm, k_hbm, v_hbm, q_ref, k_ref, v_ref, m2, m3, m1, m0, by_head, arrivals):
     width, rows = q_ref.shape
     copies = [
         pltpu.make_async_copy(source, target, arrivals.at[at])
@@ -254,7 +254,7 @@
                         :, phase * LANES : (phase + 1) * LANES
                     ]
     me = lax.axis_index("seq")
-    for shift, message in enumerate((m0, m1, m2, m3)):
+    for shift, message in ((2, m2), (3, m3), (1, m1), (0, m0)):
         message[...] = by_head[jnp.bitwise_xor(me, shift)]
 
 
@@ -416,7 +416,7 @@
     count = rows // 2
     bf16, f32 = jnp.bfloat16, jnp.float32
     turned = [pltpu.with_memory_space_constraint(block.T, pltpu.HBM) for block in (query_rows, key_rows, value_rows)]
-    *here, m0, m1, m2, m3 = call(
+    *here, m2, m3, m1, m0 = call(
         pack_kernel,
         [jax.ShapeDtypeStruct((width, rows), bf16)] * 3 + [jax.ShapeDtypeStruct((3 * HEAD_DIM, count), bf16)] * heads,
         turned,
@@ -424,7 +424,8 @@
         1 << 28,
         pltpu.HBM,
     )
-    arrived = [m0, *(exchanged(message, step) for step, message in ((1, m1), (2, m2), (3, m3)))]
+    n2, n3 = exchanged(m2, 2), exchanged(m3, 3)
+    arrived = (n3, n2, exchanged(m1, 1), m0)
     near = call(
         near_kernel,
         jax.ShapeDtypeStruct((heads, HEAD_DIM + TAIL, rows), f32),
@@ -459,7 +460,7 @@
             cost_estimate=pl.CostEstimate(flops=len(steps) << 29, bytes_accessed=len(steps) << 20, transcendentals=0),
         )(*args)
 
-    near, m0, m1, m2, m3 = lax.optimization_barrier((near, *arrived))
+    m3, m2, m1, m0, near = lax.optimization_barrier((*arrived, near))
     f2, f3 = far((m2, m3, m0, m1))
     f2, f3, m0, m1, m2, m3 = lax.optimization_barrier((f2, f3, m0, m1, m2, m3))
     g2, g3 = exchanged(f2, 2), exchanged(f3, 3)

time: 44.4 us -> 42.9 us (0.966)
  starting transfers between devices: 10.5 us -> 9.37 us
    ppermute x6, starting transfers between devices: 10.5 us -> 9.37 us  [exchanged(): lax.ppermute(block, 'seq', [(i, i ^ step) for i in range(lax.axis_size('s...]
  transfers between devices with their start and end apart: 6 -> 6, of which waited for: 2 -> 2; matrix products, arithmetic and copies ran while one was open for 0% -> 0% of each run, Pallas kernels for 36% -> 37%
where the time goes in v6:
time: 42.9 us; the launch traced here: 42.8 us
  Pallas kernels  26.5 us (62%)
  starting transfers between devices  9.37 us (22%)
  waiting for transfers between devices  6.6 us (15%)
    pallas_call x4, Pallas kernels, call(): pl.pallas_call(kernel, out_shape=outs, in_specs=[pl.BlockSpec(memory_spac...  23.3 us
    ppermute x6, starting transfers between devices, exchanged(): lax.ppermute(block, 'seq', [(i, i ^ step) for i in range(lax.axis_size('s...  9.37 us
    ppermute x6, waiting for transfers between devices, exchanged(): lax.ppermute(block, 'seq', [(i, i ^ step) for i in range(lax.axis_size('s...  6.6 us
    pallas_call x3, Pallas kernels, merged(): pl.pallas_call(functools.partial(merge_kernel, steps), out_shape=jax.Shap...  3.24 us
  transfers between devices with their start and end apart: 6, of which 2 were waited for; matrix products, arithmetic and copies ran while one was open for 0% of the time, Pallas kernels for 37%

profile of v6, /device:TPU:0, one launch (start us, length us, event | category | flops | bytes accessed | tf_op | source)
XLA Modules:
  0.0 42.8 jit_solution(10612737488626221830)
XLA Ops:
  0.0 1.8 %shard_map.37 = (bf16[192,1024]{1,0:T(8,128)(2,1)S(1)}, bf16[192,1024]{1,0:T(8,128)(2,1)S(1)}, bf16[192,1024]{1,0:T(8,128)(2,1)S(1)}, bf16[144,512]{1,0:T(8,128)...) custom-call(bf16[192,1024]{1,0:T(8,128)(2,1)} %bitcast.4, ...), custom_call_target="tpu_custom_call" | custom-call | flops 268435456 | bytes 2097152 | tf_op jit(solution)/shard_map/pallas_call | solution.py:215
  1.8 5.1 %collective-permute-start = (bf16[144,512]{1,0:T(8,128)(2,1)S(1)}, bf16[144,512]{1,0:T(8,128)(2,1)S(1)}, u32[]{:S(2)}, u32[]{:S(2)}) collective-permute-start(bf16[144,512]{1,0:T(8,128)(2,1)S(1)} %get-tuple-element.27), channel_id=1, source_target_pairs={{0,12},{4,8},{8,4},{12,0},{1,13},{5,9},{9,5},{13,1},{2,14},{6,10},... | collective-permute-start | bytes 442376 | tf_op jit(solution)/shard_map/ppermute | solution.py:410
  6.9 0.0 collective-permute-start.1
  6.9 0.6 %collective-permute-start.2 = (bf16[144,512]{1,0:T(8,128)(2,1)S(1)}, bf16[144,512]{1,0:T(8,128)(2,1)S(1)}, u32[]{:S(2)}, u32[]{:S(2)}) collective-permute-start(bf16[144,512]{1,0:T(8,128)(2,1)S(1)} %get-tuple-element.29), channel_id=1, source_target_pairs={{0,4},{4,0},{8,12},{12,8},{1,5},{5,1},{9,13},{13,9},{2,6},{6,2},{1... | collective-permute-start | bytes 442376 | tf_op jit(solution)/shard_map/ppermute | solution.py:410
  7.6 6.2 %shard_map.38.near_ref = f32[4,56,1024]{2,1,0:T(8,128)S(1)} custom-call(bf16[192,1024]{1,0:T(8,128)(2,1)S(1)} %get-tuple-element.31.qt_ref, bf16[192,1024]{1,0:T(8,128)(2,1)S(1)} %get-tuple-element.32.kt_ref, bf16[192,1024]{1,0:T(8,128)(2,1)S(1)} %get-tuple-element.33.vt_ref), custom_call_target="tpu_custom_call" | custom-call | flops 4294967296 | bytes 2097152 | tf_op jit(solution)/shard_map/pallas_call | solution.py:215
  13.8 0.0 collective-permute-done.m1.m3
  13.8 5.6 %collective-permute-done.1.m0.m2 = bf16[144,512]{1,0:T(8,128)(2,1)S(1)} collective-permute-done((bf16[144,512]{1,0:T(8,128)(2,1)S(1)}, bf16[144,512]{1,0:T(8,128)(2,1)S(1)}, u32[]{:S(2)}, u32[]{:S(2)}) %collective-permute-start.1) | collective-permute-done | bytes 147488 | tf_op jit(solution)/shard_map/ppermute | solution.py:410
  19.4 0.0 collective-permute-done.2.m3.m1
  19.4 7.7 %shard_map.39 = (bf16[56,512]{1,0:T(8,128)(2,1)S(1)}, bf16[56,512]{1,0:T(8,128)(2,1)S(1)}) custom-call(bf16[144,512]{1,0:T(8,128)(2,1)S(1)} %collective-permute-done.1.m0.m2, bf16[144,512]{1,0:T(8,128)(2,1)S(1)} %collective-permute-done.m1.m3, bf16[144,512]{1,0:T(8,128)(2,1)S(1)} %get-tuple-element.41.m2.m0, bf16[144,512]{1,0:T(8,128)(2,1)S(1)} %collective-permute-done.2.m3.m1), custom_call_target="tpu_custom_call" | custom-call | flops 2147483648 | bytes 2097152 | tf_op jit(solution)/shard_map/pallas_call | solution.py:215
  27.1 0.1 collective-permute-start.4
  27.2 2.6 %collective-permute-start.5 = (bf16[56,512]{1,0:T(8,128)(2,1)S(1)}, bf16[56,512]{1,0:T(8,128)(2,1)S(1)}, u32[]{:S(2)}, u32[]{:S(2)}) collective-permute-start(bf16[56,512]{1,0:T(8,128)(2,1)S(1)} %get-tuple-element.47), channel_id=1, source_target_pairs={{0,12},{4,8},{8,4},{12,0},{1,13},{5,9},{9,5},{13,1},{2,14},{6,10},... | collective-permute-start | bytes 172040 | tf_op jit(solution)/shard_map/ppermute | solution.py:410
  29.8 7.5 %shard_map.40 = (bf16[56,512]{1,0:T(8,128)(2,1)S(1)}, bf16[56,512]{1,0:T(8,128)(2,1)S(1)}) custom-call(bf16[144,512]{1,0:T(8,128)(2,1)S(1)} %get-tuple-element.41.m2.m0, bf16[144,512]{1,0:T(8,128)(2,1)S(1)} %collective-permute-done.2.m3.m1, bf16[144,512]{1,0:T(8,128)(2,1)S(1)} %collective-permute-done.1.m0.m2, bf16[144,512]{1,0:T(8,128)(2,1)S(1)} %collective-permute-done.m1.m3), custom_call_target="tpu_custom_call" | custom-call | flops 2147483648 | bytes 2097152 | tf_op jit(solution)/shard_map/pallas_call | solution.py:215
  37.3 0.9 %collective-permute-start.3 = (bf16[56,512]{1,0:T(8,128)(2,1)S(1)}, bf16[56,512]{1,0:T(8,128)(2,1)S(1)}, u32[]{:S(2)}, u32[]{:S(2)}) collective-permute-start(bf16[56,512]{1,0:T(8,128)(2,1)S(1)} %get-tuple-element.45), channel_id=1, source_target_pairs={{0,4},{4,0},{8,12},{12,8},{1,5},{5,1},{9,13},{13,9},{2,6},{6,2},{1... | collective-permute-start | bytes 172040 | tf_op jit(solution)/shard_map/ppermute | solution.py:410
  38.3 1.0 %shard_map.41.refs_2_ = bf16[192,1024]{1,0:T(8,128)(2,1)} custom-call(f32[4,56,1024]{2,1,0:T(8,128)S(1)} %shard_map.38.near_ref, bf16[56,512]{1,0:T(8,128)(2,1)S(1)} %get-tuple-element.48.refs_0_), custom_call_target="tpu_custom_call" | custom-call | flops 536870912 | bytes 1048576 | tf_op jit(solution)/shard_map/pallas_call | solution.py:452
  39.3 0.0 collective-permute-done.4.refs_0_
  39.3 0.0 collective-permute-done.5.refs_1_
  39.3 1.2 %shard_map.42.refs_1_ = bf16[192,1024]{1,0:T(8,128)(2,1)} custom-call(f32[4,56,1024]{2,1,0:T(8,128)S(1)} %shard_map.38.near_ref, bf16[56,512]{1,0:T(8,128)(2,1)S(1)} %collective-permute-done.4.refs_0_, bf16[56,512]{1,0:T(8,128)(2,1)S(1)} %collective-permute-done.5.refs_1_, bf16[192,1024]{1,0:T(8,128)(2,1)} %shard_map.41.refs_2_), custom_call_target="tpu_custom_call", output_to_operand_aliasing={{}: (3, {})} | custom-call | flops 1073741824 | bytes 2097152 | tf_op jit(solution)/shard_map/pallas_call | solution.py:452
  40.5 1.0 %collective-permute-done.3.refs_0_ = bf16[56,512]{1,0:T(8,128)(2,1)S(1)} collective-permute-done((bf16[56,512]{1,0:T(8,128)(2,1)S(1)}, bf16[56,512]{1,0:T(8,128)(2,1)S(1)}, u32[]{:S(2)}, u32[]{:S(2)}) %collective-permute-start.3) | collective-permute-done | bytes 57376 | tf_op jit(solution)/shard_map/ppermute | solution.py:410
  41.6 1.0 %shard_map.43 = bf16[192,1024]{1,0:T(8,128)(2,1)} custom-call(f32[4,56,1024]{2,1,0:T(8,128)S(1)} %shard_map.38.near_ref, bf16[56,512]{1,0:T(8,128)(2,1)S(1)} %collective-permute-done.3.refs_0_, bf16[192,1024]{1,0:T(8,128)(2,1)} %shard_map.42.refs_1_), custom_call_target="tpu_custom_call", output_to_operand_aliasing={{}: (2, {})} | custom-call | flops 536870912 | bytes 1048576 | tf_op jit(solution)/shard_map/pallas_call | solution.py:452
Async XLA Ops:
  1.8 12.0 %collective-permute-start = (bf16[144,512]{1,0:T(8,128)(2,1)S(1)}, bf16[144,512]{1,0:T(8,128)(2,1)S(1)}, u32[]{:S(2)}, u32[]{:S(2)}) collective-permute-start(bf16[144,512]{1,0:T(8,128)(2,1)S(1)} %get-tuple-element.27), channel_id=1, source_target_pairs={{0,12},{4,8},{8,4},{12,0},{1,13},{5,9},{9,5},{13,1},{2,14},{6,10},... | collective-permute-start | bytes 442376 | tf_op jit(solution)/shard_map/ppermute | solution.py:410
  6.9 12.5 %collective-permute-start.1 = (bf16[144,512]{1,0:T(8,128)(2,1)S(1)}, bf16[144,512]{1,0:T(8,128)(2,1)S(1)}, u32[]{:S(2)}, u32[]{:S(2)}) collective-permute-start(bf16[144,512]{1,0:T(8,128)(2,1)S(1)} %get-tuple-element.28), channel_id=1, source_target_pairs={{0,8},{4,12},{8,0},{12,4},{1,9},{5,13},{9,1},{13,5},{2,10},{6,14},... | collective-permute-start | bytes 442376 | tf_op jit(solution)/shard_map/ppermute | solution.py:410
  6.9 12.5 %collective-permute-start.2 = (bf16[144,512]{1,0:T(8,128)(2,1)S(1)}, bf16[144,512]{1,0:T(8,128)(2,1)S(1)}, u32[]{:S(2)}, u32[]{:S(2)}) collective-permute-start(bf16[144,512]{1,0:T(8,128)(2,1)S(1)} %get-tuple-element.29), channel_id=1, source_target_pairs={{0,4},{4,0},{8,12},{12,8},{1,5},{5,1},{9,13},{13,9},{2,6},{6,2},{1... | collective-permute-start | bytes 442376 | tf_op jit(solution)/shard_map/ppermute | solution.py:410
  27.1 12.2 %collective-permute-start.4 = (bf16[56,512]{1,0:T(8,128)(2,1)S(1)}, bf16[56,512]{1,0:T(8,128)(2,1)S(1)}, u32[]{:S(2)}, u32[]{:S(2)}) collective-permute-start(bf16[56,512]{1,0:T(8,128)(2,1)S(1)} %get-tuple-element.46), channel_id=1, source_target_pairs={{0,8},{4,12},{8,0},{12,4},{1,9},{5,13},{9,1},{13,5},{2,10},{6,14},... | collective-permute-start | bytes 172040 | tf_op jit(solution)/shard_map/ppermute | solution.py:410
  27.2 12.1 %collective-permute-start.5 = (bf16[56,512]{1,0:T(8,128)(2,1)S(1)}, bf16[56,512]{1,0:T(8,128)(2,1)S(1)}, u32[]{:S(2)}, u32[]{:S(2)}) collective-permute-start(bf16[56,512]{1,0:T(8,128)(2,1)S(1)} %get-tuple-element.47), channel_id=1, source_target_pairs={{0,12},{4,8},{8,4},{12,0},{1,13},{5,9},{9,5},{13,1},{2,14},{6,10},... | collective-permute-start | bytes 172040 | tf_op jit(solution)/shard_map/ppermute | solution.py:410
  37.3 4.2 %collective-permute-start.3 = (bf16[56,512]{1,0:T(8,128)(2,1)S(1)}, bf16[56,512]{1,0:T(8,128)(2,1)S(1)}, u32[]{:S(2)}, u32[]{:S(2)}) collective-permute-start(bf16[56,512]{1,0:T(8,128)(2,1)S(1)} %get-tuple-element.45), channel_id=1, source_target_pairs={{0,4},{4,0},{8,12},{12,8},{1,5},{5,1},{9,13},{13,9},{2,6},{6,2},{1... | collective-permute-start | bytes 172040 | tf_op jit(solution)/shard_map/ppermute | solution.py:410

commit v7 on v6

--- a/solution.py
+++ b/solution.py
@@ -189,6 +189,7 @@
 LANES = 128
 SPAN = STRIDES * LANES
 NEAR_KEYS = 256
+LOW_HEADS = 1
 TAIL = 8
 LOG2E = 1.4426950408889634
 FACTOR = HEAD_DIM ** (-0.5) * LOG2E
@@ -276,10 +277,13 @@
     return dot_nn(values, jnp.exp2(dot_nn(keys, queries) * FACTOR).astype(jnp.bfloat16))
 
 
-def shifted(keys, queries, values):
-    scores = dot_nn(keys, queries)
-    top = jnp.max(scores, axis=0, keepdims=True) * FACTOR
-    return dot_nn(values, jnp.exp2(scores * FACTOR - top).astype(jnp.bfloat16)), top
+def shifted(groups, queries):
+    scores = [dot_nn(keys, queries) for keys, _ in groups]
+    top = functools.reduce(jnp.maximum, [jnp.max(block, axis=0, keepdims=True) for block in scores]) * FACTOR
+    terms = [
+        dot_nn(values, jnp.exp2(block * FACTOR - top).astype(jnp.bfloat16)) for block, (_, values) in zip(scores, groups)
+    ]
+    return functools.reduce(jnp.add, terms), top
 
 
 def in_range(totals):
@@ -288,18 +292,17 @@
     return jnp.logical_and(jnp.min(low) >= LEAST_TOTAL, jnp.max(high) <= MOST_TOTAL)
 
 
-def near_kernel(qt_ref, kt_ref, vt_ref, out_ref, keys_ref):
-    width, rows = qt_ref.shape
-    heads = width // HEAD_DIM
-    keys = upright(kt_ref[...])
+def near_kernel(first, qt_ref, kt_ref, vt_ref, out_ref, keys_ref):
+    rows = qt_ref.shape[1]
+    heads = out_ref.shape[0]
     for head in range(heads):
-        keys_ref[head] = keys[:, head * HEAD_DIM : (head + 1) * HEAD_DIM]
+        keys_ref[head] = upright(kt_ref[pl.ds((first + head) * HEAD_DIM, HEAD_DIM), :])
     blocks = [(head, start) for head in range(heads) for start in range(0, rows, SPAN)]
     pieces = range(0, rows, NEAR_KEYS)
 
     def scores_of(block, piece):
         head, start = block
-        queries = qt_ref[pl.ds(head * HEAD_DIM, HEAD_DIM), pl.ds(start, SPAN)]
+        queries = qt_ref[pl.ds((first + head) * HEAD_DIM, HEAD_DIM), pl.ds(start, SPAN)]
         return dot_nn(keys_ref[head, pl.ds(piece, NEAR_KEYS), :], queries)
 
     def folded(values, join, held):
@@ -319,7 +322,7 @@
                 peaks = folded(later[-1], jnp.maximum, peaks)
             probs = jnp.exp2(scores * FACTOR - top)
             totals = folded(probs, jnp.add, totals)
-            values = vt_ref[pl.ds(head * HEAD_DIM, HEAD_DIM), pl.ds(piece, NEAR_KEYS)]
+            values = vt_ref[pl.ds((first + head) * HEAD_DIM, HEAD_DIM), pl.ds(piece, NEAR_KEYS)]
             term = dot_nn(values, probs.astype(jnp.bfloat16))
             result = term if result is None else result + term
         lanes = pl.ds(start, SPAN)
@@ -340,39 +343,76 @@
     return jnp.concatenate([result[:HEAD_DIM] / total, parts], axis=0).astype(jnp.bfloat16)
 
 
-def far_kernel(m0, m1, m2, m3, o0, o1, keys_ref, queries_ref, values_ref):
-    count = m0.shape[1]
+def fill(messages, keys_ref, queries_ref, values_ref):
+    count = messages[0].shape[1]
     half = count // 2
-    sources, outs = (m0, m1, m2, m3), (o0, o1)
     twice = jnp.where(lax.broadcasted_iota(jnp.int32, (1, count), 1) < half, 2.0, 1.0).astype(jnp.bfloat16)
-    for at, source in enumerate(sources):
-        keys_ref[pl.ds(at * count, count), :] = upright(source[pl.ds(HEAD_DIM, HEAD_DIM), :])
-        values = with_ones(source[pl.ds(2 * HEAD_DIM, HEAD_DIM), :])
-        values_ref[0, :, pl.ds(at * count, count)] = values * twice
-        values_ref[1, :, pl.ds(at * count, count)] = values
-    totals = []
+    for at, message in enumerate(messages):
+        if keys_ref is not None:
+            keys_ref[pl.ds(at * count, count), :] = upright(message[pl.ds(HEAD_DIM, HEAD_DIM), :])
+        if values_ref is not None:
+            values = with_ones(message[pl.ds(2 * HEAD_DIM, HEAD_DIM), :])
+            values_ref[0, :, pl.ds(at * count, count)] = values * twice
+            values_ref[1, :, pl.ds(at * count, count)] = values
+        if queries_ref is not None:
+            for klass in range(2):
+                queries_ref[klass, :, pl.ds(at * half, half)] = message[pl.ds(0, HEAD_DIM), pl.ds(klass * half, half)]
+
+
+def early_kernel(m0, m1, keys_ref, part_ref, queries_ref, values_ref):
+    fill((m0, m1), keys_ref, queries_ref, values_ref)
     for klass in range(2):
+        part_ref[klass] = plain(keys_ref[...], queries_ref[klass], values_ref[klass])
+
+
+def store(outs, klass, at, block):
+    half = block.shape[1]
+    outs[at][:, pl.ds(pl.multiple_of(klass * half, LANES), half)] = block
+
+
+def settle(results, outs, groups, queries_ref):
+    half = outs[0].shape[1] // 2
+    for klass, result in enumerate(results):
+        done = finished(result, None)
         for at in range(2):
-            queries_ref[klass, :, pl.ds(at * half, half)] = sources[at][pl.ds(0, HEAD_DIM), pl.ds(klass * half, half)]
-        result = plain(keys_ref[...], queries_ref[klass], values_ref[klass])
-        done = finished(result, None)
-        totals.append(result[HEAD_DIM : HEAD_DIM + 1])
-        for at, out in enumerate(outs):
-            out[:, pl.ds(klass * half, half)] = done[:, at * half : (at + 1) * half]
-
-    @pl.when(jnp.logical_not(in_range(totals)))
+            store(outs, klass, at, done[:, at * half : (at + 1) * half])
+
+    @pl.when(jnp.logical_not(in_range([result[HEAD_DIM : HEAD_DIM + 1] for result in results])))
     def again():
         @pl.loop(0, 2)
         def one_class(klass):
-            for at, out in enumerate(outs):
-                result, top = shifted(keys_ref[...], queries_ref[klass, :, pl.ds(at * half, half)], values_ref[klass])
-                out[:, pl.ds(pl.multiple_of(klass * half, LANES), half)] = finished(result, top)
-
-
-def merge_kernel(steps, near_ref, *refs):
+            for at in range(2):
+                blocks = [(keys[...], values[klass]) for keys, values in groups()]
+                store(outs, klass, at, finished(*shifted(blocks, queries_ref[klass, :, pl.ds(at * half, half)])))
+
+
+def cross_kernel(m2, m3, m0, m1, near_keys, o2, o3, far_keys, queries_ref, near_values, far_values):
+    fill((m2, m3), far_keys, queries_ref, far_values)
+    fill((m0, m1), None, None, near_values)
+    groups = ((near_keys, near_values), (far_keys, far_values))
+    results = [
+        functools.reduce(jnp.add, [plain(keys[...], queries_ref[klass], values[klass]) for keys, values in groups])
+        for klass in range(2)
+    ]
+    settle(results, (o2, o3), lambda: groups, queries_ref)
+
+
+def late_kernel(m0, m1, m2, m3, near_keys, far_keys, part_ref, o0, o1, queries_ref, near_values, far_values):
+    fill((m0, m1), None, queries_ref, None)
+    fill((m2, m3), None, None, far_values)
+    results = [part_ref[klass] + plain(far_keys[...], queries_ref[klass], far_values[klass]) for klass in range(2)]
+
+    def groups():
+        fill((m0, m1), None, None, near_values)
+        return ((near_keys, near_values), (far_keys, far_values))
+
+    settle(results, (o0, o1), groups, queries_ref)
+
+
+def merge_kernel(steps, low_ref, high_ref, *refs):
     results = refs[: len(steps)]
     out_hbm, rows_ref, sent = refs[-3:]
-    rows = near_ref.shape[2]
+    each, _, rows = low_ref.shape
     half = rows // STRIDES
     me = lax.axis_index("seq")
     position = lax.broadcasted_iota(jnp.int32, (1, SPAN), 1)
@@ -388,9 +428,11 @@
             lanes = pl.ds(block * SPAN, SPAN)
             piece = [result[:, pl.ds(klass * half + block * LANES, LANES)] for klass in range(2)]
             there = dot_nn(jnp.concatenate(piece, axis=1), place)
-            near = near_ref[head, pl.ds(0, HEAD_DIM), lanes]
-            total = near_ref[head, pl.ds(HEAD_DIM, 1), lanes]
-            top = near_ref[head, pl.ds(HEAD_DIM + 1, 1), lanes]
+            in_low = low_ref[jnp.minimum(head, each - 1), :, lanes]
+            level = jnp.where(head < each, in_low, high_ref[jnp.maximum(head - each, 0), :, lanes])
+            near = level[:HEAD_DIM]
+            total = level[HEAD_DIM : HEAD_DIM + 1]
+            top = level[HEAD_DIM + 1 : HEAD_DIM + 2]
             lse = there[HEAD_DIM : HEAD_DIM + 1] + there[HEAD_DIM + 1 : HEAD_DIM + 2] + there[HEAD_DIM + 2 : HEAD_DIM + 3]
             near_lse = top + jnp.log2(total)
             peak = jnp.where(used, jnp.maximum(near_lse, lse), near_lse)
@@ -425,34 +467,27 @@
         pltpu.HBM,
     )
     n2, n3 = exchanged(m2, 2), exchanged(m3, 3)
-    arrived = (n3, n2, exchanged(m1, 1), m0)
-    near = call(
-        near_kernel,
-        jax.ShapeDtypeStruct((heads, HEAD_DIM + TAIL, rows), f32),
-        here,
-        [pltpu.VMEM((heads, rows, HEAD_DIM), bf16)],
-        4 * heads * rows * rows * 256,
-    )
-    def far(messages):
+
+    def near(first, some):
         return call(
-            far_kernel,
-            [jax.ShapeDtypeStruct((HEAD_DIM + TAIL, count), bf16)] * 2,
-            messages,
-            [
-                pltpu.VMEM((heads * count, HEAD_DIM), bf16),
-                pltpu.VMEM((2, HEAD_DIM, count), bf16),
-                pltpu.VMEM((2, HEAD_DIM + 2 * TAIL, heads * count), bf16),
-            ],
-            2 * heads * rows * rows * 256,
+            functools.partial(near_kernel, first),
+            jax.ShapeDtypeStruct((some, HEAD_DIM + TAIL, rows), f32),
+            here,
+            [pltpu.VMEM((some, rows, HEAD_DIM), bf16)],
+            4 * some * rows * rows * 256,
         )
 
+    low = near(0, LOW_HEADS)
+    low, m1, *here = lax.optimization_barrier((low, m1, *here))
+    n1 = exchanged(m1, 1)
+    high = near(LOW_HEADS, heads - LOW_HEADS)
     def merged(steps, results, begun):
         vmem, hbm = pl.BlockSpec(memory_space=pltpu.VMEM), pl.BlockSpec(memory_space=pl.ANY)
-        args = (near, *results, *begun)
+        args = (low, high, *results, *begun)
         return pl.pallas_call(
             functools.partial(merge_kernel, steps),
             out_shape=jax.ShapeDtypeStruct((width, rows), bf16),
-            in_specs=[vmem] * (1 + len(results)) + [hbm] * len(begun),
+            in_specs=[vmem] * (2 + len(results)) + [hbm] * len(begun),
             out_specs=hbm,
             scratch_shapes=[pltpu.VMEM((len(steps), HEAD_DIM, rows), bf16), pltpu.SemaphoreType.DMA((len(steps),))],
             input_output_aliases={len(args) - 1: 0} if begun else {},
@@ -460,11 +495,26 @@
             cost_estimate=pl.CostEstimate(flops=len(steps) << 29, bytes_accessed=len(steps) << 20, transcendentals=0),
         )(*args)
 
-    m3, m2, m1, m0, near = lax.optimization_barrier((*arrived, near))
-    f2, f3 = far((m2, m3, m0, m1))
-    f2, f3, m0, m1, m2, m3 = lax.optimization_barrier((f2, f3, m0, m1, m2, m3))
+    result = [jax.ShapeDtypeStruct((HEAD_DIM + TAIL, count), bf16)] * 2
+    pair_keys = jax.ShapeDtypeStruct((2 * count, HEAD_DIM), bf16)
+    queries = pltpu.VMEM((2, HEAD_DIM, count), bf16)
+    values = pltpu.VMEM((2, HEAD_DIM + 2 * TAIL, 2 * count), bf16)
+    work = 2 * heads * rows * rows * 256
+    n1, high = lax.optimization_barrier((n1, high))
+    near_keys, part = call(
+        early_kernel,
+        [pair_keys, jax.ShapeDtypeStruct((2, HEAD_DIM + 2 * TAIL, count), f32)],
+        (m0, n1),
+        [queries, values],
+        work // 2,
+    )
+    n3, n2, near_keys, part = lax.optimization_barrier((n3, n2, near_keys, part))
+    f2, f3, far_keys = call(
+        cross_kernel, [*result, pair_keys], (n2, n3, m0, n1, near_keys), [queries, values, values], work
+    )
+    f2, f3, m0, n1 = lax.optimization_barrier((f2, f3, m0, n1))
     g2, g3 = exchanged(f2, 2), exchanged(f3, 3)
-    g0, f1 = far((m0, m1, m2, m3))
+    g0, f1 = call(late_kernel, result, (m0, n1, n2, n3, near_keys, far_keys, part), [queries, values, values], work // 2)
     g1 = exchanged(f1, 1)
     own = merged((0,), (g0,), ())
     most = merged((2, 3), (g2, g3), (own,))

time: 42.9 us -> 39.8 us (0.928)
  Pallas kernels: 26.5 us -> 24.8 us
  waiting for transfers between devices: 6.6 us -> 5.14 us
    pallas_call x4 -> x6, Pallas kernels: 23.3 us -> 21.6 us  [call(): pl.pallas_call(kernel, out_shape=outs, in_specs=[pl.BlockSpec(memory_spac...]
    ppermute x6, waiting for transfers between devices: 6.6 us -> 5.14 us  [exchanged(): lax.ppermute(block, 'seq', [(i, i ^ step) for i in range(lax.axis_size('s...]
  transfers between devices with their start and end apart: 6 -> 6, of which waited for: 2 -> 3; matrix products, arithmetic and copies ran while one was open for 0% -> 0% of each run, Pallas kernels for 37% -> 39%
where the time goes in v7:
time: 39.8 us; the launch traced here: 39.6 us
  Pallas kernels  24.8 us (62%)
  starting transfers between devices  9.46 us (24%)
  waiting for transfers between devices  5.14 us (13%)
    pallas_call x6, Pallas kernels, call(): pl.pallas_call(kernel, out_shape=outs, in_specs=[pl.BlockSpec(memory_spac...  21.6 us
    ppermute x6, starting transfers between devices, exchanged(): lax.ppermute(block, 'seq', [(i, i ^ step) for i in range(lax.axis_size('s...  9.46 us
    ppermute x6, waiting for transfers between devices, exchanged(): lax.ppermute(block, 'seq', [(i, i ^ step) for i in range(lax.axis_size('s...  5.14 us
    pallas_call x3, Pallas kernels, merged(): pl.pallas_call(functools.partial(merge_kernel, steps), out_shape=jax.Shap...  3.2 us
  transfers between devices with their start and end apart: 6, of which 3 were waited for; matrix products, arithmetic and copies ran while one was open for 0% of the time, Pallas kernels for 39%

profile of v7, /device:TPU:0, one launch (start us, length us, event | category | flops | bytes accessed | tf_op | source)
XLA Modules:
  0.0 39.6 jit_solution(8860371949869461207)
XLA Ops:
  0.0 1.8 %shard_map.37 = (bf16[192,1024]{1,0:T(8,128)(2,1)S(1)}, bf16[192,1024]{1,0:T(8,128)(2,1)S(1)}, bf16[192,1024]{1,0:T(8,128)(2,1)S(1)}, bf16[144,512]{1,0:T(8,128)...) custom-call(bf16[192,1024]{1,0:T(8,128)(2,1)} %bitcast.4, ...), custom_call_target="tpu_custom_call" | custom-call | flops 268435456 | bytes 2097152 | tf_op jit(solution)/shard_map/pallas_call | solution.py:216
  1.8 5.1 %collective-permute-start.1 = (bf16[144,512]{1,0:T(8,128)(2,1)S(1)}, bf16[144,512]{1,0:T(8,128)(2,1)S(1)}, u32[]{:S(2)}, u32[]{:S(2)}) collective-permute-start(bf16[144,512]{1,0:T(8,128)(2,1)S(1)} %get-tuple-element.44), channel_id=1, source_target_pairs={{0,12},{4,8},{8,4},{12,0},{1,13},{5,9},{9,5},{13,1},{2,14},{6,10},... | collective-permute-start | bytes 442376 | tf_op jit(solution)/shard_map/ppermute | solution.py:452
  6.9 0.0 collective-permute-start.2
  6.9 1.9 %shard_map.38.low_ref = f32[1,56,1024]{2,1,0:T(8,128)S(1)} custom-call(bf16[192,1024]{1,0:T(8,128)(2,1)S(1)} %get-tuple-element.40.qt_ref, bf16[192,1024]{1,0:T(8,128)(2,1)S(1)} %get-tuple-element.41.kt_ref, bf16[192,1024]{1,0:T(8,128)(2,1)S(1)} %get-tuple-element.42.vt_ref), custom_call_target="tpu_custom_call" | custom-call | flops 1073741824 | bytes 2097152 | tf_op jit(solution)/shard_map/pallas_call | solution.py:216
  8.8 0.7 %collective-permute-start = (bf16[144,512]{1,0:T(8,128)(2,1)S(1)}, bf16[144,512]{1,0:T(8,128)(2,1)S(1)}, u32[]{:S(2)}, u32[]{:S(2)}) collective-permute-start(bf16[144,512]{1,0:T(8,128)(2,1)S(1)} %get-tuple-element.39), channel_id=1, source_target_pairs={{0,4},{4,0},{8,12},{12,8},{1,5},{5,1},{9,13},{13,9},{2,6},{6,2},{1... | collective-permute-start | bytes 442376 | tf_op jit(solution)/shard_map/ppermute | solution.py:452
  9.5 5.0 %shard_map.39.high_ref = f32[3,56,1024]{2,1,0:T(8,128)S(1)} custom-call(bf16[192,1024]{1,0:T(8,128)(2,1)S(1)} %get-tuple-element.40.qt_ref, bf16[192,1024]{1,0:T(8,128)(2,1)S(1)} %get-tuple-element.41.kt_ref, bf16[192,1024]{1,0:T(8,128)(2,1)S(1)} %get-tuple-element.42.vt_ref), custom_call_target="tpu_custom_call" | custom-call | flops 3221225472 | bytes 2097152 | tf_op jit(solution)/shard_map/pallas_call | solution.py:216
  14.6 1.8 %collective-permute-done.m1 = bf16[144,512]{1,0:T(8,128)(2,1)S(1)} collective-permute-done((bf16[144,512]{1,0:T(8,128)(2,1)S(1)}, bf16[144,512]{1,0:T(8,128)(2,1)S(1)}, u32[]{:S(2)}, u32[]{:S(2)}) %collective-permute-start) | collective-permute-done | bytes 147488 | tf_op jit(solution)/shard_map/ppermute | solution.py:452
  16.4 1.2 %shard_map.40 = (bf16[1024,48]{1,0:T(8,128)(2,1)S(1)}, f32[2,64,512]{2,1,0:T(8,128)S(1)}) custom-call(bf16[144,512]{1,0:T(8,128)(2,1)S(1)} %get-tuple-element.55.m0, bf16[144,512]{1,0:T(8,128)(2,1)S(1)} %collective-permute-done.m1), custom_call_target="tpu_custom_call" | custom-call | flops 1073741824 | bytes 2097152 | tf_op jit(solution)/shard_map/pallas_call | solution.py:216
  17.6 0.0 collective-permute-done.1.m3
  17.6 1.8 %collective-permute-done.2.m2 = bf16[144,512]{1,0:T(8,128)(2,1)S(1)} collective-permute-done((bf16[144,512]{1,0:T(8,128)(2,1)S(1)}, bf16[144,512]{1,0:T(8,128)(2,1)S(1)}, u32[]{:S(2)}, u32[]{:S(2)}) %collective-permute-start.2) | collective-permute-done | bytes 147488 | tf_op jit(solution)/shard_map/ppermute | solution.py:452
  19.4 6.5 %shard_map.41 = (bf16[56,512]{1,0:T(8,128)(2,1)S(1)}, bf16[56,512]{1,0:T(8,128)(2,1)S(1)}, bf16[1024,48]{1,0:T(8,128)(2,1)S(1)}) custom-call(bf16[144,512]{1,0:T(8,128)(2,1)S(1)} %collective-permute-done.2.m2, bf16[144,512]{1,0:T(8,128)(2,1)S(1)} %collective-permute-done.1.m3, bf16[144,512]{1,0:T(8,128)(2,1)S(1)} %get-tuple-element.55.m0, ...), custom_call_target="tpu_custom_call" | custom-call | flops 2147483648 | bytes 2097152 | tf_op jit(solution)/shard_map/pallas_call | solution.py:216
  25.9 0.1 collective-permute-start.4
  26.0 3.0 %collective-permute-start.5 = (bf16[56,512]{1,0:T(8,128)(2,1)S(1)}, bf16[56,512]{1,0:T(8,128)(2,1)S(1)}, u32[]{:S(2)}, u32[]{:S(2)}) collective-permute-start(bf16[56,512]{1,0:T(8,128)(2,1)S(1)} %get-tuple-element.61), channel_id=1, source_target_pairs={{0,12},{4,8},{8,4},{12,0},{1,13},{5,9},{9,5},{13,1},{2,14},{6,10},... | collective-permute-start | bytes 172040 | tf_op jit(solution)/shard_map/ppermute | solution.py:452
  29.0 5.2 %shard_map.42 = (bf16[56,512]{1,0:T(8,128)(2,1)S(1)}, bf16[56,512]{1,0:T(8,128)(2,1)S(1)}) custom-call(bf16[144,512]{1,0:T(8,128)(2,1)S(1)} %get-tuple-element.55.m0, bf16[144,512]{1,0:T(8,128)(2,1)S(1)} %collective-permute-done.m1, bf16[144,512]{1,0:T(8,128)(2,1)S(1)} %collective-permute-done.2.m2, bf16[144,512]{1,0:T(8,128)(2,1)S(1)} %collective-permute-done.1.m3, ...), custom_call_target="tpu_custom_call" | custom-call | flops 1073741824 | bytes 2097152 | tf_op jit(solution)/shard_map/pallas_call | solution.py:216
  34.2 0.5 %collective-permute-start.3 = (bf16[56,512]{1,0:T(8,128)(2,1)S(1)}, bf16[56,512]{1,0:T(8,128)(2,1)S(1)}, u32[]{:S(2)}, u32[]{:S(2)}) collective-permute-start(bf16[56,512]{1,0:T(8,128)(2,1)S(1)} %get-tuple-element.59), channel_id=1, source_target_pairs={{0,4},{4,0},{8,12},{12,8},{1,5},{5,1},{9,13},{13,9},{2,6},{6,2},{1... | collective-permute-start | bytes 172040 | tf_op jit(solution)/shard_map/ppermute | solution.py:452
  34.7 1.0 %shard_map.43.refs_2_ = bf16[192,1024]{1,0:T(8,128)(2,1)} custom-call(f32[1,56,1024]{2,1,0:T(8,128)S(1)} %shard_map.38.low_ref, f32[3,56,1024]{2,1,0:T(8,128)S(1)} %shard_map.39.high_ref, bf16[56,512]{1,0:T(8,128)(2,1)S(1)} %get-tuple-element.62.refs_0_), custom_call_target="tpu_custom_call" | custom-call | flops 536870912 | bytes 1048576 | tf_op jit(solution)/shard_map/pallas_call | solution.py:487
  35.8 0.0 collective-permute-done.4.refs_0_
  35.8 0.0 collective-permute-done.5.refs_1_
  35.8 1.2 %shard_map.44.refs_1_ = bf16[192,1024]{1,0:T(8,128)(2,1)} custom-call(f32[1,56,1024]{2,1,0:T(8,128)S(1)} %shard_map.38.low_ref, f32[3,56,1024]{2,1,0:T(8,128)S(1)} %shard_map.39.high_ref, bf16[56,512]{1,0:T(8,128)(2,1)S(1)} %collective-permute-done.4.refs_0_, bf16[56,512]{1,0:T(8,128)(2,1)S(1)} %collective-permute-done.5.refs_1_, ...), custom_call_target="tpu_custom_call", output_to_operand_aliasing={{}: (4, {})} | custom-call | flops 1073741824 | bytes 2097152 | tf_op jit(solution)/shard_map/pallas_call | solution.py:487
  37.0 1.5 %collective-permute-done.3.refs_0_ = bf16[56,512]{1,0:T(8,128)(2,1)S(1)} collective-permute-done((bf16[56,512]{1,0:T(8,128)(2,1)S(1)}, bf16[56,512]{1,0:T(8,128)(2,1)S(1)}, u32[]{:S(2)}, u32[]{:S(2)}) %collective-permute-start.3) | collective-permute-done | bytes 57376 | tf_op jit(solution)/shard_map/ppermute | solution.py:452
  38.5 1.0 %shard_map.45 = bf16[192,1024]{1,0:T(8,128)(2,1)} custom-call(f32[1,56,1024]{2,1,0:T(8,128)S(1)} %shard_map.38.low_ref, f32[3,56,1024]{2,1,0:T(8,128)S(1)} %shard_map.39.high_ref, bf16[56,512]{1,0:T(8,128)(2,1)S(1)} %collective-permute-done.3.refs_0_, bf16[192,1024]{1,0:T(8,128)(2,1)} %shard_map.44.refs_1_), custom_call_target="tpu_custom_call", output_to_operand_aliasing={{}: (3, {})} | custom-call | flops 536870912 | bytes 1048576 | tf_op jit(solution)/shard_map/pallas_call | solution.py:487
Async XLA Ops:
  1.8 15.8 %collective-permute-start.1 = (bf16[144,512]{1,0:T(8,128)(2,1)S(1)}, bf16[144,512]{1,0:T(8,128)(2,1)S(1)}, u32[]{:S(2)}, u32[]{:S(2)}) collective-permute-start(bf16[144,512]{1,0:T(8,128)(2,1)S(1)} %get-tuple-element.44), channel_id=1, source_target_pairs={{0,12},{4,8},{8,4},{12,0},{1,13},{5,9},{9,5},{13,1},{2,14},{6,10},... | collective-permute-start | bytes 442376 | tf_op jit(solution)/shard_map/ppermute | solution.py:452
  6.9 12.5 %collective-permute-start.2 = (bf16[144,512]{1,0:T(8,128)(2,1)S(1)}, bf16[144,512]{1,0:T(8,128)(2,1)S(1)}, u32[]{:S(2)}, u32[]{:S(2)}) collective-permute-start(bf16[144,512]{1,0:T(8,128)(2,1)S(1)} %get-tuple-element.45), channel_id=1, source_target_pairs={{0,8},{4,12},{8,0},{12,4},{1,9},{5,13},{9,1},{13,5},{2,10},{6,14},... | collective-permute-start | bytes 442376 | tf_op jit(solution)/shard_map/ppermute | solution.py:452
  8.8 7.6 %collective-permute-start = (bf16[144,512]{1,0:T(8,128)(2,1)S(1)}, bf16[144,512]{1,0:T(8,128)(2,1)S(1)}, u32[]{:S(2)}, u32[]{:S(2)}) collective-permute-start(bf16[144,512]{1,0:T(8,128)(2,1)S(1)} %get-tuple-element.39), channel_id=1, source_target_pairs={{0,4},{4,0},{8,12},{12,8},{1,5},{5,1},{9,13},{13,9},{2,6},{6,2},{1... | collective-permute-start | bytes 442376 | tf_op jit(solution)/shard_map/ppermute | solution.py:452
  25.9 9.9 %collective-permute-start.4 = (bf16[56,512]{1,0:T(8,128)(2,1)S(1)}, bf16[56,512]{1,0:T(8,128)(2,1)S(1)}, u32[]{:S(2)}, u32[]{:S(2)}) collective-permute-start(bf16[56,512]{1,0:T(8,128)(2,1)S(1)} %get-tuple-element.60), channel_id=1, source_target_pairs={{0,8},{4,12},{8,0},{12,4},{1,9},{5,13},{9,1},{13,5},{2,10},{6,14},... | collective-permute-start | bytes 172040 | tf_op jit(solution)/shard_map/ppermute | solution.py:452
  26.0 9.8 %collective-permute-start.5 = (bf16[56,512]{1,0:T(8,128)(2,1)S(1)}, bf16[56,512]{1,0:T(8,128)(2,1)S(1)}, u32[]{:S(2)}, u32[]{:S(2)}) collective-permute-start(bf16[56,512]{1,0:T(8,128)(2,1)S(1)} %get-tuple-element.61), channel_id=1, source_target_pairs={{0,12},{4,8},{8,4},{12,0},{1,13},{5,9},{9,5},{13,1},{2,14},{6,10},... | collective-permute-start | bytes 172040 | tf_op jit(solution)/shard_map/ppermute | solution.py:452
  34.2 4.2 %collective-permute-start.3 = (bf16[56,512]{1,0:T(8,128)(2,1)S(1)}, bf16[56,512]{1,0:T(8,128)(2,1)S(1)}, u32[]{:S(2)}, u32[]{:S(2)}) collective-permute-start(bf16[56,512]{1,0:T(8,128)(2,1)S(1)} %get-tuple-element.59), channel_id=1, source_target_pairs={{0,4},{4,0},{8,12},{12,8},{1,5},{5,1},{9,13},{13,9},{2,6},{6,2},{1... | collective-permute-start | bytes 172040 | tf_op jit(solution)/shard_map/ppermute | solution.py:452

commit v8 on v7

--- a/solution.py
+++ b/solution.py
@@ -226,21 +226,29 @@
 
 def pack_kernel(q_hbm, k_hbm, v_hbm, q_ref, k_ref, v_ref, m2, m3, m1, m0, by_head, arrivals):
     width, rows = q_ref.shape
+    blocks = range(rows // SPAN)
     copies = [
-        pltpu.make_async_copy(source, target, arrivals.at[at])
-        for at, (source, target) in enumerate(((q_hbm, q_ref), (k_hbm, k_ref), (v_hbm, v_ref)))
+        [
+            pltpu.make_async_copy(
+                source.at[:, pl.ds(block * SPAN, SPAN)], target.at[:, pl.ds(block * SPAN, SPAN)], arrivals.at[block, at]
+            )
+            for at, (source, target) in enumerate(((q_hbm, q_ref), (k_hbm, k_ref), (v_hbm, v_ref)))
+        ]
+        for block in blocks
     ]
-    for copy in copies:
-        copy.start()
-    for copy in copies:
-        copy.wait()
+    for block in blocks:
+        for copy in copies[block]:
+            copy.start()
     heads = width // HEAD_DIM
-    for parity in range(2):
-        pick = one_hot(
-            (SPAN, 2 * LANES), lambda row, column: row == column % LANES * STRIDES + column // LANES * 2 + parity
-        )
-        mine = range(parity, heads, 2)
-        for block in range(rows // SPAN):
+    picks = [
+        one_hot((SPAN, 2 * LANES), lambda row, column: row == column % LANES * STRIDES + column // LANES * 2 + parity)
+        for parity in range(2)
+    ]
+    for block in blocks:
+        for copy in copies[block]:
+            copy.wait()
+        for parity, pick in enumerate(picks):
+            mine = range(parity, heads, 2)
             pieces = [
                 ref[pl.ds(head * HEAD_DIM, HEAD_DIM), pl.ds(block * SPAN, SPAN)]
                 for head in mine
@@ -273,16 +281,31 @@
     return jnp.concatenate(pieces, axis=0).astype(jnp.bfloat16)
 
 
-def plain(keys, queries, values):
-    return dot_nn(values, jnp.exp2(dot_nn(keys, queries) * FACTOR).astype(jnp.bfloat16))
-
-
-def shifted(groups, queries):
-    scores = [dot_nn(keys, queries) for keys, _ in groups]
+def doubled(scores, shift):
+    half = scores.shape[0] // 2
+    one = jnp.where(lax.broadcasted_iota(jnp.int32, (1, scores.shape[1]), 1) < half, 1.0, 0.0)
+    first = jnp.exp2(scores[:half] * FACTOR + (one - shift))
+    second = jnp.exp2(scores[half:] * FACTOR - shift)
+    return jnp.concatenate([first.astype(jnp.bfloat16), second.astype(jnp.bfloat16)], axis=0)
+
+
+def plain(*jobs):
+    steps = [(at, queries, keys, values) for at, (queries, groups) in enumerate(jobs) for keys, values in groups]
+    results = [None] * len(jobs)
+    ahead = dot_nn(steps[0][2][...], steps[0][1])
+    for now, (at, _, _, values) in enumerate(steps):
+        scores = ahead
+        if now + 1 < len(steps):
+            ahead = dot_nn(steps[now + 1][2][...], steps[now + 1][1])
+        term = dot_nn(values, doubled(scores, 0.0))
+        results[at] = term if results[at] is None else results[at] + term
+    return results
+
+
+def shifted(queries, groups):
+    scores = [dot_nn(keys[...], queries) for keys, _ in groups]
     top = functools.reduce(jnp.maximum, [jnp.max(block, axis=0, keepdims=True) for block in scores]) * FACTOR
-    terms = [
-        dot_nn(values, jnp.exp2(block * FACTOR - top).astype(jnp.bfloat16)) for block, (_, values) in zip(scores, groups)
-    ]
+    terms = [dot_nn(values, doubled(block, top)) for block, (_, values) in zip(scores, groups)]
     return functools.reduce(jnp.add, terms), top
 
 
@@ -343,80 +366,62 @@
     return jnp.concatenate([result[:HEAD_DIM] / total, parts], axis=0).astype(jnp.bfloat16)
 
 
-def fill(messages, keys_ref, queries_ref, values_ref):
-    count = messages[0].shape[1]
-    half = count // 2
-    twice = jnp.where(lax.broadcasted_iota(jnp.int32, (1, count), 1) < half, 2.0, 1.0).astype(jnp.bfloat16)
-    for at, message in enumerate(messages):
-        if keys_ref is not None:
-            keys_ref[pl.ds(at * count, count), :] = upright(message[pl.ds(HEAD_DIM, HEAD_DIM), :])
-        if values_ref is not None:
-            values = with_ones(message[pl.ds(2 * HEAD_DIM, HEAD_DIM), :])
-            values_ref[0, :, pl.ds(at * count, count)] = values * twice
-            values_ref[1, :, pl.ds(at * count, count)] = values
-        if queries_ref is not None:
-            for klass in range(2):
-                queries_ref[klass, :, pl.ds(at * half, half)] = message[pl.ds(0, HEAD_DIM), pl.ds(klass * half, half)]
-
-
-def early_kernel(m0, m1, keys_ref, part_ref, queries_ref, values_ref):
-    fill((m0, m1), keys_ref, queries_ref, values_ref)
-    for klass in range(2):
-        part_ref[klass] = plain(keys_ref[...], queries_ref[klass], values_ref[klass])
-
-
-def store(outs, klass, at, block):
-    half = block.shape[1]
-    outs[at][:, pl.ds(pl.multiple_of(klass * half, LANES), half)] = block
-
-
-def settle(results, outs, groups, queries_ref):
-    half = outs[0].shape[1] // 2
-    for klass, result in enumerate(results):
-        done = finished(result, None)
-        for at in range(2):
-            store(outs, klass, at, done[:, at * half : (at + 1) * half])
+def make_keys(keys_ref, message):
+    keys_ref[...] = upright(message[pl.ds(HEAD_DIM, HEAD_DIM), :])
+
+
+def values_of(message):
+    return with_ones(message[pl.ds(2 * HEAD_DIM, HEAD_DIM), :])
+
+
+def queries_of(message):
+    return message[pl.ds(0, HEAD_DIM), :]
+
+
+def settle(results, outs, messages, every):
+    for result, out in zip(results, outs):
+        out[...] = finished(result, None)
 
     @pl.when(jnp.logical_not(in_range([result[HEAD_DIM : HEAD_DIM + 1] for result in results])))
     def again():
-        @pl.loop(0, 2)
-        def one_class(klass):
-            for at in range(2):
-                blocks = [(keys[...], values[klass]) for keys, values in groups()]
-                store(outs, klass, at, finished(*shifted(blocks, queries_ref[klass, :, pl.ds(at * half, half)])))
-
-
-def cross_kernel(m2, m3, m0, m1, near_keys, o2, o3, far_keys, queries_ref, near_values, far_values):
-    fill((m2, m3), far_keys, queries_ref, far_values)
-    fill((m0, m1), None, None, near_values)
-    groups = ((near_keys, near_values), (far_keys, far_values))
-    results = [
-        functools.reduce(jnp.add, [plain(keys[...], queries_ref[klass], values[klass]) for keys, values in groups])
-        for klass in range(2)
-    ]
-    settle(results, (o2, o3), lambda: groups, queries_ref)
-
-
-def late_kernel(m0, m1, m2, m3, near_keys, far_keys, part_ref, o0, o1, queries_ref, near_values, far_values):
-    fill((m0, m1), None, queries_ref, None)
-    fill((m2, m3), None, None, far_values)
-    results = [part_ref[klass] + plain(far_keys[...], queries_ref[klass], far_values[klass]) for klass in range(2)]
-
-    def groups():
-        fill((m0, m1), None, None, near_values)
-        return ((near_keys, near_values), (far_keys, far_values))
-
-    settle(results, (o0, o1), groups, queries_ref)
+        for message, out in zip(messages, outs):
+            out[...] = finished(*shifted(queries_of(message), every()))
+
+
+def early_kernel(m0, ma, keys0, keysa, part0, parta):
+    make_keys(keys0, m0)
+    make_keys(keysa, ma)
+    groups = ((keys0, values_of(m0)), (keysa, values_of(ma)))
+    part0[...], parta[...] = plain((queries_of(m0), groups), (queries_of(ma), groups))
+
+
+def cross_kernel(m0, m1, m2, m3, keys0, keys3, part3, f2, f3, keys1, keys2):
+    make_keys(keys1, m1)
+    make_keys(keys2, m2)
+    groups = [(keys, values_of(message)) for keys, message in ((keys0, m0), (keys1, m1), (keys2, m2), (keys3, m3))]
+    whole, rest = plain((queries_of(m2), groups), (queries_of(m3), groups[1:3]))
+    settle((whole, part3[...] + rest), (f2, f3), (m2, m3), lambda: groups)
+
+
+def next_kernel(m0, m1, m2, m3, keys0, keys1, keys2, keys3, f1):
+    groups = [(keys, values_of(message)) for keys, message in ((keys0, m0), (keys1, m1), (keys2, m2), (keys3, m3))]
+    (whole,) = plain((queries_of(m1), groups))
+    settle((whole,), (f1,), (m1,), lambda: groups)
+
+
+def own_kernel(m0, m1, m2, m3, keys0, keys1, keys2, keys3, part0, low_ref, high_ref, rows_ref, f0):
+    groups = [(keys, values_of(message)) for keys, message in ((keys0, m0), (keys1, m1), (keys2, m2), (keys3, m3))]
+    (rest,) = plain((queries_of(m0), groups[1:3]))
+    settle((part0[...] + rest,), (f0,), (m0,), lambda: groups)
+    merge_kernel((0,), low_ref, high_ref, f0, rows_ref)
 
 
 def merge_kernel(steps, low_ref, high_ref, *refs):
-    results = refs[: len(steps)]
-    out_hbm, rows_ref, sent = refs[-3:]
+    *results, rows_ref = refs
     each, _, rows = low_ref.shape
     half = rows // STRIDES
     me = lax.axis_index("seq")
     position = lax.broadcasted_iota(jnp.int32, (1, SPAN), 1)
-    copies = []
     for at, (step, result) in enumerate(zip(steps, results)):
         head = jnp.bitwise_xor(me, step)
         place = one_hot(
@@ -441,9 +446,22 @@
             share = 1.0 / (total * weight + far)
             merged = near * (weight * share) + there[:HEAD_DIM] * (far * share)
             rows_ref[at, :, lanes] = merged.astype(jnp.bfloat16)
+
+
+def last_kernel(low_ref, high_ref, own_ref, far_ref, result, out_hbm, rows_ref, sent):
+    me = lax.axis_index("seq")
+
+    def sending(step, rows):
+        head = jnp.bitwise_xor(me, step)
         features = pl.ds(pl.multiple_of(head * HEAD_DIM, HEAD_DIM), HEAD_DIM)
-        copies.append(pltpu.make_async_copy(rows_ref.at[at], out_hbm.at[features], sent.at[at]))
-        copies[-1].start()
+        return pltpu.make_async_copy(rows, out_hbm.at[features], sent.at[step])
+
+    copies = [sending(0, own_ref.at[0]), sending(2, far_ref.at[0]), sending(3, far_ref.at[1])]
+    for copy in copies:
+        copy.start()
+    merge_kernel((1,), low_ref, high_ref, result, rows_ref)
+    copies.append(sending(1, rows_ref.at[0]))
+    copies[-1].start()
     for copy in copies:
         copy.wait()
 
@@ -462,7 +480,7 @@
         pack_kernel,
         [jax.ShapeDtypeStruct((width, rows), bf16)] * 3 + [jax.ShapeDtypeStruct((3 * HEAD_DIM, count), bf16)] * heads,
         turned,
-        [pltpu.VMEM((heads, 3 * HEAD_DIM, count), bf16), pltpu.SemaphoreType.DMA((3,))],
+        [pltpu.VMEM((heads, 3 * HEAD_DIM, count), bf16), pltpu.SemaphoreType.DMA((rows // SPAN, 3))],
         1 << 28,
         pltpu.HBM,
     )
@@ -481,44 +499,43 @@
     low, m1, *here = lax.optimization_barrier((low, m1, *here))
     n1 = exchanged(m1, 1)
     high = near(LOW_HEADS, heads - LOW_HEADS)
-    def merged(steps, results, begun):
-        vmem, hbm = pl.BlockSpec(memory_space=pltpu.VMEM), pl.BlockSpec(memory_space=pl.ANY)
-        args = (low, high, *results, *begun)
-        return pl.pallas_call(
-            functools.partial(merge_kernel, steps),
-            out_shape=jax.ShapeDtypeStruct((width, rows), bf16),
-            in_specs=[vmem] * (2 + len(results)) + [hbm] * len(begun),
-            out_specs=hbm,
-            scratch_shapes=[pltpu.VMEM((len(steps), HEAD_DIM, rows), bf16), pltpu.SemaphoreType.DMA((len(steps),))],
-            input_output_aliases={len(args) - 1: 0} if begun else {},
-            compiler_params=pltpu.CompilerParams(vmem_limit_bytes=VMEM_BYTES),
-            cost_estimate=pl.CostEstimate(flops=len(steps) << 29, bytes_accessed=len(steps) << 20, transcendentals=0),
-        )(*args)
-
-    result = [jax.ShapeDtypeStruct((HEAD_DIM + TAIL, count), bf16)] * 2
-    pair_keys = jax.ShapeDtypeStruct((2 * count, HEAD_DIM), bf16)
-    queries = pltpu.VMEM((2, HEAD_DIM, count), bf16)
-    values = pltpu.VMEM((2, HEAD_DIM + 2 * TAIL, 2 * count), bf16)
-    work = 2 * heads * rows * rows * 256
-    n1, high = lax.optimization_barrier((n1, high))
-    near_keys, part = call(
-        early_kernel,
-        [pair_keys, jax.ShapeDtypeStruct((2, HEAD_DIM + 2 * TAIL, count), f32)],
-        (m0, n1),
-        [queries, values],
-        work // 2,
-    )
-    n3, n2, near_keys, part = lax.optimization_barrier((n3, n2, near_keys, part))
-    f2, f3, far_keys = call(
-        cross_kernel, [*result, pair_keys], (n2, n3, m0, n1, near_keys), [queries, values, values], work
-    )
-    f2, f3, m0, n1 = lax.optimization_barrier((f2, f3, m0, n1))
+    result = jax.ShapeDtypeStruct((HEAD_DIM + TAIL, count), bf16)
+    part = jax.ShapeDtypeStruct((HEAD_DIM + 2 * TAIL, count), f32)
+    keys = jax.ShapeDtypeStruct((count, HEAD_DIM), bf16)
+    work = 4 * count * count * 256
+    n3, high = lax.optimization_barrier((n3, high))
+    keys0, keys3, part0, part3 = call(early_kernel, [keys, keys, part, part], (m0, n3), [], 4 * work)
+    keys0, keys3, n1, n2 = lax.optimization_barrier((keys0, keys3, n1, n2))
+    f2, f3, keys1, keys2 = call(
+        cross_kernel, [result, result, keys, keys], (m0, n1, n2, n3, keys0, keys3, part3), [], 6 * work
+    )
+    f2, f3, keys2 = lax.optimization_barrier((f2, f3, keys2))
     g2, g3 = exchanged(f2, 2), exchanged(f3, 3)
-    g0, f1 = call(late_kernel, result, (m0, n1, n2, n3, near_keys, far_keys, part), [queries, values, values], work // 2)
+    every = (m0, n1, n2, n3, keys0, keys1, keys2, keys3)
+    f1 = call(next_kernel, result, every, [], 4 * work)
+    f1, part0 = lax.optimization_barrier((f1, part0))
     g1 = exchanged(f1, 1)
-    own = merged((0,), (g0,), ())
-    most = merged((2, 3), (g2, g3), (own,))
-    return merged((1,), (g1,), (most,)).T
+    own = call(
+        own_kernel,
+        jax.ShapeDtypeStruct((1, HEAD_DIM, rows), bf16),
+        (*every, part0, low, high),
+        [pltpu.VMEM((HEAD_DIM + TAIL, count), bf16)],
+        2 * work,
+    )
+    def merged(steps, results):
+        shape = jax.ShapeDtypeStruct((len(steps), HEAD_DIM, rows), bf16)
+        return call(functools.partial(merge_kernel, steps), shape, (low, high, *results), [], len(steps) << 29)
+
+    others = merged((2, 3), (g2, g3))
+    return pl.pallas_call(
+        last_kernel,
+        out_shape=jax.ShapeDtypeStruct((width, rows), bf16),
+        in_specs=[pl.BlockSpec(memory_space=pltpu.VMEM)] * 5,
+        out_specs=pl.BlockSpec(memory_space=pl.ANY),
+        scratch_shapes=[pltpu.VMEM((1, HEAD_DIM, rows), bf16), pltpu.SemaphoreType.DMA((heads,))],
+        compiler_params=pltpu.CompilerParams(vmem_limit_bytes=VMEM_BYTES),
+        cost_estimate=pl.CostEstimate(flops=1 << 29, bytes_accessed=1 << 20, transcendentals=0),
+    )(low, high, own, others, g1).T
 
 
 def per_device(query_rows, key_rows, value_rows):

time: 39.8 us -> 36.2 us (0.910)
  Pallas kernels: 24.8 us -> 22.7 us
  waiting for transfers between devices: 5.14 us -> 3.57 us
    pallas_call x3 -> x1, Pallas kernels: 3.2 us -> 1.03 us  [whole_slide(): pl.pallas_call(last_kernel, out_shape=jax.ShapeDtypeStruct((width, rows),...]
    ppermute x6, waiting for transfers between devices: 5.14 us -> 3.57 us  [exchanged(): lax.ppermute(block, 'seq', [(i, i ^ step) for i in range(lax.axis_size('s...]
    pallas_call x6 -> x8, Pallas kernels: 21.6 us -> 21.7 us  [call(): pl.pallas_call(kernel, out_shape=outs, in_specs=[pl.BlockSpec(memory_spac...]
  transfers between devices with their start and end apart: 6 -> 6, of which waited for: 3 -> 1; matrix products, arithmetic and copies ran while one was open for 0% -> 0% of each run, Pallas kernels for 39% -> 40%
where the time goes in v8:
time: 36.2 us; the launch traced here: 36 us
  Pallas kernels  22.7 us (63%)
  starting transfers between devices  9.48 us (26%)
  waiting for transfers between devices  3.57 us (10%)
    pallas_call x8, Pallas kernels, call(): pl.pallas_call(kernel, out_shape=outs, in_specs=[pl.BlockSpec(memory_spac...  21.7 us
    ppermute x6, starting transfers between devices, exchanged(): lax.ppermute(block, 'seq', [(i, i ^ step) for i in range(lax.axis_size('s...  9.48 us
    ppermute x6, waiting for transfers between devices, exchanged(): lax.ppermute(block, 'seq', [(i, i ^ step) for i in range(lax.axis_size('s...  3.57 us
    pallas_call x1, Pallas kernels, whole_slide(): pl.pallas_call(last_kernel, out_shape=jax.ShapeDtypeStruct((width, rows),...  1.03 us
  transfers between devices with their start and end apart: 6, of which 1 were waited for; matrix products, arithmetic and copies ran while one was open for 0% of the time, Pallas kernels for 40%

profile of v8, /device:TPU:0, one launch (start us, length us, event | category | flops | bytes accessed | tf_op | source)
XLA Modules:
  0.0 36.0 jit_solution(11025039640181777900)
XLA Ops:
  0.0 1.9 %shard_map.37 = (bf16[192,1024]{1,0:T(8,128)(2,1)S(1)}, bf16[192,1024]{1,0:T(8,128)(2,1)S(1)}, bf16[192,1024]{1,0:T(8,128)(2,1)S(1)}, bf16[144,512]{1,0:T(8,128)...) custom-call(bf16[192,1024]{1,0:T(8,128)(2,1)} %bitcast.4, ...), custom_call_target="tpu_custom_call" | custom-call | flops 268435456 | bytes 2097152 | tf_op jit(solution)/shard_map/pallas_call | solution.py:216
  1.9 5.1 %collective-permute-start = (bf16[144,512]{1,0:T(8,128)(2,1)S(1)}, bf16[144,512]{1,0:T(8,128)(2,1)S(1)}, u32[]{:S(2)}, u32[]{:S(2)}) collective-permute-start(bf16[144,512]{1,0:T(8,128)(2,1)S(1)} %get-tuple-element.41), channel_id=1, source_target_pairs={{0,12},{4,8},{8,4},{12,0},{1,13},{5,9},{9,5},{13,1},{2,14},{6,10},... | collective-permute-start | bytes 442376 | tf_op jit(solution)/shard_map/ppermute | solution.py:470
  7.0 0.0 collective-permute-start.2
  7.0 1.9 %shard_map.38.low_ref = f32[1,56,1024]{2,1,0:T(8,128)S(1)} custom-call(bf16[192,1024]{1,0:T(8,128)(2,1)S(1)} %get-tuple-element.42.qt_ref, bf16[192,1024]{1,0:T(8,128)(2,1)S(1)} %get-tuple-element.43.kt_ref, bf16[192,1024]{1,0:T(8,128)(2,1)S(1)} %get-tuple-element.44.vt_ref), custom_call_target="tpu_custom_call" | custom-call | flops 1073741824 | bytes 2097152 | tf_op jit(solution)/shard_map/pallas_call | solution.py:216
  8.9 0.7 %collective-permute-start.1 = (bf16[144,512]{1,0:T(8,128)(2,1)S(1)}, bf16[144,512]{1,0:T(8,128)(2,1)S(1)}, u32[]{:S(2)}, u32[]{:S(2)}) collective-permute-start(bf16[144,512]{1,0:T(8,128)(2,1)S(1)} %get-tuple-element.50), channel_id=1, source_target_pairs={{0,4},{4,0},{8,12},{12,8},{1,5},{5,1},{9,13},{13,9},{2,6},{6,2},{1... | collective-permute-start | bytes 442376 | tf_op jit(solution)/shard_map/ppermute | solution.py:470
  9.6 5.0 %shard_map.39.high_ref = f32[3,56,1024]{2,1,0:T(8,128)S(1)} custom-call(bf16[192,1024]{1,0:T(8,128)(2,1)S(1)} %get-tuple-element.42.qt_ref, bf16[192,1024]{1,0:T(8,128)(2,1)S(1)} %get-tuple-element.43.kt_ref, bf16[192,1024]{1,0:T(8,128)(2,1)S(1)} %get-tuple-element.44.vt_ref), custom_call_target="tpu_custom_call" | custom-call | flops 3221225472 | bytes 2097152 | tf_op jit(solution)/shard_map/pallas_call | solution.py:216
  14.7 0.0 collective-permute-done.ma.m3
  14.7 1.2 %shard_map.40 = (bf16[512,48]{1,0:T(8,128)(2,1)S(1)}, bf16[512,48]{1,0:T(8,128)(2,1)S(1)}, f32[64,512]{1,0:T(8,128)S(1)}, f32[64,512]{1,0:T(8,128)S(1)}) custom-call(bf16[144,512]{1,0:T(8,128)(2,1)S(1)} %get-tuple-element.46.m0, bf16[144,512]{1,0:T(8,128)(2,1)S(1)} %collective-permute-done.ma.m3), custom_call_target="tpu_custom_call" | custom-call | flops 1073741824 | bytes 2097152 | tf_op jit(solution)/shard_map/pallas_call | solution.py:216
  15.9 3.6 %collective-permute-done.2.m2 = bf16[144,512]{1,0:T(8,128)(2,1)S(1)} collective-permute-done((bf16[144,512]{1,0:T(8,128)(2,1)S(1)}, bf16[144,512]{1,0:T(8,128)(2,1)S(1)}, u32[]{:S(2)}, u32[]{:S(2)}) %collective-permute-start.2) | collective-permute-done | bytes 147488 | tf_op jit(solution)/shard_map/ppermute | solution.py:470
  19.5 0.0 collective-permute-done.1.m1
  19.5 5.4 %shard_map.41 = (bf16[56,512]{1,0:T(8,128)(2,1)S(1)}, bf16[56,512]{1,0:T(8,128)(2,1)S(1)}, bf16[512,48]{1,0:T(8,128)(2,1)S(1)}, bf16[512,48]{1,0:T(8,128)(2,1)S(1)}) custom-call(bf16[144,512]{1,0:T(8,128)(2,1)S(1)} %get-tuple-element.46.m0, bf16[144,512]{1,0:T(8,128)(2,1)S(1)} %collective-permute-done.1.m1, bf16[144,512]{1,0:T(8,128)(2,1)S(1)} %collective-permute-done.2.m2, ...), custom_call_target="tpu_custom_call" | custom-call | flops 1610612736 | bytes 2097152 | tf_op jit(solution)/shard_map/pallas_call | solution.py:216
  24.8 0.9 %collective-permute-start.3 = (bf16[56,512]{1,0:T(8,128)(2,1)S(1)}, bf16[56,512]{1,0:T(8,128)(2,1)S(1)}, u32[]{:S(2)}, u32[]{:S(2)}) collective-permute-start(bf16[56,512]{1,0:T(8,128)(2,1)S(1)} %get-tuple-element.64), channel_id=1, source_target_pairs={{0,8},{4,12},{8,0},{12,4},{1,9},{5,13},{9,1},{13,5},{2,10},{6,14},... | collective-permute-start | bytes 172040 | tf_op jit(solution)/shard_map/ppermute | solution.py:470
  25.7 1.7 %collective-permute-start.4 = (bf16[56,512]{1,0:T(8,128)(2,1)S(1)}, bf16[56,512]{1,0:T(8,128)(2,1)S(1)}, u32[]{:S(2)}, u32[]{:S(2)}) collective-permute-start(bf16[56,512]{1,0:T(8,128)(2,1)S(1)} %get-tuple-element.65), channel_id=1, source_target_pairs={{0,12},{4,8},{8,4},{12,0},{1,13},{5,9},{9,5},{13,1},{2,14},{6,10},... | collective-permute-start | bytes 172040 | tf_op jit(solution)/shard_map/ppermute | solution.py:470
  27.5 2.9 %shard_map.42 = bf16[56,512]{1,0:T(8,128)(2,1)S(1)} custom-call(bf16[144,512]{1,0:T(8,128)(2,1)S(1)} %get-tuple-element.46.m0, bf16[144,512]{1,0:T(8,128)(2,1)S(1)} %collective-permute-done.1.m1, bf16[144,512]{1,0:T(8,128)(2,1)S(1)} %collective-permute-done.2.m2, bf16[144,512]{1,0:T(8,128)(2,1)S(1)} %collective-permute-done.ma.m3, ...), custom_call_target="tpu_custom_call" | custom-call | flops 1073741824 | bytes 2097152 | tf_op jit(solution)/shard_map/pallas_call | solution.py:216
  30.4 1.0 %collective-permute-start.5 = (bf16[56,512]{1,0:T(8,128)(2,1)S(1)}, bf16[56,512]{1,0:T(8,128)(2,1)S(1)}, u32[]{:S(2)}, u32[]{:S(2)}) collective-permute-start(bf16[56,512]{1,0:T(8,128)(2,1)S(1)} %shard_map.42), channel_id=1, source_target_pairs={{0,4},{4,0},{8,12},{12,8},{1,5},{5,1},{9,13},{13,9},{2,6},{6,2},{1... | collective-permute-start | bytes 172040 | tf_op jit(solution)/shard_map/ppermute | solution.py:470
  31.4 2.9 %shard_map.43.own_ref = bf16[1,48,1024]{2,1,0:T(8,128)(2,1)S(1)} custom-call(bf16[144,512]{1,0:T(8,128)(2,1)S(1)} %get-tuple-element.46.m0, bf16[144,512]{1,0:T(8,128)(2,1)S(1)} %collective-permute-done.1.m1, bf16[144,512]{1,0:T(8,128)(2,1)S(1)} %collective-permute-done.2.m2, bf16[144,512]{1,0:T(8,128)(2,1)S(1)} %collective-permute-done.ma.m3, ...), custom_call_target="tpu_custom_call" | custom-call | flops 536870912 | bytes 2097152 | tf_op jit(solution)/shard_map/pallas_call | solution.py:216
  34.3 0.0 collective-permute-done.3.refs_0_
  34.3 0.0 collective-permute-done.4.refs_1_
  34.3 0.5 %shard_map.44.far_ref = bf16[2,48,1024]{2,1,0:T(8,128)(2,1)S(1)} custom-call(f32[1,56,1024]{2,1,0:T(8,128)S(1)} %shard_map.38.low_ref, f32[3,56,1024]{2,1,0:T(8,128)S(1)} %shard_map.39.high_ref, bf16[56,512]{1,0:T(8,128)(2,1)S(1)} %collective-permute-done.3.refs_0_, bf16[56,512]{1,0:T(8,128)(2,1)S(1)} %collective-permute-done.4.refs_1_), custom_call_target="tpu_custom_call" | custom-call | flops 1073741824 | bytes 2097152 | tf_op jit(solution)/shard_map/pallas_call | solution.py:216
  34.8 0.0 collective-permute-done.5.result
  34.8 1.0 %shard_map.45 = bf16[192,1024]{1,0:T(8,128)(2,1)} custom-call(f32[1,56,1024]{2,1,0:T(8,128)S(1)} %shard_map.38.low_ref, f32[3,56,1024]{2,1,0:T(8,128)S(1)} %shard_map.39.high_ref, bf16[1,48,1024]{2,1,0:T(8,128)(2,1)S(1)} %shard_map.43.own_ref, bf16[2,48,1024]{2,1,0:T(8,128)(2,1)S(1)} %shard_map.44.far_ref, bf16[56,512]{1,0:T(8,128)(2,1)S(1)} %collective-permute-done.5.result), custom_call_target="tpu_custom_call" | custom-call | flops 536870912 | bytes 1048576 | tf_op jit(solution)/shard_map/pallas_call | solution.py:530
Async XLA Ops:
  1.9 12.8 %collective-permute-start = (bf16[144,512]{1,0:T(8,128)(2,1)S(1)}, bf16[144,512]{1,0:T(8,128)(2,1)S(1)}, u32[]{:S(2)}, u32[]{:S(2)}) collective-permute-start(bf16[144,512]{1,0:T(8,128)(2,1)S(1)} %get-tuple-element.41), channel_id=1, source_target_pairs={{0,12},{4,8},{8,4},{12,0},{1,13},{5,9},{9,5},{13,1},{2,14},{6,10},... | collective-permute-start | bytes 442376 | tf_op jit(solution)/shard_map/ppermute | solution.py:470
  7.0 12.5 %collective-permute-start.2 = (bf16[144,512]{1,0:T(8,128)(2,1)S(1)}, bf16[144,512]{1,0:T(8,128)(2,1)S(1)}, u32[]{:S(2)}, u32[]{:S(2)}) collective-permute-start(bf16[144,512]{1,0:T(8,128)(2,1)S(1)} %get-tuple-element.51), channel_id=1, source_target_pairs={{0,8},{4,12},{8,0},{12,4},{1,9},{5,13},{9,1},{13,5},{2,10},{6,14},... | collective-permute-start | bytes 442376 | tf_op jit(solution)/shard_map/ppermute | solution.py:470
  8.9 10.6 %collective-permute-start.1 = (bf16[144,512]{1,0:T(8,128)(2,1)S(1)}, bf16[144,512]{1,0:T(8,128)(2,1)S(1)}, u32[]{:S(2)}, u32[]{:S(2)}) collective-permute-start(bf16[144,512]{1,0:T(8,128)(2,1)S(1)} %get-tuple-element.50), channel_id=1, source_target_pairs={{0,4},{4,0},{8,12},{12,8},{1,5},{5,1},{9,13},{13,9},{2,6},{6,2},{1... | collective-permute-start | bytes 442376 | tf_op jit(solution)/shard_map/ppermute | solution.py:470
  24.8 9.4 %collective-permute-start.3 = (bf16[56,512]{1,0:T(8,128)(2,1)S(1)}, bf16[56,512]{1,0:T(8,128)(2,1)S(1)}, u32[]{:S(2)}, u32[]{:S(2)}) collective-permute-start(bf16[56,512]{1,0:T(8,128)(2,1)S(1)} %get-tuple-element.64), channel_id=1, source_target_pairs={{0,8},{4,12},{8,0},{12,4},{1,9},{5,13},{9,1},{13,5},{2,10},{6,14},... | collective-permute-start | bytes 172040 | tf_op jit(solution)/shard_map/ppermute | solution.py:470
  25.7 8.5 %collective-permute-start.4 = (bf16[56,512]{1,0:T(8,128)(2,1)S(1)}, bf16[56,512]{1,0:T(8,128)(2,1)S(1)}, u32[]{:S(2)}, u32[]{:S(2)}) collective-permute-start(bf16[56,512]{1,0:T(8,128)(2,1)S(1)} %get-tuple-element.65), channel_id=1, source_target_pairs={{0,12},{4,8},{8,4},{12,0},{1,13},{5,9},{9,5},{13,1},{2,14},{6,10},... | collective-permute-start | bytes 172040 | tf_op jit(solution)/shard_map/ppermute | solution.py:470
  30.4 4.5 %collective-permute-start.5 = (bf16[56,512]{1,0:T(8,128)(2,1)S(1)}, bf16[56,512]{1,0:T(8,128)(2,1)S(1)}, u32[]{:S(2)}, u32[]{:S(2)}) collective-permute-start(bf16[56,512]{1,0:T(8,128)(2,1)S(1)} %shard_map.42), channel_id=1, source_target_pairs={{0,4},{4,0},{8,12},{12,8},{1,5},{5,1},{9,13},{13,9},{2,6},{6,2},{1... | collective-permute-start | bytes 172040 | tf_op jit(solution)/shard_map/ppermute | solution.py:470

commit v9 on v8

--- a/solution.py
+++ b/solution.py
@@ -395,11 +395,16 @@
     part0[...], parta[...] = plain((queries_of(m0), groups), (queries_of(ma), groups))
 
 
-def cross_kernel(m0, m1, m2, m3, keys0, keys3, part3, f2, f3, keys1, keys2):
+def middle_kernel(m1, m3, part3, keys1, more3):
     make_keys(keys1, m1)
+    (term,) = plain((queries_of(m3), ((keys1, values_of(m1)),)))
+    more3[...] = part3[...] + term
+
+
+def cross_kernel(m0, m1, m2, m3, keys0, keys1, keys3, part3, f2, f3, keys2):
     make_keys(keys2, m2)
-    groups = [(keys, values_of(message)) for keys, message in ((keys0, m0), (keys1, m1), (keys2, m2), (keys3, m3))]
-    whole, rest = plain((queries_of(m2), groups), (queries_of(m3), groups[1:3]))
+    groups = [(keys, values_of(message)) for keys, message in ((keys0, m0), (keys1, m1), (keys3, m3), (keys2, m2))]
+    whole, rest = plain((queries_of(m2), groups), (queries_of(m3), groups[3:]))
     settle((whole, part3[...] + rest), (f2, f3), (m2, m3), lambda: groups)
 
 
@@ -505,9 +510,11 @@
     work = 4 * count * count * 256
     n3, high = lax.optimization_barrier((n3, high))
     keys0, keys3, part0, part3 = call(early_kernel, [keys, keys, part, part], (m0, n3), [], 4 * work)
-    keys0, keys3, n1, n2 = lax.optimization_barrier((keys0, keys3, n1, n2))
-    f2, f3, keys1, keys2 = call(
-        cross_kernel, [result, result, keys, keys], (m0, n1, n2, n3, keys0, keys3, part3), [], 6 * work
+    keys0, keys3, n1 = lax.optimization_barrier((keys0, keys3, n1))
+    keys1, part3 = call(middle_kernel, [keys, part], (n1, n3, part3), [], work)
+    keys1, n2 = lax.optimization_barrier((keys1, n2))
+    f2, f3, keys2 = call(
+        cross_kernel, [result, result, keys], (m0, n1, n2, n3, keys0, keys1, keys3, part3), [], 5 * work
     )
     f2, f3, keys2 = lax.optimization_barrier((f2, f3, keys2))
     g2, g3 = exchanged(f2, 2), exchanged(f3, 3)

time: 36.2 us -> 35.8 us (0.989)
  waiting for transfers between devices: 3.57 us -> 2.99 us
    ppermute x6, waiting for transfers between devices: 3.57 us -> 2.99 us  [exchanged(): lax.ppermute(block, 'seq', [(i, i ^ step) for i in range(lax.axis_size('s...]
    pallas_call x8 -> x9, Pallas kernels: 21.7 us -> 21.9 us  [call(): pl.pallas_call(kernel, out_shape=outs, in_specs=[pl.BlockSpec(memory_spac...]
  transfers between devices with their start and end apart: 6 -> 6, of which waited for: 1 -> 2; matrix products, arithmetic and copies ran while one was open for 0% -> 0% of each run, Pallas kernels for 40% -> 42%
where the time goes in v9:
time: 35.8 us; the launch traced here: 35.7 us
  Pallas kernels  22.9 us (64%)
  starting transfers between devices  9.47 us (26%)
  waiting for transfers between devices  2.99 us (8%)
    pallas_call x9, Pallas kernels, call(): pl.pallas_call(kernel, out_shape=outs, in_specs=[pl.BlockSpec(memory_spac...  21.9 us
    ppermute x6, starting transfers between devices, exchanged(): lax.ppermute(block, 'seq', [(i, i ^ step) for i in range(lax.axis_size('s...  9.47 us
    ppermute x6, waiting for transfers between devices, exchanged(): lax.ppermute(block, 'seq', [(i, i ^ step) for i in range(lax.axis_size('s...  2.99 us
    pallas_call x1, Pallas kernels, whole_slide(): pl.pallas_call(last_kernel, out_shape=jax.ShapeDtypeStruct((width, rows),...  1.03 us
  transfers between devices with their start and end apart: 6, of which 2 were waited for; matrix products, arithmetic and copies ran while one was open for 0% of the time, Pallas kernels for 42%

profile of v9, /device:TPU:0, one launch (start us, length us, event | category | flops | bytes accessed | tf_op | source)
XLA Modules:
  0.0 35.7 jit_solution(18061266048724333968)
XLA Ops:
  0.0 1.9 %shard_map.37 = (bf16[192,1024]{1,0:T(8,128)(2,1)S(1)}, bf16[192,1024]{1,0:T(8,128)(2,1)S(1)}, bf16[192,1024]{1,0:T(8,128)(2,1)S(1)}, bf16[144,512]{1,0:T(8,128)...) custom-call(bf16[192,1024]{1,0:T(8,128)(2,1)} %bitcast.4, ...), custom_call_target="tpu_custom_call" | custom-call | flops 268435456 | bytes 2097152 | tf_op jit(solution)/shard_map/pallas_call | solution.py:216
  1.9 5.1 %collective-permute-start = (bf16[144,512]{1,0:T(8,128)(2,1)S(1)}, bf16[144,512]{1,0:T(8,128)(2,1)S(1)}, u32[]{:S(2)}, u32[]{:S(2)}) collective-permute-start(bf16[144,512]{1,0:T(8,128)(2,1)S(1)} %get-tuple-element.40), channel_id=1, source_target_pairs={{0,12},{4,8},{8,4},{12,0},{1,13},{5,9},{9,5},{13,1},{2,14},{6,10},... | collective-permute-start | bytes 442376 | tf_op jit(solution)/shard_map/ppermute | solution.py:475
  7.0 0.0 collective-permute-start.2
  7.0 1.9 %shard_map.38.low_ref = f32[1,56,1024]{2,1,0:T(8,128)S(1)} custom-call(bf16[192,1024]{1,0:T(8,128)(2,1)S(1)} %get-tuple-element.41.qt_ref, bf16[192,1024]{1,0:T(8,128)(2,1)S(1)} %get-tuple-element.42.kt_ref, bf16[192,1024]{1,0:T(8,128)(2,1)S(1)} %get-tuple-element.43.vt_ref), custom_call_target="tpu_custom_call" | custom-call | flops 1073741824 | bytes 2097152 | tf_op jit(solution)/shard_map/pallas_call | solution.py:216
  8.9 0.7 %collective-permute-start.1 = (bf16[144,512]{1,0:T(8,128)(2,1)S(1)}, bf16[144,512]{1,0:T(8,128)(2,1)S(1)}, u32[]{:S(2)}, u32[]{:S(2)}) collective-permute-start(bf16[144,512]{1,0:T(8,128)(2,1)S(1)} %get-tuple-element.49), channel_id=1, source_target_pairs={{0,4},{4,0},{8,12},{12,8},{1,5},{5,1},{9,13},{13,9},{2,6},{6,2},{1... | collective-permute-start | bytes 442376 | tf_op jit(solution)/shard_map/ppermute | solution.py:475
  9.6 5.0 %shard_map.39.high_ref = f32[3,56,1024]{2,1,0:T(8,128)S(1)} custom-call(bf16[192,1024]{1,0:T(8,128)(2,1)S(1)} %get-tuple-element.41.qt_ref, bf16[192,1024]{1,0:T(8,128)(2,1)S(1)} %get-tuple-element.42.kt_ref, bf16[192,1024]{1,0:T(8,128)(2,1)S(1)} %get-tuple-element.43.vt_ref), custom_call_target="tpu_custom_call" | custom-call | flops 3221225472 | bytes 2097152 | tf_op jit(solution)/shard_map/pallas_call | solution.py:216
  14.7 0.0 collective-permute-done.ma.m3
  14.7 1.2 %shard_map.40 = (bf16[512,48]{1,0:T(8,128)(2,1)S(1)}, bf16[512,48]{1,0:T(8,128)(2,1)S(1)}, f32[64,512]{1,0:T(8,128)S(1)}, f32[64,512]{1,0:T(8,128)S(1)}) custom-call(bf16[144,512]{1,0:T(8,128)(2,1)S(1)} %get-tuple-element.45.m0, bf16[144,512]{1,0:T(8,128)(2,1)S(1)} %collective-permute-done.ma.m3), custom_call_target="tpu_custom_call" | custom-call | flops 1073741824 | bytes 2097152 | tf_op jit(solution)/shard_map/pallas_call | solution.py:216
  15.9 0.6 %collective-permute-done.1.m1 = bf16[144,512]{1,0:T(8,128)(2,1)S(1)} collective-permute-done((bf16[144,512]{1,0:T(8,128)(2,1)S(1)}, bf16[144,512]{1,0:T(8,128)(2,1)S(1)}, u32[]{:S(2)}, u32[]{:S(2)}) %collective-permute-start.1) | collective-permute-done | bytes 147488 | tf_op jit(solution)/shard_map/ppermute | solution.py:475
  16.5 0.6 %shard_map.41 = (bf16[512,48]{1,0:T(8,128)(2,1)S(1)}, f32[64,512]{1,0:T(8,128)S(1)}) custom-call(bf16[144,512]{1,0:T(8,128)(2,1)S(1)} %collective-permute-done.1.m1, bf16[144,512]{1,0:T(8,128)(2,1)S(1)} %collective-permute-done.ma.m3, f32[64,512]{1,0:T(8,128)S(1)} %get-tuple-element.51.part3), custom_call_target="tpu_custom_call" | custom-call | flops 268435456 | bytes 2097152 | tf_op jit(solution)/shard_map/pallas_call | solution.py:216
  17.0 2.4 %collective-permute-done.2.m2 = bf16[144,512]{1,0:T(8,128)(2,1)S(1)} collective-permute-done((bf16[144,512]{1,0:T(8,128)(2,1)S(1)}, bf16[144,512]{1,0:T(8,128)(2,1)S(1)}, u32[]{:S(2)}, u32[]{:S(2)}) %collective-permute-start.2) | collective-permute-done | bytes 147488 | tf_op jit(solution)/shard_map/ppermute | solution.py:475
  19.5 5.0 %shard_map.42 = (bf16[56,512]{1,0:T(8,128)(2,1)S(1)}, bf16[56,512]{1,0:T(8,128)(2,1)S(1)}, bf16[512,48]{1,0:T(8,128)(2,1)S(1)}) custom-call(bf16[144,512]{1,0:T(8,128)(2,1)S(1)} %get-tuple-element.45.m0, bf16[144,512]{1,0:T(8,128)(2,1)S(1)} %collective-permute-done.1.m1, bf16[144,512]{1,0:T(8,128)(2,1)S(1)} %collective-permute-done.2.m2, ...), custom_call_target="tpu_custom_call" | custom-call | flops 1342177280 | bytes 2097152 | tf_op jit(solution)/shard_map/pallas_call | solution.py:216
  24.5 1.5 %collective-permute-start.3 = (bf16[56,512]{1,0:T(8,128)(2,1)S(1)}, bf16[56,512]{1,0:T(8,128)(2,1)S(1)}, u32[]{:S(2)}, u32[]{:S(2)}) collective-permute-start(bf16[56,512]{1,0:T(8,128)(2,1)S(1)} %get-tuple-element.62), channel_id=1, source_target_pairs={{0,8},{4,12},{8,0},{12,4},{1,9},{5,13},{9,1},{13,5},{2,10},{6,14},... | collective-permute-start | bytes 172040 | tf_op jit(solution)/shard_map/ppermute | solution.py:475
  25.9 1.2 %collective-permute-start.4 = (bf16[56,512]{1,0:T(8,128)(2,1)S(1)}, bf16[56,512]{1,0:T(8,128)(2,1)S(1)}, u32[]{:S(2)}, u32[]{:S(2)}) collective-permute-start(bf16[56,512]{1,0:T(8,128)(2,1)S(1)} %get-tuple-element.63), channel_id=1, source_target_pairs={{0,12},{4,8},{8,4},{12,0},{1,13},{5,9},{9,5},{13,1},{2,14},{6,10},... | collective-permute-start | bytes 172040 | tf_op jit(solution)/shard_map/ppermute | solution.py:475
  27.1 2.9 %shard_map.43 = bf16[56,512]{1,0:T(8,128)(2,1)S(1)} custom-call(bf16[144,512]{1,0:T(8,128)(2,1)S(1)} %get-tuple-element.45.m0, bf16[144,512]{1,0:T(8,128)(2,1)S(1)} %collective-permute-done.1.m1, bf16[144,512]{1,0:T(8,128)(2,1)S(1)} %collective-permute-done.2.m2, bf16[144,512]{1,0:T(8,128)(2,1)S(1)} %collective-permute-done.ma.m3, ...), custom_call_target="tpu_custom_call" | custom-call | flops 1073741824 | bytes 2097152 | tf_op jit(solution)/shard_map/pallas_call | solution.py:216
  30.0 1.0 %collective-permute-start.5 = (bf16[56,512]{1,0:T(8,128)(2,1)S(1)}, bf16[56,512]{1,0:T(8,128)(2,1)S(1)}, u32[]{:S(2)}, u32[]{:S(2)}) collective-permute-start(bf16[56,512]{1,0:T(8,128)(2,1)S(1)} %shard_map.43), channel_id=1, source_target_pairs={{0,4},{4,0},{8,12},{12,8},{1,5},{5,1},{9,13},{13,9},{2,6},{6,2},{1... | collective-permute-start | bytes 172040 | tf_op jit(solution)/shard_map/ppermute | solution.py:475
  31.0 2.9 %shard_map.44.own_ref = bf16[1,48,1024]{2,1,0:T(8,128)(2,1)S(1)} custom-call(bf16[144,512]{1,0:T(8,128)(2,1)S(1)} %get-tuple-element.45.m0, bf16[144,512]{1,0:T(8,128)(2,1)S(1)} %collective-permute-done.1.m1, bf16[144,512]{1,0:T(8,128)(2,1)S(1)} %collective-permute-done.2.m2, bf16[144,512]{1,0:T(8,128)(2,1)S(1)} %collective-permute-done.ma.m3, ...), custom_call_target="tpu_custom_call" | custom-call | flops 536870912 | bytes 2097152 | tf_op jit(solution)/shard_map/pallas_call | solution.py:216
  33.9 0.0 collective-permute-done.3.refs_0_
  33.9 0.0 collective-permute-done.4.refs_1_
  33.9 0.5 %shard_map.45.far_ref = bf16[2,48,1024]{2,1,0:T(8,128)(2,1)S(1)} custom-call(f32[1,56,1024]{2,1,0:T(8,128)S(1)} %shard_map.38.low_ref, f32[3,56,1024]{2,1,0:T(8,128)S(1)} %shard_map.39.high_ref, bf16[56,512]{1,0:T(8,128)(2,1)S(1)} %collective-permute-done.3.refs_0_, bf16[56,512]{1,0:T(8,128)(2,1)S(1)} %collective-permute-done.4.refs_1_), custom_call_target="tpu_custom_call" | custom-call | flops 1073741824 | bytes 2097152 | tf_op jit(solution)/shard_map/pallas_call | solution.py:216
  34.5 0.0 collective-permute-done.5.result
  34.5 1.0 %shard_map.46 = bf16[192,1024]{1,0:T(8,128)(2,1)} custom-call(f32[1,56,1024]{2,1,0:T(8,128)S(1)} %shard_map.38.low_ref, f32[3,56,1024]{2,1,0:T(8,128)S(1)} %shard_map.39.high_ref, bf16[1,48,1024]{2,1,0:T(8,128)(2,1)S(1)} %shard_map.44.own_ref, bf16[2,48,1024]{2,1,0:T(8,128)(2,1)S(1)} %shard_map.45.far_ref, bf16[56,512]{1,0:T(8,128)(2,1)S(1)} %collective-permute-done.5.result), custom_call_target="tpu_custom_call" | custom-call | flops 536870912 | bytes 1048576 | tf_op jit(solution)/shard_map/pallas_call | solution.py:537
Async XLA Ops:
  1.9 12.8 %collective-permute-start = (bf16[144,512]{1,0:T(8,128)(2,1)S(1)}, bf16[144,512]{1,0:T(8,128)(2,1)S(1)}, u32[]{:S(2)}, u32[]{:S(2)}) collective-permute-start(bf16[144,512]{1,0:T(8,128)(2,1)S(1)} %get-tuple-element.40), channel_id=1, source_target_pairs={{0,12},{4,8},{8,4},{12,0},{1,13},{5,9},{9,5},{13,1},{2,14},{6,10},... | collective-permute-start | bytes 442376 | tf_op jit(solution)/shard_map/ppermute | solution.py:475
  7.0 12.5 %collective-permute-start.2 = (bf16[144,512]{1,0:T(8,128)(2,1)S(1)}, bf16[144,512]{1,0:T(8,128)(2,1)S(1)}, u32[]{:S(2)}, u32[]{:S(2)}) collective-permute-start(bf16[144,512]{1,0:T(8,128)(2,1)S(1)} %get-tuple-element.53), channel_id=1, source_target_pairs={{0,8},{4,12},{8,0},{12,4},{1,9},{5,13},{9,1},{13,5},{2,10},{6,14},... | collective-permute-start | bytes 442376 | tf_op jit(solution)/shard_map/ppermute | solution.py:475
  8.9 7.6 %collective-permute-start.1 = (bf16[144,512]{1,0:T(8,128)(2,1)S(1)}, bf16[144,512]{1,0:T(8,128)(2,1)S(1)}, u32[]{:S(2)}, u32[]{:S(2)}) collective-permute-start(bf16[144,512]{1,0:T(8,128)(2,1)S(1)} %get-tuple-element.49), channel_id=1, source_target_pairs={{0,4},{4,0},{8,12},{12,8},{1,5},{5,1},{9,13},{13,9},{2,6},{6,2},{1... | collective-permute-start | bytes 442376 | tf_op jit(solution)/shard_map/ppermute | solution.py:475
  24.5 9.4 %collective-permute-start.3 = (bf16[56,512]{1,0:T(8,128)(2,1)S(1)}, bf16[56,512]{1,0:T(8,128)(2,1)S(1)}, u32[]{:S(2)}, u32[]{:S(2)}) collective-permute-start(bf16[56,512]{1,0:T(8,128)(2,1)S(1)} %get-tuple-element.62), channel_id=1, source_target_pairs={{0,8},{4,12},{8,0},{12,4},{1,9},{5,13},{9,1},{13,5},{2,10},{6,14},... | collective-permute-start | bytes 172040 | tf_op jit(solution)/shard_map/ppermute | solution.py:475
  25.9 8.0 %collective-permute-start.4 = (bf16[56,512]{1,0:T(8,128)(2,1)S(1)}, bf16[56,512]{1,0:T(8,128)(2,1)S(1)}, u32[]{:S(2)}, u32[]{:S(2)}) collective-permute-start(bf16[56,512]{1,0:T(8,128)(2,1)S(1)} %get-tuple-element.63), channel_id=1, source_target_pairs={{0,12},{4,8},{8,4},{12,0},{1,13},{5,9},{9,5},{13,1},{2,14},{6,10},... | collective-permute-start | bytes 172040 | tf_op jit(solution)/shard_map/ppermute | solution.py:475
  30.0 4.4 %collective-permute-start.5 = (bf16[56,512]{1,0:T(8,128)(2,1)S(1)}, bf16[56,512]{1,0:T(8,128)(2,1)S(1)}, u32[]{:S(2)}, u32[]{:S(2)}) collective-permute-start(bf16[56,512]{1,0:T(8,128)(2,1)S(1)} %shard_map.43), channel_id=1, source_target_pairs={{0,4},{4,0},{8,12},{12,8},{1,5},{5,1},{9,13},{13,9},{2,6},{6,2},{1... | collective-permute-start | bytes 172040 | tf_op jit(solution)/shard_map/ppermute | solution.py:475

commit v10 on v9

--- a/solution.py
+++ b/solution.py
@@ -224,47 +224,54 @@
     )(*args)
 
 
-def pack_kernel(q_hbm, k_hbm, v_hbm, q_ref, k_ref, v_ref, m2, m3, m1, m0, by_head, arrivals):
-    width, rows = q_ref.shape
-    blocks = range(rows // SPAN)
+def pick_for(head):
+    return one_hot(
+        (SPAN, 2 * LANES),
+        lambda row, column: row == column % LANES * STRIDES + (head + column // LANES * 2) % STRIDES,
+    )
+
+
+def fill_message(message, pieces, pick, block):
+    half = message.shape[1] // 2
+    picked = dot_nn(jnp.concatenate(pieces, axis=0), pick).astype(jnp.bfloat16)
+    for klass in range(2):
+        lanes = pl.ds(klass * half + block * LANES, LANES)
+        message[:, lanes] = picked[:, klass * LANES : (klass + 1) * LANES]
+
+
+def first_pack_kernel(q_hbm, k_hbm, v_hbm, message, held, arrivals):
+    head = jnp.bitwise_xor(lax.axis_index("seq"), 3)
+    features = pl.ds(pl.multiple_of(head * HEAD_DIM, 16), HEAD_DIM)
     copies = [
-        [
-            pltpu.make_async_copy(
-                source.at[:, pl.ds(block * SPAN, SPAN)], target.at[:, pl.ds(block * SPAN, SPAN)], arrivals.at[block, at]
-            )
-            for at, (source, target) in enumerate(((q_hbm, q_ref), (k_hbm, k_ref), (v_hbm, v_ref)))
-        ]
-        for block in blocks
+        pltpu.make_async_copy(source.at[features], held.at[at], arrivals.at[at])
+        for at, source in enumerate((q_hbm, k_hbm, v_hbm))
     ]
-    for block in blocks:
-        for copy in copies[block]:
-            copy.start()
-    heads = width // HEAD_DIM
-    picks = [
-        one_hot((SPAN, 2 * LANES), lambda row, column: row == column % LANES * STRIDES + column // LANES * 2 + parity)
-        for parity in range(2)
+    for copy in copies:
+        copy.start()
+    pick = pick_for(head)
+    for copy in copies:
+        copy.wait()
+    for block in range(held.shape[2] // SPAN):
+        fill_message(message, [held[at, :, pl.ds(block * SPAN, SPAN)] for at in range(3)], pick, block)
+
+
+def pack_kernel(q_hbm, k_hbm, v_hbm, q_ref, k_ref, v_ref, m2, m1, m0, arrivals):
+    copies = [
+        pltpu.make_async_copy(source, target, arrivals.at[at])
+        for at, (source, target) in enumerate(((q_hbm, q_ref), (k_hbm, k_ref), (v_hbm, v_ref)))
     ]
-    for block in blocks:
-        for copy in copies[block]:
-            copy.wait()
-        for parity, pick in enumerate(picks):
-            mine = range(parity, heads, 2)
-            pieces = [
-                ref[pl.ds(head * HEAD_DIM, HEAD_DIM), pl.ds(block * SPAN, SPAN)]
-                for head in mine
-                for ref in (q_ref, k_ref, v_ref)
-            ]
-            picked = dot_nn(jnp.concatenate(pieces, axis=0), pick).astype(jnp.bfloat16)
-            for at, head in enumerate(mine):
-                features = picked[at * 3 * HEAD_DIM : (at + 1) * 3 * HEAD_DIM]
-                for klass in range(2):
-                    phase = (head + 2 * klass) % STRIDES // 2
-                    by_head[head, :, pl.ds(klass * rows // STRIDES + block * LANES, LANES)] = features[
-                        :, phase * LANES : (phase + 1) * LANES
-                    ]
+    for copy in copies:
+        copy.start()
     me = lax.axis_index("seq")
-    for shift, message in ((2, m2), (3, m3), (1, m1), (0, m0)):
-        message[...] = by_head[jnp.bitwise_xor(me, shift)]
+    heads = [(jnp.bitwise_xor(me, step), message) for step, message in ((2, m2), (1, m1), (0, m0))]
+    picks = [pick_for(head) for head, _ in heads]
+    for copy in copies:
+        copy.wait()
+    for (head, message), pick in zip(heads, picks):
+        features = pl.ds(pl.multiple_of(head * HEAD_DIM, 16), HEAD_DIM)
+        for block in range(q_ref.shape[1] // SPAN):
+            pieces = [ref[features, pl.ds(block * SPAN, SPAN)] for ref in (q_ref, k_ref, v_ref)]
+            fill_message(message, pieces, pick, block)
 
 
 def with_ones(block):
@@ -388,11 +395,10 @@
             out[...] = finished(*shifted(queries_of(message), every()))
 
 
-def early_kernel(m0, ma, keys0, keysa, part0, parta):
+def early_kernel(m0, m3, keys0, keys3, part3):
     make_keys(keys0, m0)
-    make_keys(keysa, ma)
-    groups = ((keys0, values_of(m0)), (keysa, values_of(ma)))
-    part0[...], parta[...] = plain((queries_of(m0), groups), (queries_of(ma), groups))
+    make_keys(keys3, m3)
+    (part3[...],) = plain((queries_of(m3), ((keys0, values_of(m0)), (keys3, values_of(m3)))))
 
 
 def middle_kernel(m1, m3, part3, keys1, more3):
@@ -414,10 +420,10 @@
     settle((whole,), (f1,), (m1,), lambda: groups)
 
 
-def own_kernel(m0, m1, m2, m3, keys0, keys1, keys2, keys3, part0, low_ref, high_ref, rows_ref, f0):
+def own_kernel(m0, m1, m2, m3, keys0, keys1, keys2, keys3, low_ref, high_ref, rows_ref, f0):
     groups = [(keys, values_of(message)) for keys, message in ((keys0, m0), (keys1, m1), (keys2, m2), (keys3, m3))]
-    (rest,) = plain((queries_of(m0), groups[1:3]))
-    settle((part0[...] + rest,), (f0,), (m0,), lambda: groups)
+    (whole,) = plain((queries_of(m0), groups))
+    settle((whole,), (f0,), (m0,), lambda: groups)
     merge_kernel((0,), low_ref, high_ref, f0, rows_ref)
 
 
@@ -480,16 +486,27 @@
     heads = width // HEAD_DIM
     count = rows // 2
     bf16, f32 = jnp.bfloat16, jnp.float32
-    turned = [pltpu.with_memory_space_constraint(block.T, pltpu.HBM) for block in (query_rows, key_rows, value_rows)]
-    *here, m2, m3, m1, m0 = call(
+    message = jax.ShapeDtypeStruct((3 * HEAD_DIM, count), bf16)
+    turned = [block.T for block in (query_rows, key_rows, value_rows)]
+    m3 = call(
+        first_pack_kernel,
+        message,
+        [pltpu.with_memory_space_constraint(block, pltpu.HBM) for block in turned],
+        [pltpu.VMEM((3, HEAD_DIM, rows), bf16), pltpu.SemaphoreType.DMA((3,))],
+        1 << 27,
+        pltpu.HBM,
+    )
+    n3 = exchanged(m3, 3)
+    m3, *turned = lax.optimization_barrier((m3, *turned))
+    *here, m2, m1, m0 = call(
         pack_kernel,
-        [jax.ShapeDtypeStruct((width, rows), bf16)] * 3 + [jax.ShapeDtypeStruct((3 * HEAD_DIM, count), bf16)] * heads,
-        turned,
-        [pltpu.VMEM((heads, 3 * HEAD_DIM, count), bf16), pltpu.SemaphoreType.DMA((rows // SPAN, 3))],
+        [jax.ShapeDtypeStruct((width, rows), bf16)] * 3 + [message] * 3,
+        [pltpu.with_memory_space_constraint(block, pltpu.HBM) for block in turned],
+        [pltpu.SemaphoreType.DMA((3,))],
         1 << 28,
         pltpu.HBM,
     )
-    n2, n3 = exchanged(m2, 2), exchanged(m3, 3)
+    n2 = exchanged(m2, 2)
 
     def near(first, some):
         return call(
@@ -509,7 +526,7 @@
     keys = jax.ShapeDtypeStruct((count, HEAD_DIM), bf16)
     work = 4 * count * count * 256
     n3, high = lax.optimization_barrier((n3, high))
-    keys0, keys3, part0, part3 = call(early_kernel, [keys, keys, part, part], (m0, n3), [], 4 * work)
+    keys0, keys3, part3 = call(early_kernel, [keys, keys, part], (m0, n3), [], 2 * work)
     keys0, keys3, n1 = lax.optimization_barrier((keys0, keys3, n1))
     keys1, part3 = call(middle_kernel, [keys, part], (n1, n3, part3), [], work)
     keys1, n2 = lax.optimization_barrier((keys1, n2))
@@ -520,12 +537,13 @@
     g2, g3 = exchanged(f2, 2), exchanged(f3, 3)
     every = (m0, n1, n2, n3, keys0, keys1, keys2, keys3)
     f1 = call(next_kernel, result, every, [], 4 * work)
-    f1, part0 = lax.optimization_barrier((f1, part0))
+    f1, keys2 = lax.optimization_barrier((f1, keys2))
+    every = (m0, n1, n2, n3, keys0, keys1, keys2, keys3)
     g1 = exchanged(f1, 1)
     own = call(
         own_kernel,
         jax.ShapeDtypeStruct((1, HEAD_DIM, rows), bf16),
-        (*every, part0, low, high),
+        (*every, low, high),
         [pltpu.VMEM((HEAD_DIM + TAIL, count), bf16)],
         2 * work,
     )

time: 35.8 us -> 35.6 us (level)
  waiting for transfers between devices: 2.99 us -> 1.76 us
  Pallas kernels: 22.9 us -> 23.9 us
    ppermute x6, waiting for transfers between devices: 2.99 us -> 1.76 us  [exchanged(): lax.ppermute(block, 'seq', [(i, i ^ step) for i in range(lax.axis_size('s...]
    pallas_call x9 -> x10, Pallas kernels: 21.9 us -> 22.9 us  [call(): pl.pallas_call(kernel, out_shape=outs, in_specs=[pl.BlockSpec(memory_spac...]
  transfers between devices with their start and end apart: 6 -> 6, of which waited for: 2 -> 1; matrix products, arithmetic and copies ran while one was open for 0% -> 0% of each run, Pallas kernels for 42% -> 47%
where the time goes in v10:
time: 35.6 us; the launch traced here: 35.4 us
  Pallas kernels  23.9 us (67%)
  starting transfers between devices  9.44 us (27%)
  waiting for transfers between devices  1.76 us (5%)
    pallas_call x10, Pallas kernels, call(): pl.pallas_call(kernel, out_shape=outs, in_specs=[pl.BlockSpec(memory_spac...  22.9 us
    ppermute x6, starting transfers between devices, exchanged(): lax.ppermute(block, 'seq', [(i, i ^ step) for i in range(lax.axis_size('s...  9.44 us
    ppermute x6, waiting for transfers between devices, exchanged(): lax.ppermute(block, 'seq', [(i, i ^ step) for i in range(lax.axis_size('s...  1.76 us
    pallas_call x1, Pallas kernels, whole_slide(): pl.pallas_call(last_kernel, out_shape=jax.ShapeDtypeStruct((width, rows),...  1.03 us
  transfers between devices with their start and end apart: 6, of which 1 were waited for; matrix products, arithmetic and copies ran while one was open for 0% of the time, Pallas kernels for 47%

profile of v10, /device:TPU:0, one launch (start us, length us, event | category | flops | bytes accessed | tf_op | source)
XLA Modules:
  0.0 35.4 jit_solution(5885866134340683340)
XLA Ops:
  0.0 1.3 %shard_map.37 = bf16[144,512]{1,0:T(8,128)(2,1)S(1)} custom-call(bf16[192,1024]{1,0:T(8,128)(2,1)} %bitcast.4, bf16[192,1024]{1,0:T(8,128)(2,1)} %bitcast.6, bf16[192,1024]{1,0:T(8,128)(2,1)} %bitcast.8), custom_call_target="tpu_custom_call" | custom-call | flops 134217728 | bytes 2097152 | tf_op jit(solution)/shard_map/pallas_call | solution.py:216
  1.3 5.1 %collective-permute-start = (bf16[144,512]{1,0:T(8,128)(2,1)S(1)}, bf16[144,512]{1,0:T(8,128)(2,1)S(1)}, u32[]{:S(2)}, u32[]{:S(2)}) collective-permute-start(bf16[144,512]{1,0:T(8,128)(2,1)S(1)} %shard_map.37), channel_id=1, source_target_pairs={{0,12},{4,8},{8,4},{12,0},{1,13},{5,9},{9,5},{13,1},{2,14},{6,10},... | collective-permute-start | bytes 442376 | tf_op jit(solution)/shard_map/ppermute | solution.py:481
  6.4 1.6 %shard_map.38 = (bf16[192,1024]{1,0:T(8,128)(2,1)S(1)}, bf16[192,1024]{1,0:T(8,128)(2,1)S(1)}, bf16[192,1024]{1,0:T(8,128)(2,1)S(1)}, bf16[144,512]{1,0:T(8,128)...) custom-call(bf16[192,1024]{1,0:T(8,128)(2,1)} %bitcast.5, bf16[192,1024]{1,0:T(8,128)(2,1)} %bitcast.7, ...), custom_call_target="tpu_custom_call" | custom-call | flops 268435456 | bytes 2097152 | tf_op jit(solution)/shard_map/pallas_call | solution.py:216
  8.0 0.1 collective-permute-start.2
  8.1 1.9 %shard_map.39.low_ref = f32[1,56,1024]{2,1,0:T(8,128)S(1)} custom-call(bf16[192,1024]{1,0:T(8,128)(2,1)S(1)} %get-tuple-element.44.qt_ref, bf16[192,1024]{1,0:T(8,128)(2,1)S(1)} %get-tuple-element.45.kt_ref, bf16[192,1024]{1,0:T(8,128)(2,1)S(1)} %get-tuple-element.46.vt_ref), custom_call_target="tpu_custom_call" | custom-call | flops 1073741824 | bytes 2097152 | tf_op jit(solution)/shard_map/pallas_call | solution.py:216
  10.0 0.6 %collective-permute-start.1 = (bf16[144,512]{1,0:T(8,128)(2,1)S(1)}, bf16[144,512]{1,0:T(8,128)(2,1)S(1)}, u32[]{:S(2)}, u32[]{:S(2)}) collective-permute-start(bf16[144,512]{1,0:T(8,128)(2,1)S(1)} %get-tuple-element.52), channel_id=1, source_target_pairs={{0,4},{4,0},{8,12},{12,8},{1,5},{5,1},{9,13},{13,9},{2,6},{6,2},{1... | collective-permute-start | bytes 442376 | tf_op jit(solution)/shard_map/ppermute | solution.py:481
  10.6 5.1 %shard_map.40.high_ref = f32[3,56,1024]{2,1,0:T(8,128)S(1)} custom-call(bf16[192,1024]{1,0:T(8,128)(2,1)S(1)} %get-tuple-element.44.qt_ref, bf16[192,1024]{1,0:T(8,128)(2,1)S(1)} %get-tuple-element.45.kt_ref, bf16[192,1024]{1,0:T(8,128)(2,1)S(1)} %get-tuple-element.46.vt_ref), custom_call_target="tpu_custom_call" | custom-call | flops 3221225472 | bytes 2097152 | tf_op jit(solution)/shard_map/pallas_call | solution.py:216
  15.7 0.0 collective-permute-done.m3
  15.7 0.8 %shard_map.41 = (bf16[512,48]{1,0:T(8,128)(2,1)S(1)}, bf16[512,48]{1,0:T(8,128)(2,1)S(1)}, f32[64,512]{1,0:T(8,128)S(1)}) custom-call(bf16[144,512]{1,0:T(8,128)(2,1)S(1)} %get-tuple-element.48.m0, bf16[144,512]{1,0:T(8,128)(2,1)S(1)} %collective-permute-done.m3), custom_call_target="tpu_custom_call" | custom-call | flops 536870912 | bytes 2097152 | tf_op jit(solution)/shard_map/pallas_call | solution.py:216
  16.5 0.0 collective-permute-done.1.m1
  16.5 0.6 %shard_map.42 = (bf16[512,48]{1,0:T(8,128)(2,1)S(1)}, f32[64,512]{1,0:T(8,128)S(1)}) custom-call(bf16[144,512]{1,0:T(8,128)(2,1)S(1)} %collective-permute-done.1.m1, bf16[144,512]{1,0:T(8,128)(2,1)S(1)} %collective-permute-done.m3, f32[64,512]{1,0:T(8,128)S(1)} %get-tuple-element.54.part3), custom_call_target="tpu_custom_call" | custom-call | flops 268435456 | bytes 2097152 | tf_op jit(solution)/shard_map/pallas_call | solution.py:216
  17.1 1.7 %collective-permute-done.2.m2 = bf16[144,512]{1,0:T(8,128)(2,1)S(1)} collective-permute-done((bf16[144,512]{1,0:T(8,128)(2,1)S(1)}, bf16[144,512]{1,0:T(8,128)(2,1)S(1)}, u32[]{:S(2)}, u32[]{:S(2)}) %collective-permute-start.2) | collective-permute-done | bytes 147488 | tf_op jit(solution)/shard_map/ppermute | solution.py:481
  18.9 5.0 %shard_map.43 = (bf16[56,512]{1,0:T(8,128)(2,1)S(1)}, bf16[56,512]{1,0:T(8,128)(2,1)S(1)}, bf16[512,48]{1,0:T(8,128)(2,1)S(1)}) custom-call(bf16[144,512]{1,0:T(8,128)(2,1)S(1)} %get-tuple-element.48.m0, bf16[144,512]{1,0:T(8,128)(2,1)S(1)} %collective-permute-done.1.m1, bf16[144,512]{1,0:T(8,128)(2,1)S(1)} %collective-permute-done.2.m2, ...), custom_call_target="tpu_custom_call" | custom-call | flops 1342177280 | bytes 2097152 | tf_op jit(solution)/shard_map/pallas_call | solution.py:216
  23.8 1.0 %collective-permute-start.3 = (bf16[56,512]{1,0:T(8,128)(2,1)S(1)}, bf16[56,512]{1,0:T(8,128)(2,1)S(1)}, u32[]{:S(2)}, u32[]{:S(2)}) collective-permute-start(bf16[56,512]{1,0:T(8,128)(2,1)S(1)} %get-tuple-element.64), channel_id=1, source_target_pairs={{0,8},{4,12},{8,0},{12,4},{1,9},{5,13},{9,1},{13,5},{2,10},{6,14},... | collective-permute-start | bytes 172040 | tf_op jit(solution)/shard_map/ppermute | solution.py:481
  24.8 1.6 %collective-permute-start.4 = (bf16[56,512]{1,0:T(8,128)(2,1)S(1)}, bf16[56,512]{1,0:T(8,128)(2,1)S(1)}, u32[]{:S(2)}, u32[]{:S(2)}) collective-permute-start(bf16[56,512]{1,0:T(8,128)(2,1)S(1)} %get-tuple-element.65), channel_id=1, source_target_pairs={{0,12},{4,8},{8,4},{12,0},{1,13},{5,9},{9,5},{13,1},{2,14},{6,10},... | collective-permute-start | bytes 172040 | tf_op jit(solution)/shard_map/ppermute | solution.py:481
  26.5 2.9 %shard_map.44 = bf16[56,512]{1,0:T(8,128)(2,1)S(1)} custom-call(bf16[144,512]{1,0:T(8,128)(2,1)S(1)} %get-tuple-element.48.m0, bf16[144,512]{1,0:T(8,128)(2,1)S(1)} %collective-permute-done.1.m1, bf16[144,512]{1,0:T(8,128)(2,1)S(1)} %collective-permute-done.2.m2, bf16[144,512]{1,0:T(8,128)(2,1)S(1)} %collective-permute-done.m3, ...), custom_call_target="tpu_custom_call" | custom-call | flops 1073741824 | bytes 2097152 | tf_op jit(solution)/shard_map/pallas_call | solution.py:216
  29.4 1.0 %collective-permute-start.5 = (bf16[56,512]{1,0:T(8,128)(2,1)S(1)}, bf16[56,512]{1,0:T(8,128)(2,1)S(1)}, u32[]{:S(2)}, u32[]{:S(2)}) collective-permute-start(bf16[56,512]{1,0:T(8,128)(2,1)S(1)} %shard_map.44), channel_id=1, source_target_pairs={{0,4},{4,0},{8,12},{12,8},{1,5},{5,1},{9,13},{13,9},{2,6},{6,2},{1... | collective-permute-start | bytes 172040 | tf_op jit(solution)/shard_map/ppermute | solution.py:481
  30.4 3.3 %shard_map.45.own_ref = bf16[1,48,1024]{2,1,0:T(8,128)(2,1)S(1)} custom-call(bf16[144,512]{1,0:T(8,128)(2,1)S(1)} %get-tuple-element.48.m0, bf16[144,512]{1,0:T(8,128)(2,1)S(1)} %collective-permute-done.1.m1, bf16[144,512]{1,0:T(8,128)(2,1)S(1)} %collective-permute-done.2.m2, bf16[144,512]{1,0:T(8,128)(2,1)S(1)} %collective-permute-done.m3, ...), custom_call_target="tpu_custom_call" | custom-call | flops 536870912 | bytes 2097152 | tf_op jit(solution)/shard_map/pallas_call | solution.py:216
  33.6 0.0 collective-permute-done.3.refs_0_
  33.6 0.0 collective-permute-done.4.refs_1_
  33.7 0.5 %shard_map.46.far_ref = bf16[2,48,1024]{2,1,0:T(8,128)(2,1)S(1)} custom-call(f32[1,56,1024]{2,1,0:T(8,128)S(1)} %shard_map.39.low_ref, f32[3,56,1024]{2,1,0:T(8,128)S(1)} %shard_map.40.high_ref, bf16[56,512]{1,0:T(8,128)(2,1)S(1)} %collective-permute-done.3.refs_0_, bf16[56,512]{1,0:T(8,128)(2,1)S(1)} %collective-permute-done.4.refs_1_), custom_call_target="tpu_custom_call" | custom-call | flops 1073741824 | bytes 2097152 | tf_op jit(solution)/shard_map/pallas_call | solution.py:216
  34.2 0.0 collective-permute-done.5.result
  34.2 1.0 %shard_map.47 = bf16[192,1024]{1,0:T(8,128)(2,1)} custom-call(f32[1,56,1024]{2,1,0:T(8,128)S(1)} %shard_map.39.low_ref, f32[3,56,1024]{2,1,0:T(8,128)S(1)} %shard_map.40.high_ref, bf16[1,48,1024]{2,1,0:T(8,128)(2,1)S(1)} %shard_map.45.own_ref, bf16[2,48,1024]{2,1,0:T(8,128)(2,1)S(1)} %shard_map.46.far_ref, bf16[56,512]{1,0:T(8,128)(2,1)S(1)} %collective-permute-done.5.result), custom_call_target="tpu_custom_call" | custom-call | flops 536870912 | bytes 1048576 | tf_op jit(solution)/shard_map/pallas_call | solution.py:555
Async XLA Ops:
  1.3 14.4 %collective-permute-start = (bf16[144,512]{1,0:T(8,128)(2,1)S(1)}, bf16[144,512]{1,0:T(8,128)(2,1)S(1)}, u32[]{:S(2)}, u32[]{:S(2)}) collective-permute-start(bf16[144,512]{1,0:T(8,128)(2,1)S(1)} %shard_map.37), channel_id=1, source_target_pairs={{0,12},{4,8},{8,4},{12,0},{1,13},{5,9},{9,5},{13,1},{2,14},{6,10},... | collective-permute-start | bytes 442376 | tf_op jit(solution)/shard_map/ppermute | solution.py:481
  8.0 10.8 %collective-permute-start.2 = (bf16[144,512]{1,0:T(8,128)(2,1)S(1)}, bf16[144,512]{1,0:T(8,128)(2,1)S(1)}, u32[]{:S(2)}, u32[]{:S(2)}) collective-permute-start(bf16[144,512]{1,0:T(8,128)(2,1)S(1)} %get-tuple-element.56), channel_id=1, source_target_pairs={{0,8},{4,12},{8,0},{12,4},{1,9},{5,13},{9,1},{13,5},{2,10},{6,14},... | collective-permute-start | bytes 442376 | tf_op jit(solution)/shard_map/ppermute | solution.py:481
  10.0 6.5 %collective-permute-start.1 = (bf16[144,512]{1,0:T(8,128)(2,1)S(1)}, bf16[144,512]{1,0:T(8,128)(2,1)S(1)}, u32[]{:S(2)}, u32[]{:S(2)}) collective-permute-start(bf16[144,512]{1,0:T(8,128)(2,1)S(1)} %get-tuple-element.52), channel_id=1, source_target_pairs={{0,4},{4,0},{8,12},{12,8},{1,5},{5,1},{9,13},{13,9},{2,6},{6,2},{1... | collective-permute-start | bytes 442376 | tf_op jit(solution)/shard_map/ppermute | solution.py:481
  23.8 9.8 %collective-permute-start.3 = (bf16[56,512]{1,0:T(8,128)(2,1)S(1)}, bf16[56,512]{1,0:T(8,128)(2,1)S(1)}, u32[]{:S(2)}, u32[]{:S(2)}) collective-permute-start(bf16[56,512]{1,0:T(8,128)(2,1)S(1)} %get-tuple-element.64), channel_id=1, source_target_pairs={{0,8},{4,12},{8,0},{12,4},{1,9},{5,13},{9,1},{13,5},{2,10},{6,14},... | collective-permute-start | bytes 172040 | tf_op jit(solution)/shard_map/ppermute | solution.py:481
  24.8 8.8 %collective-permute-start.4 = (bf16[56,512]{1,0:T(8,128)(2,1)S(1)}, bf16[56,512]{1,0:T(8,128)(2,1)S(1)}, u32[]{:S(2)}, u32[]{:S(2)}) collective-permute-start(bf16[56,512]{1,0:T(8,128)(2,1)S(1)} %get-tuple-element.65), channel_id=1, source_target_pairs={{0,12},{4,8},{8,4},{12,0},{1,13},{5,9},{9,5},{13,1},{2,14},{6,10},... | collective-permute-start | bytes 172040 | tf_op jit(solution)/shard_map/ppermute | solution.py:481
  29.4 4.8 %collective-permute-start.5 = (bf16[56,512]{1,0:T(8,128)(2,1)S(1)}, bf16[56,512]{1,0:T(8,128)(2,1)S(1)}, u32[]{:S(2)}, u32[]{:S(2)}) collective-permute-start(bf16[56,512]{1,0:T(8,128)(2,1)S(1)} %shard_map.44), channel_id=1, source_target_pairs={{0,4},{4,0},{8,12},{12,8},{1,5},{5,1},{9,13},{13,9},{2,6},{6,2},{1... | collective-permute-start | bytes 172040 | tf_op jit(solution)/shard_map/ppermute | solution.py:481
